TPU v7x, 32 devices: a whole 2x2x4 slice. The times are simulated.
32 devices in a mesh: seq: 8 (over z, x), chan: 4 (over y, core).
Axes of the slice: x: 2, y: 2, z: 4, core: 2. Of those that a mesh axis runs over, the one named last changes fastest.
Arguments:
- stream_in: bfloat16 [1024, 8192], P('seq', 'chan'), may hold values from -6 to 6
- features: bfloat16 [3, 1024, 8192], P(None, 'seq', 'chan'), may hold values from -6 to 6
- conv_taps: float32 [3, 3, 8192], P(None, None, 'chan'), may hold values from -3.5 to 3.5
- decay: float32 [8192, 8], P('chan'), may hold values from 0 to 1, as said below
- residues: float32 [8192, 8], P('chan'), may hold values from -1 to 1
- state_in: float32 [8192, 8], P('chan'), may hold values from -800 to 800
- out_weight: bfloat16 [8192, 8192], P('seq', 'chan'), may hold values from -0.0625 to 0.0625
Outputs:
- block_out: bfloat16 [1024, 8192], P('seq', 'chan')
Inputs may be any that keep to these rules, and one draw needn't show every extreme that they name: `decay`: every rate is positive.
All inputs are finite; a program needn't handle non-finite values.
Results may differ from a plain program's by a relative error of at most 0.0046.
Values may be sent and summed in bfloat16 or wider, within the bound.
No kernel may reach another device: no remote copies, remote signals or barrier semaphores. Data moves between devices by JAX's collectives and lax.ppermute only.
A program may use at most 128 MiB of HBM per device.

v0:
```python
import functools

import jax
import jax.numpy as jnp
from jax import lax
from jax.experimental import pallas as pl
from jax.experimental.pallas import tpu as pltpu
from jax.sharding import PartitionSpec as P


F32 = jnp.float32
BF16 = jnp.bfloat16
LANES = 128
SUBLANES = 8
PAD = 8
PIECES = 1


class Convolved:
    def __init__(self, block_ref, halo_ref, taps_ref, stream, lanes, buf):
        tokens, count = block_ref.shape[1], taps_ref.shape[1]
        if halo_ref is None:
            buf[:PAD, :] = jnp.zeros((PAD, LANES), F32)
        else:
            buf[PAD - count + 1 : PAD, :] = halo_ref[stream, :, lanes].astype(F32)
        buf[PAD:, :] = block_ref[stream, :, lanes].astype(F32)
        self.buf, self.steps = buf, tokens // SUBLANES
        self.taps = [spread(taps_ref[stream, k : k + 1, lanes]) for k in range(count)]
        self.window = [self.row(-k) for k in range(count - 1, 0, -1)]

    def row(self, j):
        return self.buf[pl.ds(PAD + j, SUBLANES, stride=self.steps), :]

    def __call__(self, j):
        rows = self.window + [self.row(j)]
        self.window = rows[1:]
        total = self.taps[0] * rows[-1]
        for k in range(1, len(self.taps)):
            total = total + self.taps[k] * rows[-1 - k]
        return total


def spread(row):
    return jnp.broadcast_to(row, (SUBLANES, LANES))


def over_planes(count, together, body):
    planes = count // LANES
    together = math_gcd(planes, together)

    def step(i, carry):
        for which in range(together):
            body(which, i * together + which)
        return carry

    lax.fori_loop(0, planes // together, step, 0)


def math_gcd(a, b):
    return a if b == 0 else math_gcd(b, a % b)


def lanes_at(plane, start=0):
    return pl.ds(pl.multiple_of(start + plane * LANES, LANES), LANES)


def states_kernel(
    block_hbm, taps_hbm, decay_hbm, residues_hbm, carried_hbm,
    end_ref, block_ref, taps_ref, decay_ref, residues_ref, carried_ref, kb, vb, sems,
):
    tokens, count = block_ref.shape[1:]
    poles = decay_ref.shape[0]
    steps = tokens // SUBLANES
    parts = sems.shape[0] - 5
    width = count // parts
    small = [
        pltpu.make_async_copy(source, target, sems.at[parts + i])
        for i, (source, target) in enumerate(
            [
                (taps_hbm, taps_ref),
                (decay_hbm, decay_ref),
                (residues_hbm, residues_ref),
                (carried_hbm, carried_ref),
                (block_hbm.at[:1], block_ref.at[:1]),
            ]
        )
    ]
    large = []
    for i in range(parts):
        lanes = pl.ds(i * width, width)
        large.append(
            pltpu.make_async_copy(
                block_hbm.at[1:, :, lanes], block_ref.at[1:, :, lanes], sems.at[i]
            )
        )
    for copy in large[:1] + small[:2] + large[1:] + small[2:]:
        copy.start()
    later = (SUBLANES - 1) - lax.broadcasted_iota(jnp.int32, (SUBLANES, LANES), 0)
    later = (later * steps + 1).astype(F32)

    def body(first, which, plane):
        lanes = lanes_at(plane, first)
        key = Convolved(block_ref, None, taps_ref, 1, lanes, kb.at[which])
        value = Convolved(block_ref, None, taps_ref, 2, lanes, vb.at[which])
        rates = [spread(decay_ref[r : r + 1, lanes]) for r in range(poles)]
        every = jnp.exp(-decay_ref[:, lanes])
        fades = [spread(every[r : r + 1]) for r in range(poles)]
        sums = None
        for j in range(steps):
            product = key(j) * value(j)
            if sums is None:
                sums = [product] * poles
            else:
                sums = [fades[r] * sums[r] + product for r in range(poles)]
        for r in range(poles):
            ended = sums[r] * jnp.exp(-rates[r] * later)
            end_ref[r : r + 1, lanes] = jnp.sum(ended, axis=0, keepdims=True)

    for copy in small[:2]:
        copy.wait()
    for i in range(parts):
        large[i].wait()
        over_planes(width, kb.shape[0], functools.partial(body, i * width))
    for copy in small[2:]:
        copy.wait()


def gated_kernel(
    j, lines, place_ref, block_ref, halo_ref, taps_ref, decay_ref, residues_ref,
    carried_ref, prefix_ref, last_ref, *refs,
):
    brought = []
    if len(refs) == 9:
        brought = [pltpu.make_async_copy(refs[0], refs[2], refs[-1])]
        refs = refs[1:2] + refs[3:-1]
    out_ref, qb, kb, vb, pb, ob = refs
    for copy in brought:
        copy.start()
    tokens, share = out_ref.shape
    poles = decay_ref.shape[0]
    steps = tokens // SUBLANES
    first = lax.rem(place_ref[0] + j, lines) * share
    since_start = (place_ref[0] * tokens).astype(F32)
    since_last = (place_ref[1] * tokens).astype(F32)
    upper = place_ref[1] != place_ref[0]
    place = lax.broadcasted_iota(jnp.int32, (SUBLANES, LANES), 0)
    before = (place * steps).astype(F32)

    def body(which, plane):
        lanes = lanes_at(plane, first)
        key = Convolved(block_ref, halo_ref, taps_ref, 1, lanes, kb.at[which])
        value = Convolved(block_ref, halo_ref, taps_ref, 2, lanes, vb.at[which])
        rates = decay_ref[:, lanes]
        every = jnp.exp(-rates)
        state = jnp.exp(-rates * since_start) * carried_ref[:, lanes] + prefix_ref[:, lanes]
        last = jnp.exp(-rates * since_last) * last_ref[:, lanes]
        state = state + jnp.where(upper, last, 0.0)
        fades = [spread(every[r : r + 1]) for r in range(poles)]
        sums = None
        for j in range(steps):
            product = key(j) * value(j)
            pb[which, j] = product
            if sums is None:
                sums = [product] * poles
            else:
                sums = [fades[r] * sums[r] + product for r in range(poles)]
        for r in range(poles):
            rate = spread(rates[r : r + 1])
            scan = fades[r] * sums[r]
            reach = 1
            while reach < SUBLANES:
                moved = jnp.where(place >= reach, pltpu.roll(scan, reach, 0), 0.0)
                scan = scan + jnp.exp(-rate * float(reach * steps)) * moved
                reach *= 2
            earlier = jnp.where(place >= 1, pltpu.roll(scan, 1, 0), 0.0)
            sums[r] = earlier + jnp.exp(-rate * before) * spread(state[r : r + 1])
        query = Convolved(block_ref, halo_ref, taps_ref, 0, lanes, qb.at[which])
        weights = [spread(residues_ref[r : r + 1, lanes]) for r in range(poles)]
        for j in range(steps):
            product = pb[which, j]
            if j:
                sums = [fades[r] * sums[r] + product for r in range(poles)]
            else:
                sums = [sums[r] + product for r in range(poles)]
            terms = [weights[r] * sums[r] for r in range(poles)]
            while len(terms) > 1:
                terms = [a + b for a, b in zip(terms[::2], terms[1::2])] + terms[len(terms) & ~1 :]
            ob[which, pl.ds(j, SUBLANES, stride=steps), :] = query(j) * terms[0]
        out_ref[:, lanes_at(plane)] = ob[which].astype(out_ref.dtype)

    over_planes(share, kb.shape[0], body)
    for copy in brought:
        copy.wait()


VMEM = pl.BlockSpec(memory_space=pltpu.VMEM)
SMEM = pl.BlockSpec(memory_space=pltpu.SMEM)
ROOM = pltpu.CompilerParams(vmem_limit_bytes=8 << 20)
TOGETHER = 2


def end_states(*arrays):
    features, _, rates = arrays[:3]
    _, tokens, count = features.shape
    poles = rates.shape[0]
    return pl.pallas_call(
        states_kernel,
        in_specs=[pl.BlockSpec(memory_space=pltpu.HBM)] * 5,
        out_specs=[VMEM] * 6,
        out_shape=[jax.ShapeDtypeStruct((poles, count), F32)]
        + [jax.ShapeDtypeStruct(array.shape, array.dtype) for array in arrays],
        scratch_shapes=[pltpu.VMEM((TOGETHER, PAD + tokens, LANES), F32)] * 2
        + [pltpu.SemaphoreType.DMA((math_gcd(count // LANES, 4) + 5,))],
        compiler_params=ROOM,
        cost_estimate=pl.CostEstimate(
            flops=4 * poles * tokens * count, bytes_accessed=6 * tokens * count, transcendentals=0
        ),
        name="end_states",
    )(*arrays)


def gated_half(j, lines, place, share, arrays, states, brought=()):
    tokens, poles = arrays[0].shape[1], states[0].shape[0]
    shapes = [jax.ShapeDtypeStruct((tokens, share), BF16)]
    shapes += [jax.ShapeDtypeStruct(array.shape, array.dtype) for array in brought]
    return pl.pallas_call(
        functools.partial(gated_kernel, j, lines),
        in_specs=[SMEM]
        + [VMEM] * (len(arrays) + len(states))
        + [pl.BlockSpec(memory_space=pltpu.HBM)] * len(brought),
        out_specs=[VMEM] * len(shapes),
        out_shape=shapes,
        scratch_shapes=[pltpu.VMEM((TOGETHER, PAD + tokens, LANES), F32)] * 3
        + [
            pltpu.VMEM((TOGETHER, tokens // SUBLANES, SUBLANES, LANES), F32),
            pltpu.VMEM((TOGETHER, tokens, LANES), F32),
        ]
        + [pltpu.SemaphoreType.DMA] * len(brought),
        compiler_params=ROOM,
        cost_estimate=pl.CostEstimate(
            flops=8 * poles * tokens * share, bytes_accessed=8 * tokens * share, transcendentals=0
        ),
        name="gated_half",
    )(place, *arrays, *states, *brought)


def shards(stream_in, features, conv_taps, decay, residues, state_in, out_weight):
    seqs, chans = lax.axis_size("seq"), lax.axis_size("chan")
    both = ("seq", "chan")
    lines = seqs // chans
    bits = chans.bit_length() - 1
    tokens = features.shape[1]
    share, columns = out_weight.shape
    here = lax.axis_index("seq")
    turned = [sum(((c >> i) & 1) << (bits - 1 - i) for i in range(bits)) for c in range(chans)]
    places = [(a, b, c) for a in range(chans) for b in range(lines) for c in range(chans)]

    def number(a, b, c):
        return (a * lines + b) * chans + c

    def moved(block, target):
        return lax.ppermute(block, both, [(number(*p), number(*target(*p))) for p in places])

    rates, weights, carried = decay.T, residues.T, state_in.T
    reach = conv_taps.shape[1] - 1
    halo = lax.ppermute(
        features[:, tokens - reach :, :], "seq", [(s, s + 1) for s in range(seqs - 1)]
    )
    ends, features, conv_taps, rates, weights, carried = end_states(
        features, conv_taps, rates, weights, carried
    )
    ends = ends + first_tokens(features[1:, :reach], halo[1:], conv_taps[1:], rates, tokens)
    prefix = jnp.zeros_like(ends)
    width = 1
    while True:
        other = lax.ppermute(ends, "seq", [(s, s ^ width) for s in range(seqs)])
        if 2 * width >= seqs:
            break
        upper = (here & width) != 0
        within = (here % width * tokens).astype(F32)
        fade = jnp.exp(-rates * float(width * tokens))
        prefix = prefix + jnp.where(upper, jnp.exp(-rates * within) * other, 0.0)
        ends = jnp.where(upper, ends + fade * other, other + fade * ends)
        width *= 2

    order = list(range(1, lines)) + [0]
    place = jnp.stack([here, here % width]).astype(jnp.int32)
    slots = {}
    for j in order:
        gated, *rest = gated_half(
            j, lines, place, share, (features, halo, conv_taps, rates, weights),
            (carried, prefix, other), [out_weight] if j == order[-1] else [],
        )
        slots[j] = [moved(gated, lambda a, b, c, j=j: (c, (b + j) % lines, turned[a ^ c]))]
    out_weight = rest[0]
    for i in range(bits):
        flip = 1 << (bits - 1 - i)
        for j in order:
            for slot in range(1 << i):
                slots[j].append(moved(slots[j][slot], lambda a, b, c: (a, b, c ^ flip)))

    pieces = math_gcd(PIECES, columns // LANES)
    size = columns // pieces
    totals = [stream_in[:, p * size : (p + 1) * size].astype(F32) for p in range(pieces)]
    for slot in range(chans):
        for p in range(pieces):
            weight = out_weight[:, p * size : (p + 1) * size]
            mixed = jnp.dot(slots[0][slot], weight, preferred_element_type=F32)
            for j in range(1, lines):
                part = jnp.dot(slots[j][slot], weight, preferred_element_type=F32).astype(BF16)
                part = moved(part, lambda a, b, c: (a, (b - j) % lines, c))
                mixed = mixed + part.astype(F32)
            mixed = moved(mixed.astype(BF16), lambda a, b, c: (a ^ turned[c] ^ slot, b, c))
            totals[p] = totals[p] + mixed.astype(F32)
    return jnp.concatenate([total.astype(BF16) for total in totals], axis=1)


def first_tokens(features, halo, taps, rates, tokens):
    features, halo = features.astype(F32), halo.astype(F32)
    reach = halo.shape[1]
    total = jnp.zeros_like(rates)
    for t in range(reach):
        inner = sum(taps[:, k] * features[:, t - k] for k in range(t + 1))
        outer = sum(taps[:, k] * halo[:, reach + t - k] for k in range(t + 1, reach + 1))
        change = inner[0] * outer[1] + outer[0] * (inner[1] + outer[1])
        total = total + jnp.exp(-rates * float(tokens - t)) * change
    return total


def solution(mesh):
    return jax.shard_map(
        shards,
        mesh=mesh,
        in_specs=(
            P("seq", "chan"),
            P(None, "seq", "chan"),
            P(None, None, "chan"),
            P("chan", None),
            P("chan", None),
            P("chan", None),
            P("seq", "chan"),
        ),
        out_specs=P("seq", "chan"),
        check_vma=False,
    )
```

profile of v0, /device:TPU:1, one launch (start us, length us, event | category | flops | bytes accessed | tf_op | source)
XLA Modules:
  0.0 115.4 jit_solution(9581793971961633704)
XLA Ops:
  0.0 0.9 slice.73
  0.9 3.9 %collective-permute-start = (bf16[3,2,2048]{2,1,0:T(2,128)(2,1)S(1)}, bf16[3,2,2048]{2,1,0:T(2,128)(2,1)S(1)}, u32[]{:S(2)}, u32[]{:S(2)}) collective-permute-start(bf16[3,2,2048]{2,1,0:T(2,128)(2,1)S(1)} %slice.73), channel_id=1, source_target_pairs={{0,4},{4,8},{8,12},{12,16},{16,20},{20,24},{24,28},{1,5},{5,9},{9,... | collective-permute-start | bytes 73736 | tf_op jit(solution)/shard_map/ppermute | solution.py:266
  4.9 0.0 copy-start.1
  4.9 1.4 %copy-done.1 = bf16[3,128,2048]{2,1,0:T(8,128)(2,1)S(1)} copy-done((bf16[3,128,2048]{2,1,0:T(8,128)(2,1)S(1)}, bf16[3,128,2048]{2,1,0:T(8,128)(2,1)}, u32[]{:S(2)}) %copy-start.1) | copy-done | bytes 1572888
  6.3 0.9 copy-done.2
  7.2 0.8 copy-done.3
  8.0 0.8 copy-done.4
  8.9 0.8 copy-done.5
  9.7 2.3 %end_states.1 = (f32[8,2048]{1,0:T(8,128)S(1)}, bf16[3,128,2048]{2,1,0:T(8,128)(2,1)S(1)}, f32[3,3,2048]{2,1,0:T(4,128)S(1)}, f32[8,2048]{1,0:T(8,128)S(1)}, f32...) custom-call(bf16[3,128,2048]{2,1,0:T(8,128)(2,1)S(1)} %copy-done.1, f32[3,3,2048]{2,1,0:T(4,128)S(1)} %copy-done.2, ...), custom_call_target="tpu_custom_call" | custom-call | flops 8388608 | bytes 1572864 | tf_op jit(solution)/shard_map/end_states/pallas_call | solution.py:206
  12.0 0.1 fusion.5
  12.2 1.3 %collective-permute-start.1 = (f32[8,2048]{1,0:T(8,128)S(1)}, f32[8,2048]{1,0:T(8,128)S(1)}, u32[]{:S(2)}, u32[]{:S(2)}) collective-permute-start(f32[8,2048]{1,0:T(8,128)S(1)} %add_add_fusion), channel_id=1, source_target_pairs={{0,4},{4,0},{8,12},{12,8},{16,20},{20,16},{24,28},{28,24},{1,5},{5... | collective-permute-start | bytes 196616 | tf_op jit(solution)/shard_map/ppermute | solution.py:276
  13.5 1.8 %collective-permute-done.1 = f32[8,2048]{1,0:T(8,128)S(1)} collective-permute-done((f32[8,2048]{1,0:T(8,128)S(1)}, f32[8,2048]{1,0:T(8,128)S(1)}, u32[]{:S(2)}, u32[]{:S(2)}) %collective-permute-start.1) | collective-permute-done | bytes 65568 | tf_op jit(solution)/shard_map/ppermute | solution.py:276
  15.4 1.4 %collective-permute-start.2 = (f32[8,2048]{1,0:T(8,128)S(1)}, f32[8,2048]{1,0:T(8,128)S(1)}, u32[]{:S(2)}, u32[]{:S(2)}) collective-permute-start(f32[8,2048]{1,0:T(8,128)S(1)} %add_select_fusion.1), channel_id=1, source_target_pairs={{0,8},{4,12},{8,0},{12,4},{16,24},{20,28},{24,16},{28,20},{1,9},{5... | collective-permute-start | bytes 196616 | tf_op jit(solution)/shard_map/ppermute | solution.py:276
  16.8 1.8 %collective-permute-done.2 = f32[8,2048]{1,0:T(8,128)S(1)} collective-permute-done((f32[8,2048]{1,0:T(8,128)S(1)}, f32[8,2048]{1,0:T(8,128)S(1)}, u32[]{:S(2)}, u32[]{:S(2)}) %collective-permute-start.2) | collective-permute-done | bytes 65568 | tf_op jit(solution)/shard_map/ppermute | solution.py:276
  18.6 0.1 add_select_fusion
  18.6 2.4 %collective-permute-start.3 = (f32[8,2048]{1,0:T(8,128)S(1)}, f32[8,2048]{1,0:T(8,128)S(1)}, u32[]{:S(2)}, u32[]{:S(2)}) collective-permute-start(f32[8,2048]{1,0:T(8,128)S(1)} %get-tuple-element.21), channel_id=1, source_target_pairs={{0,16},{4,20},{8,24},{12,28},{16,0},{20,4},{24,8},{28,12},{1,17},{... | collective-permute-start | bytes 196616 | tf_op jit(solution)/shard_map/ppermute | solution.py:276
  21.0 0.1 pad_add_fusion.place_ref
  21.1 1.6 %collective-permute-done.3.last_ref = f32[8,2048]{1,0:T(8,128)S(1)} collective-permute-done((f32[8,2048]{1,0:T(8,128)S(1)}, f32[8,2048]{1,0:T(8,128)S(1)}, u32[]{:S(2)}, u32[]{:S(2)}) %collective-permute-start.3) | collective-permute-done | bytes 65568 | tf_op jit(solution)/shard_map/ppermute | solution.py:276
  22.7 2.4 %gated_half.3 = bf16[128,1024]{1,0:T(8,128)(2,1)S(1)} custom-call(s32[2]{0:T(128)S(1)} %pad_add_fusion.place_ref, bf16[3,128,2048]{2,1,0:T(8,128)(2,1)S(1)} %get-tuple-element.13.block_ref, bf16[3,2,2048]{2,1,0:T(2,128)(2,1)S(1)} %collective-permute-done.halo_ref, f32[3,3,2048]{2,1,0:T(4,128)S(1)} %get-tuple-element.14.taps_ref, ...), custom_call_target="tpu_custom_call" | custom-call | flops 8388608 | bytes 1048576 | tf_op jit(solution)/shard_map/gated_half/pallas_call | solution.py:226
  25.1 7.6 %collective-permute-start.5 = (bf16[128,1024]{1,0:T(8,128)(2,1)S(1)}, bf16[128,1024]{1,0:T(8,128)(2,1)S(1)}, u32[]{:S(2)}, u32[]{:S(2)}) collective-permute-start(bf16[128,1024]{1,0:T(8,128)(2,1)S(1)} %gated_half.3), channel_id=1, source_target_pairs={{0,4},{1,14},{2,21},{3,31},{4,0},{5,10},{6,17},{7,27},{8,6},{9,12}... | collective-permute-start | bytes 786440 | tf_op jit(solution)/shard_map/ppermute | solution.py:262
  32.7 2.2 %copy-done = bf16[1024,2048]{1,0:T(8,128)(2,1)S(1)} copy-done((bf16[1024,2048]{1,0:T(8,128)(2,1)S(1)}, bf16[1024,2048]{1,0:T(8,128)(2,1)}, u32[]{:S(2)}) %copy-start) | copy-done | bytes 4194328
  34.9 2.7 %gated_half.2 = (bf16[128,1024]{1,0:T(8,128)(2,1)S(1)}, bf16[1024,2048]{1,0:T(8,128)(2,1)S(1)}) custom-call(s32[2]{0:T(128)S(1)} %pad_add_fusion.place_ref, bf16[3,128,2048]{2,1,0:T(8,128)(2,1)S(1)} %get-tuple-element.13.block_ref, bf16[3,2,2048]{2,1,0:T(2,128)(2,1)S(1)} %collective-permute-done.halo_ref, f32[3,3,2048]{2,1,0:T(4,128)S(1)} %get-tuple-element.14.taps_ref, ...), custom_call_target="tpu_custom_call" | custom-call | flops 8388608 | bytes 1048576 | tf_op jit(solution)/shard_map/gated_half/pallas_call | solution.py:226
  37.6 1.9 %collective-permute-start.4 = (bf16[128,1024]{1,0:T(8,128)(2,1)S(1)}, bf16[128,1024]{1,0:T(8,128)(2,1)S(1)}, u32[]{:S(2)}, u32[]{:S(2)}) collective-permute-start(bf16[128,1024]{1,0:T(8,128)(2,1)S(1)} %get-tuple-element.19), channel_id=1, source_target_pairs={{0,0},{1,10},{2,17},{3,27},{4,4},{5,14},{6,21},{7,31},{8,2},{9,8},... | collective-permute-start | bytes 786440 | tf_op jit(solution)/shard_map/ppermute | solution.py:262
  39.5 8.1 %collective-permute-done.5 = bf16[128,1024]{1,0:T(8,128)(2,1)S(1)} collective-permute-done((bf16[128,1024]{1,0:T(8,128)(2,1)S(1)}, bf16[128,1024]{1,0:T(8,128)(2,1)S(1)}, u32[]{:S(2)}, u32[]{:S(2)}) %collective-permute-start.5) | collective-permute-done | bytes 262176 | tf_op jit(solution)/shard_map/ppermute | solution.py:262
  47.6 0.7 convolution_convert_fusion.3
  48.3 1.2 %collective-permute-start.6 = (bf16[128,2048]{1,0:T(8,128)(2,1)S(1)}, bf16[128,2048]{1,0:T(8,128)(2,1)S(1)}, u32[]{:S(2)}, u32[]{:S(2)}) collective-permute-start(bf16[128,2048]{1,0:T(8,128)(2,1)S(1)} %convolution_convert_fusion.3), channel_id=1, source_target_pairs={{0,4},{1,5},{2,6},{3,7},{4,0},{5,1},{6,2},{7,3},{8,12},{9,13},{10,... | collective-permute-start | bytes 1572872 | tf_op jit(solution)/shard_map/ppermute | solution.py:262
  49.6 3.5 %collective-permute-done.4 = bf16[128,1024]{1,0:T(8,128)(2,1)S(1)} collective-permute-done((bf16[128,1024]{1,0:T(8,128)(2,1)S(1)}, bf16[128,1024]{1,0:T(8,128)(2,1)S(1)}, u32[]{:S(2)}, u32[]{:S(2)}) %collective-permute-start.4) | collective-permute-done | bytes 262176 | tf_op jit(solution)/shard_map/ppermute | solution.py:262
  53.1 0.7 convolution_convert_fusion.2
  53.9 2.0 %collective-permute-start.10 = (bf16[128,2048]{1,0:T(8,128)(2,1)S(1)}, bf16[128,2048]{1,0:T(8,128)(2,1)S(1)}, u32[]{:S(2)}, u32[]{:S(2)}) collective-permute-start(bf16[128,2048]{1,0:T(8,128)(2,1)S(1)} %convolution_convert_fusion.2), channel_id=1, source_target_pairs={{0,4},{1,5},{2,6},{3,7},{4,0},{5,1},{6,2},{7,3},{8,12},{9,13},{10,... | collective-permute-start | bytes 1572872 | tf_op jit(solution)/shard_map/ppermute | solution.py:262
  55.9 0.7 convolution_convert_fusion.1
  56.6 0.1 collective-permute-start.14
  56.7 2.2 %collective-permute-done.8 = bf16[128,1024]{1,0:T(8,128)(2,1)S(1)} collective-permute-done((bf16[128,1024]{1,0:T(8,128)(2,1)S(1)}, bf16[128,1024]{1,0:T(8,128)(2,1)S(1)}, u32[]{:S(2)}, u32[]{:S(2)}) %collective-permute-start.8) | collective-permute-done | bytes 262176 | tf_op jit(solution)/shard_map/ppermute | solution.py:262
  58.9 3.5 %collective-permute-done.6 = bf16[128,2048]{1,0:T(8,128)(2,1)S(1)} collective-permute-done((bf16[128,2048]{1,0:T(8,128)(2,1)S(1)}, bf16[128,2048]{1,0:T(8,128)(2,1)S(1)}, u32[]{:S(2)}, u32[]{:S(2)}) %collective-permute-start.6) | collective-permute-done | bytes 524320 | tf_op jit(solution)/shard_map/ppermute | solution.py:262
  62.4 0.7 fusion
  63.1 5.1 %collective-permute-start.7 = (bf16[128,2048]{1,0:T(8,128)(2,1)S(1)}, bf16[128,2048]{1,0:T(8,128)(2,1)S(1)}, u32[]{:S(2)}, u32[]{:S(2)}) collective-permute-start(bf16[128,2048]{1,0:T(8,128)(2,1)S(1)} %fusion), channel_id=1, source_target_pairs={{0,0},{1,17},{2,10},{3,27},{4,4},{5,21},{6,14},{7,31},{8,8},{9,25}... | collective-permute-start | bytes 1572872 | tf_op jit(solution)/shard_map/ppermute | solution.py:262
  68.2 0.7 convolution_convert_fusion
  68.9 4.6 %collective-permute-done.10 = bf16[128,2048]{1,0:T(8,128)(2,1)S(1)} collective-permute-done((bf16[128,2048]{1,0:T(8,128)(2,1)S(1)}, bf16[128,2048]{1,0:T(8,128)(2,1)S(1)}, u32[]{:S(2)}, u32[]{:S(2)}) %collective-permute-start.10) | collective-permute-done | bytes 524320 | tf_op jit(solution)/shard_map/ppermute | solution.py:262
  73.6 1.2 %collective-permute-start.18 = (bf16[128,2048]{1,0:T(8,128)(2,1)S(1)}, bf16[128,2048]{1,0:T(8,128)(2,1)S(1)}, u32[]{:S(2)}, u32[]{:S(2)}) collective-permute-start(bf16[128,2048]{1,0:T(8,128)(2,1)S(1)} %convolution_convert_fusion), channel_id=1, source_target_pairs={{0,4},{1,5},{2,6},{3,7},{4,0},{5,1},{6,2},{7,3},{8,12},{9,13},{10,... | collective-permute-start | bytes 1572872 | tf_op jit(solution)/shard_map/ppermute | solution.py:262
  74.8 0.7 fusion.1
  75.5 2.1 %collective-permute-start.11 = (bf16[128,2048]{1,0:T(8,128)(2,1)S(1)}, bf16[128,2048]{1,0:T(8,128)(2,1)S(1)}, u32[]{:S(2)}, u32[]{:S(2)}) collective-permute-start(bf16[128,2048]{1,0:T(8,128)(2,1)S(1)} %fusion.1), channel_id=1, source_target_pairs={{0,8},{1,25},{2,2},{3,19},{4,12},{5,29},{6,6},{7,23},{8,0},{9,17},... | collective-permute-start | bytes 1572872 | tf_op jit(solution)/shard_map/ppermute | solution.py:262
  77.6 7.2 %collective-permute-done.14 = bf16[128,2048]{1,0:T(8,128)(2,1)S(1)} collective-permute-done((bf16[128,2048]{1,0:T(8,128)(2,1)S(1)}, bf16[128,2048]{1,0:T(8,128)(2,1)S(1)}, u32[]{:S(2)}, u32[]{:S(2)}) %collective-permute-start.14) | collective-permute-done | bytes 524320 | tf_op jit(solution)/shard_map/ppermute | solution.py:262
  84.8 0.7 fusion.2
  85.6 0.7 collective-permute-start.15
  86.3 8.1 %collective-permute-done.18 = bf16[128,2048]{1,0:T(8,128)(2,1)S(1)} collective-permute-done((bf16[128,2048]{1,0:T(8,128)(2,1)S(1)}, bf16[128,2048]{1,0:T(8,128)(2,1)S(1)}, u32[]{:S(2)}, u32[]{:S(2)}) %collective-permute-start.18) | collective-permute-done | bytes 524320 | tf_op jit(solution)/shard_map/ppermute | solution.py:262
  94.4 0.7 fusion.3
  95.1 3.2 %collective-permute-start.19 = (bf16[128,2048]{1,0:T(8,128)(2,1)S(1)}, bf16[128,2048]{1,0:T(8,128)(2,1)S(1)}, u32[]{:S(2)}, u32[]{:S(2)}) collective-permute-start(bf16[128,2048]{1,0:T(8,128)(2,1)S(1)} %fusion.3), channel_id=1, source_target_pairs={{0,24},{1,9},{2,18},{3,3},{4,28},{5,13},{6,22},{7,7},{8,16},{9,1},... | collective-permute-start | bytes 1572872 | tf_op jit(solution)/shard_map/ppermute | solution.py:262
  98.3 15.8 %collective-permute-done.19 = bf16[128,2048]{1,0:T(8,128)(2,1)S(1)} collective-permute-done((bf16[128,2048]{1,0:T(8,128)(2,1)S(1)}, bf16[128,2048]{1,0:T(8,128)(2,1)S(1)}, u32[]{:S(2)}, u32[]{:S(2)}) %collective-permute-start.19) | collective-permute-done | bytes 524320 | tf_op jit(solution)/shard_map/ppermute | solution.py:262
  114.1 1.3 %add_convert_fusion = bf16[128,2048]{1,0:T(8,128)(2,1)} fusion(bf16[128,2048]{1,0:T(8,128)(2,1)S(1)} %collective-permute-done.19, bf16[128,2048]{1,0:T(8,128)(2,1)S(1)} %collective-permute-done.15, bf16[128,2048]{1,0:T(8,128)(2,1)S(1)} %collective-permute-done.11, bf16[128,2048]{1,0:T(8,128)(2,1)S(1)} %collective-permute-done.7, ...), kind=kLoop, calls=%fused_computation.12 | loop fusion | flops 2621440 | bytes 3145728 | tf_op jit(solution)/shard_map/convert_element_type | solution.py:315
  (27 shorter events, 0.2 us)
Async XLA Ops:
  0.9 11.1 %collective-permute-start = (bf16[3,2,2048]{2,1,0:T(2,128)(2,1)S(1)}, bf16[3,2,2048]{2,1,0:T(2,128)(2,1)S(1)}, u32[]{:S(2)}, u32[]{:S(2)}) collective-permute-start(bf16[3,2,2048]{2,1,0:T(2,128)(2,1)S(1)} %slice.73), channel_id=1, source_target_pairs={{0,4},{4,8},{8,12},{12,16},{16,20},{20,24},{24,28},{1,5},{5,9},{9,... | collective-permute-start | bytes 73736 | tf_op jit(solution)/shard_map/ppermute | solution.py:266
  4.9 1.4 %copy-start.1 = (bf16[3,128,2048]{2,1,0:T(8,128)(2,1)S(1)}, bf16[3,128,2048]{2,1,0:T(8,128)(2,1)}, u32[]{:S(2)}) copy-start(bf16[3,128,2048]{2,1,0:T(8,128)(2,1)} %block_hbm.1) | copy-start | bytes 4718596
  6.3 0.9 copy-start.2
  7.2 0.8 copy-start.3
  8.0 0.8 copy-start.4
  8.9 0.8 copy-start.5
  12.2 3.2 %collective-permute-start.1 = (f32[8,2048]{1,0:T(8,128)S(1)}, f32[8,2048]{1,0:T(8,128)S(1)}, u32[]{:S(2)}, u32[]{:S(2)}) collective-permute-start(f32[8,2048]{1,0:T(8,128)S(1)} %add_add_fusion), channel_id=1, source_target_pairs={{0,4},{4,0},{8,12},{12,8},{16,20},{20,16},{24,28},{28,24},{1,5},{5... | collective-permute-start | bytes 196616 | tf_op jit(solution)/shard_map/ppermute | solution.py:276
  15.4 3.2 %collective-permute-start.2 = (f32[8,2048]{1,0:T(8,128)S(1)}, f32[8,2048]{1,0:T(8,128)S(1)}, u32[]{:S(2)}, u32[]{:S(2)}) collective-permute-start(f32[8,2048]{1,0:T(8,128)S(1)} %add_select_fusion.1), channel_id=1, source_target_pairs={{0,8},{4,12},{8,0},{12,4},{16,24},{20,28},{24,16},{28,20},{1,9},{5... | collective-permute-start | bytes 196616 | tf_op jit(solution)/shard_map/ppermute | solution.py:276
  18.6 4.1 %collective-permute-start.3 = (f32[8,2048]{1,0:T(8,128)S(1)}, f32[8,2048]{1,0:T(8,128)S(1)}, u32[]{:S(2)}, u32[]{:S(2)}) collective-permute-start(f32[8,2048]{1,0:T(8,128)S(1)} %get-tuple-element.21), channel_id=1, source_target_pairs={{0,16},{4,20},{8,24},{12,28},{16,0},{20,4},{24,8},{28,12},{1,17},{... | collective-permute-start | bytes 196616 | tf_op jit(solution)/shard_map/ppermute | solution.py:276
  25.1 22.5 %collective-permute-start.5 = (bf16[128,1024]{1,0:T(8,128)(2,1)S(1)}, bf16[128,1024]{1,0:T(8,128)(2,1)S(1)}, u32[]{:S(2)}, u32[]{:S(2)}) collective-permute-start(bf16[128,1024]{1,0:T(8,128)(2,1)S(1)} %gated_half.3), channel_id=1, source_target_pairs={{0,4},{1,14},{2,21},{3,31},{4,0},{5,10},{6,17},{7,27},{8,6},{9,12}... | collective-permute-start | bytes 786440 | tf_op jit(solution)/shard_map/ppermute | solution.py:262
  32.7 2.2 %copy-start = (bf16[1024,2048]{1,0:T(8,128)(2,1)S(1)}, bf16[1024,2048]{1,0:T(8,128)(2,1)}, u32[]{:S(2)}) copy-start(bf16[1024,2048]{1,0:T(8,128)(2,1)} %refs_0_.1) | copy-start | bytes 12582916
  37.6 15.5 %collective-permute-start.4 = (bf16[128,1024]{1,0:T(8,128)(2,1)S(1)}, bf16[128,1024]{1,0:T(8,128)(2,1)S(1)}, u32[]{:S(2)}, u32[]{:S(2)}) collective-permute-start(bf16[128,1024]{1,0:T(8,128)(2,1)S(1)} %get-tuple-element.19), channel_id=1, source_target_pairs={{0,0},{1,10},{2,17},{3,27},{4,4},{5,14},{6,21},{7,31},{8,2},{9,8},... | collective-permute-start | bytes 786440 | tf_op jit(solution)/shard_map/ppermute | solution.py:262
  47.6 5.5 %collective-permute-start.9 = (bf16[128,1024]{1,0:T(8,128)(2,1)S(1)}, bf16[128,1024]{1,0:T(8,128)(2,1)S(1)}, u32[]{:S(2)}, u32[]{:S(2)}) collective-permute-start(bf16[128,1024]{1,0:T(8,128)(2,1)S(1)} %collective-permute-done.5), channel_id=1, source_target_pairs={{0,2},{1,3},{2,0},{3,1},{4,6},{5,7},{6,4},{7,5},{8,10},{9,11},{10,... | collective-permute-start | bytes 786440 | tf_op jit(solution)/shard_map/ppermute | solution.py:262
  48.3 14.0 %collective-permute-start.6 = (bf16[128,2048]{1,0:T(8,128)(2,1)S(1)}, bf16[128,2048]{1,0:T(8,128)(2,1)S(1)}, u32[]{:S(2)}, u32[]{:S(2)}) collective-permute-start(bf16[128,2048]{1,0:T(8,128)(2,1)S(1)} %convolution_convert_fusion.3), channel_id=1, source_target_pairs={{0,4},{1,5},{2,6},{3,7},{4,0},{5,1},{6,2},{7,3},{8,12},{9,13},{10,... | collective-permute-start | bytes 1572872 | tf_op jit(solution)/shard_map/ppermute | solution.py:262
  49.6 6.3 %collective-permute-start.13 = (bf16[128,1024]{1,0:T(8,128)(2,1)S(1)}, bf16[128,1024]{1,0:T(8,128)(2,1)S(1)}, u32[]{:S(2)}, u32[]{:S(2)}) collective-permute-start(bf16[128,1024]{1,0:T(8,128)(2,1)S(1)} %collective-permute-done.5), channel_id=1, source_target_pairs={{0,1},{1,0},{2,3},{3,2},{4,5},{5,4},{6,7},{7,6},{8,9},{9,8},{10,11... | collective-permute-start | bytes 786440 | tf_op jit(solution)/shard_map/ppermute | solution.py:262
  53.1 5.8 %collective-permute-start.8 = (bf16[128,1024]{1,0:T(8,128)(2,1)S(1)}, bf16[128,1024]{1,0:T(8,128)(2,1)S(1)}, u32[]{:S(2)}, u32[]{:S(2)}) collective-permute-start(bf16[128,1024]{1,0:T(8,128)(2,1)S(1)} %collective-permute-done.4), channel_id=1, source_target_pairs={{0,2},{1,3},{2,0},{3,1},{4,6},{5,7},{6,4},{7,5},{8,10},{9,11},{10,... | collective-permute-start | bytes 786440 | tf_op jit(solution)/shard_map/ppermute | solution.py:262
  53.1 22.4 %collective-permute-start.12 = (bf16[128,1024]{1,0:T(8,128)(2,1)S(1)}, bf16[128,1024]{1,0:T(8,128)(2,1)S(1)}, u32[]{:S(2)}, u32[]{:S(2)}) collective-permute-start(bf16[128,1024]{1,0:T(8,128)(2,1)S(1)} %collective-permute-done.4), channel_id=1, source_target_pairs={{0,1},{1,0},{2,3},{3,2},{4,5},{5,4},{6,7},{7,6},{8,9},{9,8},{10,11... | collective-permute-start | bytes 786440 | tf_op jit(solution)/shard_map/ppermute | solution.py:262
  53.9 19.7 %collective-permute-start.10 = (bf16[128,2048]{1,0:T(8,128)(2,1)S(1)}, bf16[128,2048]{1,0:T(8,128)(2,1)S(1)}, u32[]{:S(2)}, u32[]{:S(2)}) collective-permute-start(bf16[128,2048]{1,0:T(8,128)(2,1)S(1)} %convolution_convert_fusion.2), channel_id=1, source_target_pairs={{0,4},{1,5},{2,6},{3,7},{4,0},{5,1},{6,2},{7,3},{8,12},{9,13},{10,... | collective-permute-start | bytes 1572872 | tf_op jit(solution)/shard_map/ppermute | solution.py:262
  56.6 28.2 %collective-permute-start.14 = (bf16[128,2048]{1,0:T(8,128)(2,1)S(1)}, bf16[128,2048]{1,0:T(8,128)(2,1)S(1)}, u32[]{:S(2)}, u32[]{:S(2)}) collective-permute-start(bf16[128,2048]{1,0:T(8,128)(2,1)S(1)} %convolution_convert_fusion.1), channel_id=1, source_target_pairs={{0,4},{1,5},{2,6},{3,7},{4,0},{5,1},{6,2},{7,3},{8,12},{9,13},{10,... | collective-permute-start | bytes 1572872 | tf_op jit(solution)/shard_map/ppermute | solution.py:262
  58.9 4.2 %collective-permute-start.17 = (bf16[128,1024]{1,0:T(8,128)(2,1)S(1)}, bf16[128,1024]{1,0:T(8,128)(2,1)S(1)}, u32[]{:S(2)}, u32[]{:S(2)}) collective-permute-start(bf16[128,1024]{1,0:T(8,128)(2,1)S(1)} %collective-permute-done.9), channel_id=1, source_target_pairs={{0,1},{1,0},{2,3},{3,2},{4,5},{5,4},{6,7},{7,6},{8,9},{9,8},{10,11... | collective-permute-start | bytes 786440 | tf_op jit(solution)/shard_map/ppermute | solution.py:262
  62.4 23.9 %collective-permute-start.16 = (bf16[128,1024]{1,0:T(8,128)(2,1)S(1)}, bf16[128,1024]{1,0:T(8,128)(2,1)S(1)}, u32[]{:S(2)}, u32[]{:S(2)}) collective-permute-start(bf16[128,1024]{1,0:T(8,128)(2,1)S(1)} %collective-permute-done.8), channel_id=1, source_target_pairs={{0,1},{1,0},{2,3},{3,2},{4,5},{5,4},{6,7},{7,6},{8,9},{9,8},{10,11... | collective-permute-start | bytes 786440 | tf_op jit(solution)/shard_map/ppermute | solution.py:262
  63.1 35.2 %collective-permute-start.7 = (bf16[128,2048]{1,0:T(8,128)(2,1)S(1)}, bf16[128,2048]{1,0:T(8,128)(2,1)S(1)}, u32[]{:S(2)}, u32[]{:S(2)}) collective-permute-start(bf16[128,2048]{1,0:T(8,128)(2,1)S(1)} %fusion), channel_id=1, source_target_pairs={{0,0},{1,17},{2,10},{3,27},{4,4},{5,21},{6,14},{7,31},{8,8},{9,25}... | collective-permute-start | bytes 1572872 | tf_op jit(solution)/shard_map/ppermute | solution.py:262
  73.6 20.8 %collective-permute-start.18 = (bf16[128,2048]{1,0:T(8,128)(2,1)S(1)}, bf16[128,2048]{1,0:T(8,128)(2,1)S(1)}, u32[]{:S(2)}, u32[]{:S(2)}) collective-permute-start(bf16[128,2048]{1,0:T(8,128)(2,1)S(1)} %convolution_convert_fusion), channel_id=1, source_target_pairs={{0,4},{1,5},{2,6},{3,7},{4,0},{5,1},{6,2},{7,3},{8,12},{9,13},{10,... | collective-permute-start | bytes 1572872 | tf_op jit(solution)/shard_map/ppermute | solution.py:262
  75.5 38.6 %copy-start.6 = (bf16[128,2048]{1,0:T(8,128)(2,1)S(1)}, bf16[128,2048]{1,0:T(8,128)(2,1)}, u32[]{:S(2)}) copy-start(bf16[128,2048]{1,0:T(8,128)(2,1)} %param.7) | copy-start | bytes 1572868
  75.5 22.7 %collective-permute-start.11 = (bf16[128,2048]{1,0:T(8,128)(2,1)S(1)}, bf16[128,2048]{1,0:T(8,128)(2,1)S(1)}, u32[]{:S(2)}, u32[]{:S(2)}) collective-permute-start(bf16[128,2048]{1,0:T(8,128)(2,1)S(1)} %fusion.1), channel_id=1, source_target_pairs={{0,8},{1,25},{2,2},{3,19},{4,12},{5,29},{6,6},{7,23},{8,0},{9,17},... | collective-permute-start | bytes 1572872 | tf_op jit(solution)/shard_map/ppermute | solution.py:262
  85.6 12.7 %collective-permute-start.15 = (bf16[128,2048]{1,0:T(8,128)(2,1)S(1)}, bf16[128,2048]{1,0:T(8,128)(2,1)S(1)}, u32[]{:S(2)}, u32[]{:S(2)}) collective-permute-start(bf16[128,2048]{1,0:T(8,128)(2,1)S(1)} %fusion.2), channel_id=1, source_target_pairs={{0,16},{1,1},{2,26},{3,11},{4,20},{5,5},{6,30},{7,15},{8,24},{9,9}... | collective-permute-start | bytes 1572872 | tf_op jit(solution)/shard_map/ppermute | solution.py:262
  95.1 19.0 %collective-permute-start.19 = (bf16[128,2048]{1,0:T(8,128)(2,1)S(1)}, bf16[128,2048]{1,0:T(8,128)(2,1)S(1)}, u32[]{:S(2)}, u32[]{:S(2)}) collective-permute-start(bf16[128,2048]{1,0:T(8,128)(2,1)S(1)} %fusion.3), channel_id=1, source_target_pairs={{0,24},{1,9},{2,18},{3,3},{4,28},{5,13},{6,22},{7,7},{8,16},{9,1},... | collective-permute-start | bytes 1572872 | tf_op jit(solution)/shard_map/ppermute | solution.py:262
where the time goes:
time: 116 us; the launch traced here: 115 us
  waiting for transfers between devices  58.4 us (50%)
  starting transfers between devices  34 us (29%)
  local copies, waits for them, and re-layouts  7.93 us (7%)
  Pallas kernels  7.37 us (6%)
  matrix products  5.85 us (5%)
  other arithmetic  1.6 us (1%)
    ppermute x16, waiting for transfers between devices, moved(): lax.ppermute(block, both, [(number(*p), number(*target(*p))) for p in pla...  53.1 us
    ppermute x16, starting transfers between devices, moved(): lax.ppermute(block, both, [(number(*p), number(*target(*p))) for p in pla...  25 us
    unnamed x14, local copies, waits for them, and re-layouts  7.01 us
    ppermute x3, waiting for transfers between devices, shards(): other = lax.ppermute(ends, 'seq', [(s, s ^ width) for s in range(seqs)])  5.29 us
    pallas_call x2, Pallas kernels, gated_half(): pl.pallas_call(functools.partial(gated_kernel, j, lines), in_specs=[SMEM]...  5.11 us
    ppermute x3, starting transfers between devices, shards(): other = lax.ppermute(ends, 'seq', [(s, s ^ width) for s in range(seqs)])  5.08 us
    ppermute x1, starting transfers between devices, shards(): lax.ppermute(features[:, tokens - reach:, :], 'seq', [(s, s + 1) for s in...  3.93 us
    dot_general x4, matrix products, shards(): mixed = jnp.dot(slots[0][slot], weight, preferred_element_type=F32)  2.93 us
  transfers between devices with their start and end apart: 20, of which 11 were waited for; matrix products, arithmetic and copies ran while one was open for 5% of the time, Pallas kernels for 4%

commit v1 on v0

--- a/solution.py
+++ b/solution.py
@@ -13,7 +13,6 @@
 LANES = 128
 SUBLANES = 8
 PAD = 8
-PIECES = 1
 
 
 class Convolved:
@@ -126,17 +125,11 @@
 
 
 def gated_kernel(
-    j, lines, place_ref, block_ref, halo_ref, taps_ref, decay_ref, residues_ref,
+    j, lines, parts, place_ref, block_ref, halo_ref, taps_ref, decay_ref, residues_ref,
     carried_ref, prefix_ref, last_ref, *refs,
 ):
-    brought = []
-    if len(refs) == 9:
-        brought = [pltpu.make_async_copy(refs[0], refs[2], refs[-1])]
-        refs = refs[1:2] + refs[3:-1]
-    out_ref, qb, kb, vb, pb, ob = refs
-    for copy in brought:
-        copy.start()
-    tokens, share = out_ref.shape
+    *out_refs, qb, kb, vb, pb, ob = refs[len(refs) - parts - 5 :]
+    tokens, share = block_ref.shape[1], out_refs[0].shape[1]
     poles = decay_ref.shape[0]
     steps = tokens // SUBLANES
     first = lax.rem(place_ref[0] + j, lines) * share
@@ -186,11 +179,12 @@
             while len(terms) > 1:
                 terms = [a + b for a, b in zip(terms[::2], terms[1::2])] + terms[len(terms) & ~1 :]
             ob[which, pl.ds(j, SUBLANES, stride=steps), :] = query(j) * terms[0]
-        out_ref[:, lanes_at(plane)] = ob[which].astype(out_ref.dtype)
+        for i, out_ref in enumerate(out_refs):
+            rows = out_ref.shape[0]
+            part = ob[which, i * rows : (i + 1) * rows]
+            out_ref[:, lanes_at(plane)] = part.astype(out_ref.dtype)
 
     over_planes(share, kb.shape[0], body)
-    for copy in brought:
-        copy.wait()
 
 
 VMEM = pl.BlockSpec(memory_space=pltpu.VMEM)
@@ -219,23 +213,20 @@
     )(*arrays)
 
 
-def gated_half(j, lines, place, share, arrays, states, brought=()):
+def gated_half(j, lines, parts, place, share, arrays, states, brought=()):
     tokens, poles = arrays[0].shape[1], states[0].shape[0]
-    shapes = [jax.ShapeDtypeStruct((tokens, share), BF16)]
-    shapes += [jax.ShapeDtypeStruct(array.shape, array.dtype) for array in brought]
+    shapes = [jax.ShapeDtypeStruct((tokens // parts, share), BF16)] * parts
     return pl.pallas_call(
-        functools.partial(gated_kernel, j, lines),
+        functools.partial(gated_kernel, j, lines, parts),
         in_specs=[SMEM]
-        + [VMEM] * (len(arrays) + len(states))
-        + [pl.BlockSpec(memory_space=pltpu.HBM)] * len(brought),
+        + [VMEM] * (len(arrays) + len(states) + len(brought)),
         out_specs=[VMEM] * len(shapes),
         out_shape=shapes,
         scratch_shapes=[pltpu.VMEM((TOGETHER, PAD + tokens, LANES), F32)] * 3
         + [
             pltpu.VMEM((TOGETHER, tokens // SUBLANES, SUBLANES, LANES), F32),
             pltpu.VMEM((TOGETHER, tokens, LANES), F32),
-        ]
-        + [pltpu.SemaphoreType.DMA] * len(brought),
+        ],
         compiler_params=ROOM,
         cost_estimate=pl.CostEstimate(
             flops=8 * poles * tokens * share, bytes_accessed=8 * tokens * share, transcendentals=0
@@ -250,7 +241,7 @@
     lines = seqs // chans
     bits = chans.bit_length() - 1
     tokens = features.shape[1]
-    share, columns = out_weight.shape
+    share, _ = out_weight.shape
     here = lax.axis_index("seq")
     turned = [sum(((c >> i) & 1) << (bits - 1 - i) for i in range(bits)) for c in range(chans)]
     places = [(a, b, c) for a in range(chans) for b in range(lines) for c in range(chans)]
@@ -285,34 +276,71 @@
 
     order = list(range(1, lines)) + [0]
     place = jnp.stack([here, here % width]).astype(jnp.int32)
-    slots = {}
+    top = chans >> 1
+    blocks = {}
     for j in order:
-        gated, *rest = gated_half(
-            j, lines, place, share, (features, halo, conv_taps, rates, weights),
-            (carried, prefix, other), [out_weight] if j == order[-1] else [],
+        results = gated_half(
+            j, lines, 2 if j else 1, place, share, (features, halo, conv_taps, rates, weights),
+            (carried, prefix, other), [],
         )
-        slots[j] = [moved(gated, lambda a, b, c, j=j: (c, (b + j) % lines, turned[a ^ c]))]
-    out_weight = rest[0]
-    for i in range(bits):
-        flip = 1 << (bits - 1 - i)
-        for j in order:
+        blocks[j] = [moved(results[0], lambda a, b, c: (c, (b + j) % lines, turned[a ^ c]))]
+        if j:
+            other_half = moved(results[1], lambda a, b, c: (a, b, c ^ top))
+            blocks[j].append(
+                moved(other_half, lambda a, b, c: (c ^ top, (b + j) % lines, turned[a ^ c ^ top]))
+            )
+
+    odd = lax.axis_index("chan") % 2 == 1
+    pieces = {}
+    for j in order:
+        lower = [jnp.concatenate(blocks[j], axis=0) if len(blocks[j]) > 1 else blocks[j][0]]
+        sides = {}
+
+        def beside(slot):
+            return moved(lower[slot], lambda a, b, c: (a, b, c ^ 1))
+
+        sides[0] = beside(0)
+        for i in range(bits - 1):
+            flip = top >> i
             for slot in range(1 << i):
-                slots[j].append(moved(slots[j][slot], lambda a, b, c: (a, b, c ^ flip)))
-
-    pieces = math_gcd(PIECES, columns // LANES)
-    size = columns // pieces
-    totals = [stream_in[:, p * size : (p + 1) * size].astype(F32) for p in range(pieces)]
-    for slot in range(chans):
-        for p in range(pieces):
-            weight = out_weight[:, p * size : (p + 1) * size]
-            mixed = jnp.dot(slots[0][slot], weight, preferred_element_type=F32)
-            for j in range(1, lines):
-                part = jnp.dot(slots[j][slot], weight, preferred_element_type=F32).astype(BF16)
-                part = moved(part, lambda a, b, c: (a, (b - j) % lines, c))
-                mixed = mixed + part.astype(F32)
-            mixed = moved(mixed.astype(BF16), lambda a, b, c: (a ^ turned[c] ^ slot, b, c))
-            totals[p] = totals[p] + mixed.astype(F32)
-    return jnp.concatenate([total.astype(BF16) for total in totals], axis=1)
+                new = slot + (1 << i)
+                lower.append(moved(lower[slot], lambda a, b, c: (a, b, c ^ flip)))
+                sides[new] = beside(new)
+        for slot in range(top):
+            for group, pair in enumerate([(lower[slot], sides[slot]), (sides[slot], lower[slot])]):
+                pieces[j, group, slot] = product_of(jnp.where(odd, *pair), out_weight, j)
+
+    half = tokens // 2
+    totals = [stream_in[p * half : (p + 1) * half].astype(F32) for p in range(2)]
+    for group in range(2):
+        for slot in range(top):
+            cut = group == 0 and slot == 0
+            own = [pieces[0, group, slot]]
+            if cut:
+                own = lax.optimization_barrier((own[0][:half], own[0][half:]))
+            for p in range(2 if cut else 1):
+                start = p * half
+                stop = start + (half if cut else tokens)
+                mixed = own[p]
+                for j in range(1, lines):
+                    part = moved(
+                        pieces[j, group, slot][start:stop], lambda a, b, c: (a, (b - j) % lines, c)
+                    )
+                    mixed = mixed + part.astype(F32)
+
+                def target(a, b, c):
+                    return a ^ turned[c] ^ (slot + top * (c % 2 == group)), b, c
+
+                mixed = moved(mixed.astype(BF16), target)
+                for i in [p] if cut else [0, 1]:
+                    part = mixed if cut else mixed[i * half : (i + 1) * half]
+                    totals[i] = totals[i] + part.astype(F32)
+    return jnp.concatenate([total.astype(BF16) for total in totals], axis=0)
+
+
+def product_of(block, weight, j):
+    product = jnp.dot(block, weight, preferred_element_type=F32)
+    return product.astype(BF16) if j else lax.optimization_barrier(product)
 
 
 def first_tokens(features, halo, taps, rates, tokens):

time: 116 us -> 134 us (1.16)
  the two profiles are of different devices: /device:TPU:1 before, /device:TPU:0 now
where the time goes in v1:
time: 134 us; the launch traced here: 133 us
  waiting for transfers between devices  69.1 us (52%)
  starting transfers between devices  40.7 us (30%)
  matrix products  8.06 us (6%)
  Pallas kernels  7.1 us (5%)
  local copies, waits for them, and re-layouts  5.87 us (4%)
  other arithmetic  2.01 us (1%)
    ppermute x20, waiting for transfers between devices, moved(): lax.ppermute(block, both, [(number(*p), number(*target(*p))) for p in pla...  61.4 us
    ppermute x20, starting transfers between devices, moved(): lax.ppermute(block, both, [(number(*p), number(*target(*p))) for p in pla...  29.8 us
    dot_general x8, matrix products, product_of(): product = jnp.dot(block, weight, preferred_element_type=F32)  8.06 us
    ppermute x3, waiting for transfers between devices, shards(): other = lax.ppermute(ends, 'seq', [(s, s ^ width) for s in range(seqs)])  7.75 us
    ppermute x3, starting transfers between devices, shards(): other = lax.ppermute(ends, 'seq', [(s, s ^ width) for s in range(seqs)])  6.06 us
    ppermute x1, starting transfers between devices, shards(): lax.ppermute(features[:, tokens - reach:, :], 'seq', [(s, s + 1) for s in...  4.87 us
    unnamed x15, local copies, waits for them, and re-layouts  4.83 us
    pallas_call x2, Pallas kernels, gated_half(): pl.pallas_call(functools.partial(gated_kernel, j, lines, parts), in_specs...  4.81 us
  transfers between devices with their start and end apart: 24, of which 12 were waited for; matrix products, arithmetic and copies ran while one was open for 7% of the time, Pallas kernels for 4%

profile of v1, /device:TPU:0, one launch (start us, length us, event | category | flops | bytes accessed | tf_op | source)
XLA Modules:
  0.0 133.3 jit_solution(2553435238730097978)
XLA Ops:
  0.0 0.9 slice.110
  0.9 4.9 %collective-permute-start = (bf16[3,2,2048]{2,1,0:T(2,128)(2,1)S(1)}, bf16[3,2,2048]{2,1,0:T(2,128)(2,1)S(1)}, u32[]{:S(2)}, u32[]{:S(2)}) collective-permute-start(bf16[3,2,2048]{2,1,0:T(2,128)(2,1)S(1)} %slice.110), channel_id=1, source_target_pairs={{0,4},{4,8},{8,12},{12,16},{16,20},{20,24},{24,28},{1,5},{5,9},{9,... | collective-permute-start | bytes 73736 | tf_op jit(solution)/shard_map/ppermute | solution.py:257
  5.8 1.4 %copy-done = bf16[3,128,2048]{2,1,0:T(8,128)(2,1)S(1)} copy-done((bf16[3,128,2048]{2,1,0:T(8,128)(2,1)S(1)}, bf16[3,128,2048]{2,1,0:T(8,128)(2,1)}, u32[]{:S(2)}) %copy-start) | copy-done | bytes 1572888
  7.2 0.9 copy-done.1
  8.1 0.8 copy-done.2
  9.0 0.8 copy-done.3
  9.8 0.8 copy-done.4
  10.6 2.3 %end_states.1 = (f32[8,2048]{1,0:T(8,128)S(1)}, bf16[3,128,2048]{2,1,0:T(8,128)(2,1)S(1)}, f32[3,3,2048]{2,1,0:T(4,128)S(1)}, f32[8,2048]{1,0:T(8,128)S(1)}, f32...) custom-call(bf16[3,128,2048]{2,1,0:T(8,128)(2,1)S(1)} %copy-done, f32[3,3,2048]{2,1,0:T(4,128)S(1)} %copy-done.1, ...), custom_call_target="tpu_custom_call" | custom-call | flops 8388608 | bytes 1572864 | tf_op jit(solution)/shard_map/end_states/pallas_call | solution.py:200
  13.1 1.6 %collective-permute-start.1 = (f32[8,2048]{1,0:T(8,128)S(1)}, f32[8,2048]{1,0:T(8,128)S(1)}, u32[]{:S(2)}, u32[]{:S(2)}) collective-permute-start(f32[8,2048]{1,0:T(8,128)S(1)} %add_add_fusion), channel_id=1, source_target_pairs={{0,4},{4,0},{8,12},{12,8},{16,20},{20,16},{24,28},{28,24},{1,5},{5... | collective-permute-start | bytes 196616 | tf_op jit(solution)/shard_map/ppermute | solution.py:267
  14.8 2.7 %collective-permute-done.1 = f32[8,2048]{1,0:T(8,128)S(1)} collective-permute-done((f32[8,2048]{1,0:T(8,128)S(1)}, f32[8,2048]{1,0:T(8,128)S(1)}, u32[]{:S(2)}, u32[]{:S(2)}) %collective-permute-start.1) | collective-permute-done | bytes 65568 | tf_op jit(solution)/shard_map/ppermute | solution.py:267
  17.5 1.6 %collective-permute-start.2 = (f32[8,2048]{1,0:T(8,128)S(1)}, f32[8,2048]{1,0:T(8,128)S(1)}, u32[]{:S(2)}, u32[]{:S(2)}) collective-permute-start(f32[8,2048]{1,0:T(8,128)S(1)} %add_select_fusion.1), channel_id=1, source_target_pairs={{0,8},{4,12},{8,0},{12,4},{16,24},{20,28},{24,16},{28,20},{1,9},{5... | collective-permute-start | bytes 196616 | tf_op jit(solution)/shard_map/ppermute | solution.py:267
  19.1 2.7 %collective-permute-done.2 = f32[8,2048]{1,0:T(8,128)S(1)} collective-permute-done((f32[8,2048]{1,0:T(8,128)S(1)}, f32[8,2048]{1,0:T(8,128)S(1)}, u32[]{:S(2)}, u32[]{:S(2)}) %collective-permute-start.2) | collective-permute-done | bytes 65568 | tf_op jit(solution)/shard_map/ppermute | solution.py:267
  21.9 2.8 %collective-permute-start.3 = (f32[8,2048]{1,0:T(8,128)S(1)}, f32[8,2048]{1,0:T(8,128)S(1)}, u32[]{:S(2)}, u32[]{:S(2)}) collective-permute-start(f32[8,2048]{1,0:T(8,128)S(1)} %get-tuple-element.31), channel_id=1, source_target_pairs={{0,16},{4,20},{8,24},{12,28},{16,0},{20,4},{24,8},{28,12},{1,17},{... | collective-permute-start | bytes 196616 | tf_op jit(solution)/shard_map/ppermute | solution.py:267
  24.8 2.4 %collective-permute-done.3.last_ref = f32[8,2048]{1,0:T(8,128)S(1)} collective-permute-done((f32[8,2048]{1,0:T(8,128)S(1)}, f32[8,2048]{1,0:T(8,128)S(1)}, u32[]{:S(2)}, u32[]{:S(2)}) %collective-permute-start.3) | collective-permute-done | bytes 65568 | tf_op jit(solution)/shard_map/ppermute | solution.py:267
  27.1 2.4 %gated_half.3 = (bf16[64,1024]{1,0:T(8,128)(2,1)S(1)}, bf16[64,1024]{1,0:T(8,128)(2,1)S(1)}) custom-call(s32[2]{0:T(128)S(1)} %pad_add_fusion.place_ref, bf16[3,128,2048]{2,1,0:T(8,128)(2,1)S(1)} %get-tuple-element.15.block_ref, bf16[3,2,2048]{2,1,0:T(2,128)(2,1)S(1)} %collective-permute-done.halo_ref, f32[3,3,2048]{2,1,0:T(4,128)S(1)} %get-tuple-element.16.taps_ref, ...), custom_call_target="tpu_custom_call" | custom-call | flops 8388608 | bytes 1048576 | tf_op jit(solution)/shard_map/gated_half/pallas_call | solution.py:219
  29.5 1.6 %collective-permute-start.7 = (bf16[64,1024]{1,0:T(8,128)(2,1)S(1)}, bf16[64,1024]{1,0:T(8,128)(2,1)S(1)}, u32[]{:S(2)}, u32[]{:S(2)}) collective-permute-start(bf16[64,1024]{1,0:T(8,128)(2,1)S(1)} %get-tuple-element.23), channel_id=1, source_target_pairs={{0,2},{1,3},{2,0},{3,1},{4,6},{5,7},{6,4},{7,5},{8,10},{9,11},{10,... | collective-permute-start | bytes 393224 | tf_op jit(solution)/shard_map/ppermute | solution.py:253
  31.1 1.5 %collective-permute-start.6 = (bf16[64,1024]{1,0:T(8,128)(2,1)S(1)}, bf16[64,1024]{1,0:T(8,128)(2,1)S(1)}, u32[]{:S(2)}, u32[]{:S(2)}) collective-permute-start(bf16[64,1024]{1,0:T(8,128)(2,1)S(1)} %get-tuple-element.22), channel_id=1, source_target_pairs={{0,4},{1,14},{2,21},{3,31},{4,0},{5,10},{6,17},{7,27},{8,6},{9,12}... | collective-permute-start | bytes 393224 | tf_op jit(solution)/shard_map/ppermute | solution.py:253
  32.7 1.9 %collective-permute-done.7 = bf16[64,1024]{1,0:T(8,128)(2,1)S(1)} collective-permute-done((bf16[64,1024]{1,0:T(8,128)(2,1)S(1)}, bf16[64,1024]{1,0:T(8,128)(2,1)S(1)}, u32[]{:S(2)}, u32[]{:S(2)}) %collective-permute-start.7) | collective-permute-done | bytes 131104 | tf_op jit(solution)/shard_map/ppermute | solution.py:253
  34.6 2.4 %gated_half.2 = bf16[128,1024]{1,0:T(8,128)(2,1)S(1)} custom-call(s32[2]{0:T(128)S(1)} %pad_add_fusion.place_ref, bf16[3,128,2048]{2,1,0:T(8,128)(2,1)S(1)} %get-tuple-element.15.block_ref, bf16[3,2,2048]{2,1,0:T(2,128)(2,1)S(1)} %collective-permute-done.halo_ref, f32[3,3,2048]{2,1,0:T(4,128)S(1)} %get-tuple-element.16.taps_ref, ...), custom_call_target="tpu_custom_call" | custom-call | flops 8388608 | bytes 1048576 | tf_op jit(solution)/shard_map/gated_half/pallas_call | solution.py:219
  37.0 0.7 collective-permute-start.4
  37.7 2.6 %collective-permute-done.6 = bf16[64,1024]{1,0:T(8,128)(2,1)S(1)} collective-permute-done((bf16[64,1024]{1,0:T(8,128)(2,1)S(1)}, bf16[64,1024]{1,0:T(8,128)(2,1)S(1)}, u32[]{:S(2)}, u32[]{:S(2)}) %collective-permute-start.6) | collective-permute-done | bytes 131104 | tf_op jit(solution)/shard_map/ppermute | solution.py:253
  40.3 4.3 %collective-permute-done.8 = bf16[64,1024]{1,0:T(8,128)(2,1)S(1)} collective-permute-done((bf16[64,1024]{1,0:T(8,128)(2,1)S(1)}, bf16[64,1024]{1,0:T(8,128)(2,1)S(1)}, u32[]{:S(2)}, u32[]{:S(2)}) %collective-permute-start.8) | collective-permute-done | bytes 131104 | tf_op jit(solution)/shard_map/ppermute | solution.py:253
  45.0 7.8 %collective-permute-start.12 = (bf16[128,1024]{1,0:T(8,128)(2,1)S(1)}, bf16[128,1024]{1,0:T(8,128)(2,1)S(1)}, u32[]{:S(2)}, u32[]{:S(2)}) collective-permute-start(bf16[128,1024]{1,0:T(8,128)(2,1)S(1)} %collective-permute-done.4), channel_id=1, source_target_pairs={{0,2},{1,3},{2,0},{3,1},{4,6},{5,7},{6,4},{7,5},{8,10},{9,11},{10,... | collective-permute-start | bytes 786440 | tf_op jit(solution)/shard_map/ppermute | solution.py:253
  52.8 2.2 %collective-permute-start.5 = (bf16[128,1024]{1,0:T(8,128)(2,1)S(1)}, bf16[128,1024]{1,0:T(8,128)(2,1)S(1)}, u32[]{:S(2)}, u32[]{:S(2)}) collective-permute-start(bf16[128,1024]{1,0:T(8,128)(2,1)S(1)} %collective-permute-done.4), channel_id=1, source_target_pairs={{0,1},{1,0},{2,3},{3,2},{4,5},{5,4},{6,7},{7,6},{8,9},{9,8},{10,11... | collective-permute-start | bytes 786440 | tf_op jit(solution)/shard_map/ppermute | solution.py:253
  55.0 2.9 %convolution_convert_fusion.3 = bf16[128,2048]{1,0:T(8,128)(2,1)S(1)} fusion(bf16[1024,2048]{1,0:T(8,128)(2,1)} %param.13, bf16[128,1024]{1,0:T(8,128)(2,1)S(1)} %constant_dynamic-update-slice_fusion, bf16[128,1024]{1,0:T(8,128)(2,1)S(1)} %collective-permute-done.9, pred[]{:T(512)S(6)} %eq.8), kind=kOutput, calls=%fused_computation.3 | convolution fusion | flops 537264128 | bytes 5242881 | tf_op jit(solution)/shard_map/dot_general | solution.py:342
  57.9 2.3 %collective-permute-start.10 = (bf16[64,2048]{1,0:T(8,128)(2,1)S(1)}, bf16[64,2048]{1,0:T(8,128)(2,1)S(1)}, u32[]{:S(2)}, u32[]{:S(2)}) collective-permute-start(bf16[64,2048]{1,0:T(8,128)(2,1)S(1)} %get-tuple-element.29), channel_id=1, source_target_pairs={{0,4},{1,5},{2,6},{3,7},{4,0},{5,1},{6,2},{7,3},{8,12},{9,13},{10,... | collective-permute-start | bytes 786440 | tf_op jit(solution)/shard_map/ppermute | solution.py:253
  60.3 0.8 convolution_convert_fusion.1
  61.1 2.0 %collective-permute-start.18 = (bf16[128,2048]{1,0:T(8,128)(2,1)S(1)}, bf16[128,2048]{1,0:T(8,128)(2,1)S(1)}, u32[]{:S(2)}, u32[]{:S(2)}) collective-permute-start(bf16[128,2048]{1,0:T(8,128)(2,1)S(1)} %convolution_convert_fusion.1), channel_id=1, source_target_pairs={{0,4},{1,5},{2,6},{3,7},{4,0},{5,1},{6,2},{7,3},{8,12},{9,13},{10,... | collective-permute-start | bytes 1572872 | tf_op jit(solution)/shard_map/ppermute | solution.py:253
  63.1 0.7 fusion.4
  63.8 0.7 fusion.10
  64.8 0.6 collective-permute-start.13
  65.3 0.9 collective-permute-done.15
  66.2 0.7 convolution_convert_fusion.2
  67.1 0.7 convolution_convert_fusion
  67.8 5.2 %collective-permute-done.22 = bf16[64,2048]{1,0:T(8,128)(2,1)S(1)} collective-permute-done((bf16[64,2048]{1,0:T(8,128)(2,1)S(1)}, bf16[64,2048]{1,0:T(8,128)(2,1)S(1)}, u32[]{:S(2)}, u32[]{:S(2)}) %collective-permute-start.22) | collective-permute-done | bytes 262176 | tf_op jit(solution)/shard_map/ppermute | solution.py:253
  73.0 2.0 %collective-permute-start.20 = (bf16[128,2048]{1,0:T(8,128)(2,1)S(1)}, bf16[128,2048]{1,0:T(8,128)(2,1)S(1)}, u32[]{:S(2)}, u32[]{:S(2)}) collective-permute-start(bf16[128,2048]{1,0:T(8,128)(2,1)S(1)} %convolution_convert_fusion), channel_id=1, source_target_pairs={{0,4},{1,5},{2,6},{3,7},{4,0},{5,1},{6,2},{7,3},{8,12},{9,13},{10,... | collective-permute-start | bytes 1572872 | tf_op jit(solution)/shard_map/ppermute | solution.py:253
  75.2 0.7 fusion.1
  75.9 0.7 fusion.7
  76.6 7.6 %collective-permute-done.18 = bf16[128,2048]{1,0:T(8,128)(2,1)S(1)} collective-permute-done((bf16[128,2048]{1,0:T(8,128)(2,1)S(1)}, bf16[128,2048]{1,0:T(8,128)(2,1)S(1)}, u32[]{:S(2)}, u32[]{:S(2)}) %collective-permute-start.18) | collective-permute-done | bytes 524320 | tf_op jit(solution)/shard_map/ppermute | solution.py:253
  84.4 0.7 collective-permute-start.19
  85.1 10.4 %collective-permute-done.16 = bf16[128,2048]{1,0:T(8,128)(2,1)S(1)} collective-permute-done((bf16[128,2048]{1,0:T(8,128)(2,1)S(1)}, bf16[128,2048]{1,0:T(8,128)(2,1)S(1)}, u32[]{:S(2)}, u32[]{:S(2)}) %collective-permute-start.16) | collective-permute-done | bytes 524320 | tf_op jit(solution)/shard_map/ppermute | solution.py:253
  95.6 2.8 %collective-permute-start.17 = (bf16[128,2048]{1,0:T(8,128)(2,1)S(1)}, bf16[128,2048]{1,0:T(8,128)(2,1)S(1)}, u32[]{:S(2)}, u32[]{:S(2)}) collective-permute-start(bf16[128,2048]{1,0:T(8,128)(2,1)S(1)} %add_convert_fusion.2), channel_id=1, source_target_pairs={{0,24},{1,25},{2,18},{3,19},{4,28},{5,29},{6,22},{7,23},{8,16},{9,... | collective-permute-start | bytes 1572872 | tf_op jit(solution)/shard_map/ppermute | solution.py:253
  98.4 7.6 %collective-permute-done.20 = bf16[128,2048]{1,0:T(8,128)(2,1)S(1)} collective-permute-done((bf16[128,2048]{1,0:T(8,128)(2,1)S(1)}, bf16[128,2048]{1,0:T(8,128)(2,1)S(1)}, u32[]{:S(2)}, u32[]{:S(2)}) %collective-permute-start.20) | collective-permute-done | bytes 524320 | tf_op jit(solution)/shard_map/ppermute | solution.py:253
  106.1 3.8 %collective-permute-start.21 = (bf16[128,2048]{1,0:T(8,128)(2,1)S(1)}, bf16[128,2048]{1,0:T(8,128)(2,1)S(1)}, u32[]{:S(2)}, u32[]{:S(2)}) collective-permute-start(bf16[128,2048]{1,0:T(8,128)(2,1)S(1)} %add_convert_fusion), channel_id=1, source_target_pairs={{0,8},{1,9},{2,2},{3,3},{4,12},{5,13},{6,6},{7,7},{8,0},{9,1},{10,... | collective-permute-start | bytes 1572872 | tf_op jit(solution)/shard_map/ppermute | solution.py:253
  110.0 1.2 collective-permute-start.11
  111.2 20.8 %collective-permute-done.11 = bf16[64,2048]{1,0:T(8,128)(2,1)S(1)} collective-permute-done((bf16[64,2048]{1,0:T(8,128)(2,1)S(1)}, bf16[64,2048]{1,0:T(8,128)(2,1)S(1)}, u32[]{:S(2)}, u32[]{:S(2)}) %collective-permute-start.11) | collective-permute-done | bytes 262176 | tf_op jit(solution)/shard_map/ppermute | solution.py:253
  132.0 0.4 add_convert_fusion.5
  132.5 0.8 pad_maximum_fusion
  (45 shorter events, 1.7 us)
Async XLA Ops:
  0.9 12.0 %collective-permute-start = (bf16[3,2,2048]{2,1,0:T(2,128)(2,1)S(1)}, bf16[3,2,2048]{2,1,0:T(2,128)(2,1)S(1)}, u32[]{:S(2)}, u32[]{:S(2)}) collective-permute-start(bf16[3,2,2048]{2,1,0:T(2,128)(2,1)S(1)} %slice.110), channel_id=1, source_target_pairs={{0,4},{4,8},{8,12},{12,16},{16,20},{20,24},{24,28},{1,5},{5,9},{9,... | collective-permute-start | bytes 73736 | tf_op jit(solution)/shard_map/ppermute | solution.py:257
  5.8 1.4 %copy-start = (bf16[3,128,2048]{2,1,0:T(8,128)(2,1)S(1)}, bf16[3,128,2048]{2,1,0:T(8,128)(2,1)}, u32[]{:S(2)}) copy-start(bf16[3,128,2048]{2,1,0:T(8,128)(2,1)} %block_hbm.1) | copy-start | bytes 4718596
  7.2 0.9 copy-start.1
  8.1 0.8 copy-start.2
  8.9 0.8 copy-start.3
  9.8 0.8 copy-start.4
  13.1 4.3 %collective-permute-start.1 = (f32[8,2048]{1,0:T(8,128)S(1)}, f32[8,2048]{1,0:T(8,128)S(1)}, u32[]{:S(2)}, u32[]{:S(2)}) collective-permute-start(f32[8,2048]{1,0:T(8,128)S(1)} %add_add_fusion), channel_id=1, source_target_pairs={{0,4},{4,0},{8,12},{12,8},{16,20},{20,16},{24,28},{28,24},{1,5},{5... | collective-permute-start | bytes 196616 | tf_op jit(solution)/shard_map/ppermute | solution.py:267
  17.5 4.3 %collective-permute-start.2 = (f32[8,2048]{1,0:T(8,128)S(1)}, f32[8,2048]{1,0:T(8,128)S(1)}, u32[]{:S(2)}, u32[]{:S(2)}) collective-permute-start(f32[8,2048]{1,0:T(8,128)S(1)} %add_select_fusion.1), channel_id=1, source_target_pairs={{0,8},{4,12},{8,0},{12,4},{16,24},{20,28},{24,16},{28,20},{1,9},{5... | collective-permute-start | bytes 196616 | tf_op jit(solution)/shard_map/ppermute | solution.py:267
  21.9 5.2 %collective-permute-start.3 = (f32[8,2048]{1,0:T(8,128)S(1)}, f32[8,2048]{1,0:T(8,128)S(1)}, u32[]{:S(2)}, u32[]{:S(2)}) collective-permute-start(f32[8,2048]{1,0:T(8,128)S(1)} %get-tuple-element.31), channel_id=1, source_target_pairs={{0,16},{4,20},{8,24},{12,28},{16,0},{20,4},{24,8},{28,12},{1,17},{... | collective-permute-start | bytes 196616 | tf_op jit(solution)/shard_map/ppermute | solution.py:267
  29.5 5.0 %collective-permute-start.7 = (bf16[64,1024]{1,0:T(8,128)(2,1)S(1)}, bf16[64,1024]{1,0:T(8,128)(2,1)S(1)}, u32[]{:S(2)}, u32[]{:S(2)}) collective-permute-start(bf16[64,1024]{1,0:T(8,128)(2,1)S(1)} %get-tuple-element.23), channel_id=1, source_target_pairs={{0,2},{1,3},{2,0},{3,1},{4,6},{5,7},{6,4},{7,5},{8,10},{9,11},{10,... | collective-permute-start | bytes 393224 | tf_op jit(solution)/shard_map/ppermute | solution.py:253
  31.1 9.2 %collective-permute-start.6 = (bf16[64,1024]{1,0:T(8,128)(2,1)S(1)}, bf16[64,1024]{1,0:T(8,128)(2,1)S(1)}, u32[]{:S(2)}, u32[]{:S(2)}) collective-permute-start(bf16[64,1024]{1,0:T(8,128)(2,1)S(1)} %get-tuple-element.22), channel_id=1, source_target_pairs={{0,4},{1,14},{2,21},{3,31},{4,0},{5,10},{6,17},{7,27},{8,6},{9,12}... | collective-permute-start | bytes 393224 | tf_op jit(solution)/shard_map/ppermute | solution.py:253
  34.6 10.1 %collective-permute-start.8 = (bf16[64,1024]{1,0:T(8,128)(2,1)S(1)}, bf16[64,1024]{1,0:T(8,128)(2,1)S(1)}, u32[]{:S(2)}, u32[]{:S(2)}) collective-permute-start(bf16[64,1024]{1,0:T(8,128)(2,1)S(1)} %collective-permute-done.7), channel_id=1, source_target_pairs={{0,21},{1,31},{2,4},{3,14},{4,17},{5,27},{6,0},{7,10},{8,23},{9,29... | collective-permute-start | bytes 393224 | tf_op jit(solution)/shard_map/ppermute | solution.py:253
  37.0 8.1 %collective-permute-start.4 = (bf16[128,1024]{1,0:T(8,128)(2,1)S(1)}, bf16[128,1024]{1,0:T(8,128)(2,1)S(1)}, u32[]{:S(2)}, u32[]{:S(2)}) collective-permute-start(bf16[128,1024]{1,0:T(8,128)(2,1)S(1)} %gated_half.2), channel_id=1, source_target_pairs={{0,0},{1,10},{2,17},{3,27},{4,4},{5,14},{6,21},{7,31},{8,2},{9,8},... | collective-permute-start | bytes 786440 | tf_op jit(solution)/shard_map/ppermute | solution.py:253
  44.6 10.3 %collective-permute-start.9 = (bf16[128,1024]{1,0:T(8,128)(2,1)S(1)}, bf16[128,1024]{1,0:T(8,128)(2,1)S(1)}, u32[]{:S(2)}, u32[]{:S(2)}) collective-permute-start(bf16[128,1024]{1,0:T(8,128)(2,1)S(1)} %constant_dynamic-update-slice_fusion), channel_id=1, source_target_pairs={{0,1},{1,0},{2,3},{3,2},{4,5},{5,4},{6,7},{7,6},{8,9},{9,8},{10,11... | collective-permute-start | bytes 786440 | tf_op jit(solution)/shard_map/ppermute | solution.py:253
  44.7 15.6 %copy-start.5 = (bf16[1024,2048]{1,0:T(8,128)(2,1)S(1)}, bf16[1024,2048]{1,0:T(8,128)(2,1)}, u32[]{:S(2)}) copy-start(bf16[1024,2048]{1,0:T(8,128)(2,1)} %param.13) | copy-start | bytes 12582916
  44.8 19.8 %collective-permute-start.14 = (bf16[128,1024]{1,0:T(8,128)(2,1)S(1)}, bf16[128,1024]{1,0:T(8,128)(2,1)S(1)}, u32[]{:S(2)}, u32[]{:S(2)}) collective-permute-start(bf16[128,1024]{1,0:T(8,128)(2,1)S(1)} %constant_dynamic-update-slice_fusion), channel_id=1, source_target_pairs={{0,2},{1,3},{2,0},{3,1},{4,6},{5,7},{6,4},{7,5},{8,10},{9,11},{10,... | collective-permute-start | bytes 786440 | tf_op jit(solution)/shard_map/ppermute | solution.py:253
  45.0 19.7 %collective-permute-start.12 = (bf16[128,1024]{1,0:T(8,128)(2,1)S(1)}, bf16[128,1024]{1,0:T(8,128)(2,1)S(1)}, u32[]{:S(2)}, u32[]{:S(2)}) collective-permute-start(bf16[128,1024]{1,0:T(8,128)(2,1)S(1)} %collective-permute-done.4), channel_id=1, source_target_pairs={{0,2},{1,3},{2,0},{3,1},{4,6},{5,7},{6,4},{7,5},{8,10},{9,11},{10,... | collective-permute-start | bytes 786440 | tf_op jit(solution)/shard_map/ppermute | solution.py:253
  52.8 8.3 %collective-permute-start.5 = (bf16[128,1024]{1,0:T(8,128)(2,1)S(1)}, bf16[128,1024]{1,0:T(8,128)(2,1)S(1)}, u32[]{:S(2)}, u32[]{:S(2)}) collective-permute-start(bf16[128,1024]{1,0:T(8,128)(2,1)S(1)} %collective-permute-done.4), channel_id=1, source_target_pairs={{0,1},{1,0},{2,3},{3,2},{4,5},{5,4},{6,7},{7,6},{8,9},{9,8},{10,11... | collective-permute-start | bytes 786440 | tf_op jit(solution)/shard_map/ppermute | solution.py:253
  57.9 52.0 %collective-permute-start.10 = (bf16[64,2048]{1,0:T(8,128)(2,1)S(1)}, bf16[64,2048]{1,0:T(8,128)(2,1)S(1)}, u32[]{:S(2)}, u32[]{:S(2)}) collective-permute-start(bf16[64,2048]{1,0:T(8,128)(2,1)S(1)} %get-tuple-element.29), channel_id=1, source_target_pairs={{0,4},{1,5},{2,6},{3,7},{4,0},{5,1},{6,2},{7,3},{8,12},{9,13},{10,... | collective-permute-start | bytes 786440 | tf_op jit(solution)/shard_map/ppermute | solution.py:253
  60.2 12.8 %collective-permute-start.22 = (bf16[64,2048]{1,0:T(8,128)(2,1)S(1)}, bf16[64,2048]{1,0:T(8,128)(2,1)S(1)}, u32[]{:S(2)}, u32[]{:S(2)}) collective-permute-start(bf16[64,2048]{1,0:T(8,128)(2,1)S(1)} %get-tuple-element.30), channel_id=1, source_target_pairs={{0,4},{1,5},{2,6},{3,7},{4,0},{5,1},{6,2},{7,3},{8,12},{9,13},{10,... | collective-permute-start | bytes 786440 | tf_op jit(solution)/shard_map/ppermute | solution.py:253
  61.1 23.2 %collective-permute-start.18 = (bf16[128,2048]{1,0:T(8,128)(2,1)S(1)}, bf16[128,2048]{1,0:T(8,128)(2,1)S(1)}, u32[]{:S(2)}, u32[]{:S(2)}) collective-permute-start(bf16[128,2048]{1,0:T(8,128)(2,1)S(1)} %convolution_convert_fusion.1), channel_id=1, source_target_pairs={{0,4},{1,5},{2,6},{3,7},{4,0},{5,1},{6,2},{7,3},{8,12},{9,13},{10,... | collective-permute-start | bytes 1572872 | tf_op jit(solution)/shard_map/ppermute | solution.py:253
  64.6 1.6 %collective-permute-start.15 = (bf16[128,1024]{1,0:T(8,128)(2,1)S(1)}, bf16[128,1024]{1,0:T(8,128)(2,1)S(1)}, u32[]{:S(2)}, u32[]{:S(2)}) collective-permute-start(bf16[128,1024]{1,0:T(8,128)(2,1)S(1)} %collective-permute-done.14), channel_id=1, source_target_pairs={{0,1},{1,0},{2,3},{3,2},{4,5},{5,4},{6,7},{7,6},{8,9},{9,8},{10,11... | collective-permute-start | bytes 786440 | tf_op jit(solution)/shard_map/ppermute | solution.py:253
  64.8 10.3 %collective-permute-start.13 = (bf16[128,1024]{1,0:T(8,128)(2,1)S(1)}, bf16[128,1024]{1,0:T(8,128)(2,1)S(1)}, u32[]{:S(2)}, u32[]{:S(2)}) collective-permute-start(bf16[128,1024]{1,0:T(8,128)(2,1)S(1)} %collective-permute-done.12), channel_id=1, source_target_pairs={{0,1},{1,0},{2,3},{3,2},{4,5},{5,4},{6,7},{7,6},{8,9},{9,8},{10,11... | collective-permute-start | bytes 786440 | tf_op jit(solution)/shard_map/ppermute | solution.py:253
  66.9 28.5 %collective-permute-start.16 = (bf16[128,2048]{1,0:T(8,128)(2,1)S(1)}, bf16[128,2048]{1,0:T(8,128)(2,1)S(1)}, u32[]{:S(2)}, u32[]{:S(2)}) collective-permute-start(bf16[128,2048]{1,0:T(8,128)(2,1)S(1)} %convolution_convert_fusion.2), channel_id=1, source_target_pairs={{0,4},{1,5},{2,6},{3,7},{4,0},{5,1},{6,2},{7,3},{8,12},{9,13},{10,... | collective-permute-start | bytes 1572872 | tf_op jit(solution)/shard_map/ppermute | solution.py:253
  73.0 33.0 %collective-permute-start.20 = (bf16[128,2048]{1,0:T(8,128)(2,1)S(1)}, bf16[128,2048]{1,0:T(8,128)(2,1)S(1)}, u32[]{:S(2)}, u32[]{:S(2)}) collective-permute-start(bf16[128,2048]{1,0:T(8,128)(2,1)S(1)} %convolution_convert_fusion), channel_id=1, source_target_pairs={{0,4},{1,5},{2,6},{3,7},{4,0},{5,1},{6,2},{7,3},{8,12},{9,13},{10,... | collective-permute-start | bytes 1572872 | tf_op jit(solution)/shard_map/ppermute | solution.py:253
  75.1 36.1 %collective-permute-start.23 = (bf16[64,2048]{1,0:T(8,128)(2,1)S(1)}, bf16[64,2048]{1,0:T(8,128)(2,1)S(1)}, u32[]{:S(2)}, u32[]{:S(2)}) collective-permute-start(bf16[64,2048]{1,0:T(8,128)(2,1)S(1)} %add_convert_fusion.4), channel_id=1, source_target_pairs={{0,16},{1,17},{2,26},{3,27},{4,20},{5,21},{6,30},{7,31},{8,24},{9,... | collective-permute-start | bytes 786440 | tf_op jit(solution)/shard_map/ppermute | solution.py:253
  76.6 55.4 %copy-start.6 = (bf16[128,2048]{1,0:T(8,128)(2,1)S(1)}, bf16[128,2048]{1,0:T(8,128)(2,1)}, u32[]{:S(2)}) copy-start(bf16[128,2048]{1,0:T(8,128)(2,1)} %param.7) | copy-start | bytes 1572868
  84.4 47.6 %collective-permute-start.19 = (bf16[128,2048]{1,0:T(8,128)(2,1)S(1)}, bf16[128,2048]{1,0:T(8,128)(2,1)S(1)}, u32[]{:S(2)}, u32[]{:S(2)}) collective-permute-start(bf16[128,2048]{1,0:T(8,128)(2,1)S(1)} %add_convert_fusion.1), channel_id=1, source_target_pairs={{0,0},{1,1},{2,10},{3,11},{4,4},{5,5},{6,14},{7,15},{8,8},{9,9},{1... | collective-permute-start | bytes 1572872 | tf_op jit(solution)/shard_map/ppermute | solution.py:253
  95.6 36.4 %collective-permute-start.17 = (bf16[128,2048]{1,0:T(8,128)(2,1)S(1)}, bf16[128,2048]{1,0:T(8,128)(2,1)S(1)}, u32[]{:S(2)}, u32[]{:S(2)}) collective-permute-start(bf16[128,2048]{1,0:T(8,128)(2,1)S(1)} %add_convert_fusion.2), channel_id=1, source_target_pairs={{0,24},{1,25},{2,18},{3,19},{4,28},{5,29},{6,22},{7,23},{8,16},{9,... | collective-permute-start | bytes 1572872 | tf_op jit(solution)/shard_map/ppermute | solution.py:253
  106.1 25.9 %collective-permute-start.21 = (bf16[128,2048]{1,0:T(8,128)(2,1)S(1)}, bf16[128,2048]{1,0:T(8,128)(2,1)S(1)}, u32[]{:S(2)}, u32[]{:S(2)}) collective-permute-start(bf16[128,2048]{1,0:T(8,128)(2,1)S(1)} %add_convert_fusion), channel_id=1, source_target_pairs={{0,8},{1,9},{2,2},{3,3},{4,12},{5,13},{6,6},{7,7},{8,0},{9,1},{10,... | collective-permute-start | bytes 1572872 | tf_op jit(solution)/shard_map/ppermute | solution.py:253
  110.0 22.0 %collective-permute-start.11 = (bf16[64,2048]{1,0:T(8,128)(2,1)S(1)}, bf16[64,2048]{1,0:T(8,128)(2,1)S(1)}, u32[]{:S(2)}, u32[]{:S(2)}) collective-permute-start(bf16[64,2048]{1,0:T(8,128)(2,1)S(1)} %add_convert_fusion.6), channel_id=1, source_target_pairs={{0,16},{1,17},{2,26},{3,27},{4,20},{5,21},{6,30},{7,31},{8,24},{9,... | collective-permute-start | bytes 786440 | tf_op jit(solution)/shard_map/ppermute | solution.py:253

commit v2 on v1

--- a/solution.py
+++ b/solution.py
@@ -293,49 +293,45 @@
     odd = lax.axis_index("chan") % 2 == 1
     pieces = {}
     for j in order:
-        lower = [jnp.concatenate(blocks[j], axis=0) if len(blocks[j]) > 1 else blocks[j][0]]
-        sides = {}
-
-        def beside(slot):
-            return moved(lower[slot], lambda a, b, c: (a, b, c ^ 1))
-
-        sides[0] = beside(0)
+        lower, sides = [], []
+        for p, block in enumerate(blocks[j]):
+            lower.append(block)
+            sides.append(moved(block, lambda a, b, c: (a, b, c ^ 1)))
+            if j:
+                pieces[j, 0, 0, p] = product_of(jnp.where(odd, lower[p], sides[p]), out_weight, j)
+        if len(lower) > 1:
+            lower, sides = [jnp.concatenate(lower, axis=0)], [jnp.concatenate(sides, axis=0)]
         for i in range(bits - 1):
             flip = top >> i
             for slot in range(1 << i):
                 new = slot + (1 << i)
                 lower.append(moved(lower[slot], lambda a, b, c: (a, b, c ^ flip)))
-                sides[new] = beside(new)
+                sides.append(moved(lower[new], lambda a, b, c: (a, b, c ^ 1)))
         for slot in range(top):
             for group, pair in enumerate([(lower[slot], sides[slot]), (sides[slot], lower[slot])]):
-                pieces[j, group, slot] = product_of(jnp.where(odd, *pair), out_weight, j)
+                if (j, group, slot, 0) not in pieces:
+                    pieces[j, group, slot, 0] = product_of(jnp.where(odd, *pair), out_weight, j)
 
     half = tokens // 2
-    totals = [stream_in[p * half : (p + 1) * half].astype(F32) for p in range(2)]
+    total = stream_in.astype(F32)
     for group in range(2):
         for slot in range(top):
             cut = group == 0 and slot == 0
-            own = [pieces[0, group, slot]]
+            own = [pieces[0, group, slot, 0]]
             if cut:
                 own = lax.optimization_barrier((own[0][:half], own[0][half:]))
-            for p in range(2 if cut else 1):
-                start = p * half
-                stop = start + (half if cut else tokens)
-                mixed = own[p]
+            came = []
+            for p, mixed in enumerate(own):
                 for j in range(1, lines):
-                    part = moved(
-                        pieces[j, group, slot][start:stop], lambda a, b, c: (a, (b - j) % lines, c)
-                    )
+                    part = moved(pieces[j, group, slot, p], lambda a, b, c: (a, (b - j) % lines, c))
                     mixed = mixed + part.astype(F32)
 
                 def target(a, b, c):
                     return a ^ turned[c] ^ (slot + top * (c % 2 == group)), b, c
 
-                mixed = moved(mixed.astype(BF16), target)
-                for i in [p] if cut else [0, 1]:
-                    part = mixed if cut else mixed[i * half : (i + 1) * half]
-                    totals[i] = totals[i] + part.astype(F32)
-    return jnp.concatenate([total.astype(BF16) for total in totals], axis=0)
+                came.append(moved(mixed.astype(BF16), target))
+            total = total + (jnp.concatenate(came, axis=0) if cut else came[0]).astype(F32)
+    return total.astype(BF16)
 
 
 def product_of(block, weight, j):

time: 134 us -> 128 us (0.955)
  starting transfers between devices: 40.7 us -> 37.3 us
  waiting for transfers between devices: 69.1 us -> 66.4 us
    ppermute x20 -> x21, starting transfers between devices: 29.8 us -> 26.3 us  [moved(): lax.ppermute(block, both, [(number(*p), number(*target(*p))) for p in pla...]
    ppermute x20 -> x21, waiting for transfers between devices: 61.4 us -> 58.7 us  [moved(): lax.ppermute(block, both, [(number(*p), number(*target(*p))) for p in pla...]
    dot_general x8 -> x9, matrix products: 8.06 us -> 9 us  [product_of(): product = jnp.dot(block, weight, preferred_element_type=F32)]
  transfers between devices with their start and end apart: 24 -> 25, of which waited for: 12 -> 12; matrix products, arithmetic and copies ran while one was open for 7% -> 8% of each run, Pallas kernels for 4% -> 4%
where the time goes in v2:
time: 128 us
  waiting for transfers between devices  66.4 us (52%)
  starting transfers between devices  37.3 us (29%)
  matrix products  9 us (7%)
  Pallas kernels  7.09 us (6%)
  local copies, waits for them, and re-layouts  5.83 us (5%)
  other arithmetic  1.99 us (2%)
    ppermute x21, waiting for transfers between devices, moved(): lax.ppermute(block, both, [(number(*p), number(*target(*p))) for p in pla...  58.7 us
    ppermute x21, starting transfers between devices, moved(): lax.ppermute(block, both, [(number(*p), number(*target(*p))) for p in pla...  26.3 us
    dot_general x9, matrix products, product_of(): product = jnp.dot(block, weight, preferred_element_type=F32)  9 us
    ppermute x3, waiting for transfers between devices, shards(): other = lax.ppermute(ends, 'seq', [(s, s ^ width) for s in range(seqs)])  7.75 us
    ppermute x3, starting transfers between devices, shards(): other = lax.ppermute(ends, 'seq', [(s, s ^ width) for s in range(seqs)])  6.06 us
    ppermute x1, starting transfers between devices, shards(): lax.ppermute(features[:, tokens - reach:, :], 'seq', [(s, s + 1) for s in...  4.87 us
    unnamed x15, local copies, waits for them, and re-layouts  4.83 us
    pallas_call x2, Pallas kernels, gated_half(): pl.pallas_call(functools.partial(gated_kernel, j, lines, parts), in_specs...  4.81 us
  transfers between devices with their start and end apart: 25, of which 12 were waited for; matrix products, arithmetic and copies ran while one was open for 8% of the time, Pallas kernels for 4%

profile of v2, /device:TPU:0, one launch (start us, length us, event | category | flops | bytes accessed | tf_op | source)
XLA Modules:
  0.0 127.9 jit_solution(13750094703764542035)
XLA Ops:
  0.0 0.9 slice.79
  0.9 4.9 %collective-permute-start = (bf16[3,2,2048]{2,1,0:T(2,128)(2,1)S(1)}, bf16[3,2,2048]{2,1,0:T(2,128)(2,1)S(1)}, u32[]{:S(2)}, u32[]{:S(2)}) collective-permute-start(bf16[3,2,2048]{2,1,0:T(2,128)(2,1)S(1)} %slice.79), channel_id=1, source_target_pairs={{0,4},{4,8},{8,12},{12,16},{16,20},{20,24},{24,28},{1,5},{5,9},{9,... | collective-permute-start | bytes 73736 | tf_op jit(solution)/shard_map/ppermute | solution.py:257
  5.8 1.4 %copy-done = bf16[3,128,2048]{2,1,0:T(8,128)(2,1)S(1)} copy-done((bf16[3,128,2048]{2,1,0:T(8,128)(2,1)S(1)}, bf16[3,128,2048]{2,1,0:T(8,128)(2,1)}, u32[]{:S(2)}) %copy-start) | copy-done | bytes 1572888
  7.2 0.9 copy-done.1
  8.1 0.8 copy-done.2
  9.0 0.8 copy-done.3
  9.8 0.8 copy-done.4
  10.6 2.3 %end_states.1 = (f32[8,2048]{1,0:T(8,128)S(1)}, bf16[3,128,2048]{2,1,0:T(8,128)(2,1)S(1)}, f32[3,3,2048]{2,1,0:T(4,128)S(1)}, f32[8,2048]{1,0:T(8,128)S(1)}, f32...) custom-call(bf16[3,128,2048]{2,1,0:T(8,128)(2,1)S(1)} %copy-done, f32[3,3,2048]{2,1,0:T(4,128)S(1)} %copy-done.1, ...), custom_call_target="tpu_custom_call" | custom-call | flops 8388608 | bytes 1572864 | tf_op jit(solution)/shard_map/end_states/pallas_call | solution.py:200
  13.1 1.6 %collective-permute-start.1 = (f32[8,2048]{1,0:T(8,128)S(1)}, f32[8,2048]{1,0:T(8,128)S(1)}, u32[]{:S(2)}, u32[]{:S(2)}) collective-permute-start(f32[8,2048]{1,0:T(8,128)S(1)} %add_add_fusion), channel_id=1, source_target_pairs={{0,4},{4,0},{8,12},{12,8},{16,20},{20,16},{24,28},{28,24},{1,5},{5... | collective-permute-start | bytes 196616 | tf_op jit(solution)/shard_map/ppermute | solution.py:267
  14.8 2.7 %collective-permute-done.1 = f32[8,2048]{1,0:T(8,128)S(1)} collective-permute-done((f32[8,2048]{1,0:T(8,128)S(1)}, f32[8,2048]{1,0:T(8,128)S(1)}, u32[]{:S(2)}, u32[]{:S(2)}) %collective-permute-start.1) | collective-permute-done | bytes 65568 | tf_op jit(solution)/shard_map/ppermute | solution.py:267
  17.5 1.6 %collective-permute-start.2 = (f32[8,2048]{1,0:T(8,128)S(1)}, f32[8,2048]{1,0:T(8,128)S(1)}, u32[]{:S(2)}, u32[]{:S(2)}) collective-permute-start(f32[8,2048]{1,0:T(8,128)S(1)} %add_select_fusion.1), channel_id=1, source_target_pairs={{0,8},{4,12},{8,0},{12,4},{16,24},{20,28},{24,16},{28,20},{1,9},{5... | collective-permute-start | bytes 196616 | tf_op jit(solution)/shard_map/ppermute | solution.py:267
  19.1 2.7 %collective-permute-done.2 = f32[8,2048]{1,0:T(8,128)S(1)} collective-permute-done((f32[8,2048]{1,0:T(8,128)S(1)}, f32[8,2048]{1,0:T(8,128)S(1)}, u32[]{:S(2)}, u32[]{:S(2)}) %collective-permute-start.2) | collective-permute-done | bytes 65568 | tf_op jit(solution)/shard_map/ppermute | solution.py:267
  21.9 2.8 %collective-permute-start.3 = (f32[8,2048]{1,0:T(8,128)S(1)}, f32[8,2048]{1,0:T(8,128)S(1)}, u32[]{:S(2)}, u32[]{:S(2)}) collective-permute-start(f32[8,2048]{1,0:T(8,128)S(1)} %get-tuple-element.27), channel_id=1, source_target_pairs={{0,16},{4,20},{8,24},{12,28},{16,0},{20,4},{24,8},{28,12},{1,17},{... | collective-permute-start | bytes 196616 | tf_op jit(solution)/shard_map/ppermute | solution.py:267
  24.8 2.4 %collective-permute-done.3.last_ref = f32[8,2048]{1,0:T(8,128)S(1)} collective-permute-done((f32[8,2048]{1,0:T(8,128)S(1)}, f32[8,2048]{1,0:T(8,128)S(1)}, u32[]{:S(2)}, u32[]{:S(2)}) %collective-permute-start.3) | collective-permute-done | bytes 65568 | tf_op jit(solution)/shard_map/ppermute | solution.py:267
  27.1 2.4 %gated_half.3 = (bf16[64,1024]{1,0:T(8,128)(2,1)S(1)}, bf16[64,1024]{1,0:T(8,128)(2,1)S(1)}) custom-call(s32[2]{0:T(128)S(1)} %pad_add_fusion.place_ref, bf16[3,128,2048]{2,1,0:T(8,128)(2,1)S(1)} %get-tuple-element.15.block_ref, bf16[3,2,2048]{2,1,0:T(2,128)(2,1)S(1)} %collective-permute-done.halo_ref, f32[3,3,2048]{2,1,0:T(4,128)S(1)} %get-tuple-element.16.taps_ref, ...), custom_call_target="tpu_custom_call" | custom-call | flops 8388608 | bytes 1048576 | tf_op jit(solution)/shard_map/gated_half/pallas_call | solution.py:219
  29.5 1.6 %collective-permute-start.10 = (bf16[64,1024]{1,0:T(8,128)(2,1)S(1)}, bf16[64,1024]{1,0:T(8,128)(2,1)S(1)}, u32[]{:S(2)}, u32[]{:S(2)}) collective-permute-start(bf16[64,1024]{1,0:T(8,128)(2,1)S(1)} %get-tuple-element.24), channel_id=1, source_target_pairs={{0,2},{1,3},{2,0},{3,1},{4,6},{5,7},{6,4},{7,5},{8,10},{9,11},{10,... | collective-permute-start | bytes 393224 | tf_op jit(solution)/shard_map/ppermute | solution.py:253
  31.1 1.5 %collective-permute-start.6 = (bf16[64,1024]{1,0:T(8,128)(2,1)S(1)}, bf16[64,1024]{1,0:T(8,128)(2,1)S(1)}, u32[]{:S(2)}, u32[]{:S(2)}) collective-permute-start(bf16[64,1024]{1,0:T(8,128)(2,1)S(1)} %get-tuple-element.22), channel_id=1, source_target_pairs={{0,4},{1,14},{2,21},{3,31},{4,0},{5,10},{6,17},{7,27},{8,6},{9,12}... | collective-permute-start | bytes 393224 | tf_op jit(solution)/shard_map/ppermute | solution.py:253
  32.7 1.9 %collective-permute-done.10 = bf16[64,1024]{1,0:T(8,128)(2,1)S(1)} collective-permute-done((bf16[64,1024]{1,0:T(8,128)(2,1)S(1)}, bf16[64,1024]{1,0:T(8,128)(2,1)S(1)}, u32[]{:S(2)}, u32[]{:S(2)}) %collective-permute-start.10) | collective-permute-done | bytes 131104 | tf_op jit(solution)/shard_map/ppermute | solution.py:253
  34.6 5.7 %collective-permute-done.6 = bf16[64,1024]{1,0:T(8,128)(2,1)S(1)} collective-permute-done((bf16[64,1024]{1,0:T(8,128)(2,1)S(1)}, bf16[64,1024]{1,0:T(8,128)(2,1)S(1)}, u32[]{:S(2)}, u32[]{:S(2)}) %collective-permute-start.6) | collective-permute-done | bytes 131104 | tf_op jit(solution)/shard_map/ppermute | solution.py:253
  40.3 2.4 %gated_half.2 = bf16[128,1024]{1,0:T(8,128)(2,1)S(1)} custom-call(s32[2]{0:T(128)S(1)} %pad_add_fusion.place_ref, bf16[3,128,2048]{2,1,0:T(8,128)(2,1)S(1)} %get-tuple-element.15.block_ref, bf16[3,2,2048]{2,1,0:T(2,128)(2,1)S(1)} %collective-permute-done.halo_ref, f32[3,3,2048]{2,1,0:T(4,128)S(1)} %get-tuple-element.16.taps_ref, ...), custom_call_target="tpu_custom_call" | custom-call | flops 8388608 | bytes 1048576 | tf_op jit(solution)/shard_map/gated_half/pallas_call | solution.py:219
  42.7 0.7 collective-permute-start.4
  43.4 1.2 collective-permute-done.11
  44.6 0.6 collective-permute-start.12
  45.2 3.0 %convolution_convert_fusion.4 = bf16[64,2048]{1,0:T(8,128)(2,1)S(1)} fusion(bf16[1024,2048]{1,0:T(8,128)(2,1)} %param.13, bf16[64,1024]{1,0:T(8,128)(2,1)S(1)} %collective-permute-done.6, bf16[64,1024]{1,0:T(8,128)(2,1)S(1)} %collective-permute-done.7, pred[]{:T(512)S(6)} %eq.8), kind=kOutput, calls=%fused_computation.4 | convolution fusion | flops 268632064 | bytes 4718593 | tf_op jit(solution)/shard_map/dot_general | solution.py:338
  48.3 1.6 %collective-permute-start.8 = (bf16[64,2048]{1,0:T(8,128)(2,1)S(1)}, bf16[64,2048]{1,0:T(8,128)(2,1)S(1)}, u32[]{:S(2)}, u32[]{:S(2)}) collective-permute-start(bf16[64,2048]{1,0:T(8,128)(2,1)S(1)} %convolution_convert_fusion.4), channel_id=1, source_target_pairs={{0,4},{1,5},{2,6},{3,7},{4,0},{5,1},{6,2},{7,3},{8,12},{9,13},{10,... | collective-permute-start | bytes 786440 | tf_op jit(solution)/shard_map/ppermute | solution.py:253
  49.9 2.6 %collective-permute-start.17 = (bf16[128,1024]{1,0:T(8,128)(2,1)S(1)}, bf16[128,1024]{1,0:T(8,128)(2,1)S(1)}, u32[]{:S(2)}, u32[]{:S(2)}) collective-permute-start(bf16[128,1024]{1,0:T(8,128)(2,1)S(1)} %constant_dynamic-update-slice_fusion), channel_id=1, source_target_pairs={{0,2},{1,3},{2,0},{3,1},{4,6},{5,7},{6,4},{7,5},{8,10},{9,11},{10,... | collective-permute-start | bytes 786440 | tf_op jit(solution)/shard_map/ppermute | solution.py:253
  52.5 6.8 %collective-permute-start.5 = (bf16[128,1024]{1,0:T(8,128)(2,1)S(1)}, bf16[128,1024]{1,0:T(8,128)(2,1)S(1)}, u32[]{:S(2)}, u32[]{:S(2)}) collective-permute-start(bf16[128,1024]{1,0:T(8,128)(2,1)S(1)} %collective-permute-done.4), channel_id=1, source_target_pairs={{0,1},{1,0},{2,3},{3,2},{4,5},{5,4},{6,7},{7,6},{8,9},{9,8},{10,11... | collective-permute-start | bytes 786440 | tf_op jit(solution)/shard_map/ppermute | solution.py:253
  59.4 0.9 convolution_convert_fusion.3
  60.3 0.7 convolution_convert_fusion.1
  61.1 2.1 %collective-permute-start.21 = (bf16[128,2048]{1,0:T(8,128)(2,1)S(1)}, bf16[128,2048]{1,0:T(8,128)(2,1)S(1)}, u32[]{:S(2)}, u32[]{:S(2)}) collective-permute-start(bf16[128,2048]{1,0:T(8,128)(2,1)S(1)} %convolution_convert_fusion.1), channel_id=1, source_target_pairs={{0,4},{1,5},{2,6},{3,7},{4,0},{5,1},{6,2},{7,3},{8,12},{9,13},{10,... | collective-permute-start | bytes 1572872 | tf_op jit(solution)/shard_map/ppermute | solution.py:253
  63.1 0.7 fusion.10
  64.5 0.7 fusion.5
  65.2 2.3 %collective-permute-done.15 = bf16[128,1024]{1,0:T(8,128)(2,1)S(1)} collective-permute-done((bf16[128,1024]{1,0:T(8,128)(2,1)S(1)}, bf16[128,1024]{1,0:T(8,128)(2,1)S(1)}, u32[]{:S(2)}, u32[]{:S(2)}) %collective-permute-start.15) | collective-permute-done | bytes 262176 | tf_op jit(solution)/shard_map/ppermute | solution.py:253
  67.6 0.7 convolution_convert_fusion.2
  68.3 0.6 collective-permute-start.19
  69.1 0.7 fusion.8
  69.8 0.7 convolution_convert_fusion
  70.6 1.4 %collective-permute-start.23 = (bf16[128,2048]{1,0:T(8,128)(2,1)S(1)}, bf16[128,2048]{1,0:T(8,128)(2,1)S(1)}, u32[]{:S(2)}, u32[]{:S(2)}) collective-permute-start(bf16[128,2048]{1,0:T(8,128)(2,1)S(1)} %convolution_convert_fusion), channel_id=1, source_target_pairs={{0,4},{1,5},{2,6},{3,7},{4,0},{5,1},{6,2},{7,3},{8,12},{9,13},{10,... | collective-permute-start | bytes 1572872 | tf_op jit(solution)/shard_map/ppermute | solution.py:253
  71.9 0.7 fusion.3
  72.7 8.0 %collective-permute-done.21 = bf16[128,2048]{1,0:T(8,128)(2,1)S(1)} collective-permute-done((bf16[128,2048]{1,0:T(8,128)(2,1)S(1)}, bf16[128,2048]{1,0:T(8,128)(2,1)S(1)}, u32[]{:S(2)}, u32[]{:S(2)}) %collective-permute-start.21) | collective-permute-done | bytes 524320 | tf_op jit(solution)/shard_map/ppermute | solution.py:253
  80.8 0.7 collective-permute-start.22
  81.5 10.4 %collective-permute-done.19 = bf16[128,2048]{1,0:T(8,128)(2,1)S(1)} collective-permute-done((bf16[128,2048]{1,0:T(8,128)(2,1)S(1)}, bf16[128,2048]{1,0:T(8,128)(2,1)S(1)}, u32[]{:S(2)}, u32[]{:S(2)}) %collective-permute-start.19) | collective-permute-done | bytes 524320 | tf_op jit(solution)/shard_map/ppermute | solution.py:253
  92.0 1.6 %collective-permute-start.20 = (bf16[128,2048]{1,0:T(8,128)(2,1)S(1)}, bf16[128,2048]{1,0:T(8,128)(2,1)S(1)}, u32[]{:S(2)}, u32[]{:S(2)}) collective-permute-start(bf16[128,2048]{1,0:T(8,128)(2,1)S(1)} %add_convert_fusion.3), channel_id=1, source_target_pairs={{0,24},{1,25},{2,18},{3,19},{4,28},{5,29},{6,22},{7,23},{8,16},{9,... | collective-permute-start | bytes 1572872 | tf_op jit(solution)/shard_map/ppermute | solution.py:253
  93.6 8.6 %collective-permute-done.23 = bf16[128,2048]{1,0:T(8,128)(2,1)S(1)} collective-permute-done((bf16[128,2048]{1,0:T(8,128)(2,1)S(1)}, bf16[128,2048]{1,0:T(8,128)(2,1)S(1)}, u32[]{:S(2)}, u32[]{:S(2)}) %collective-permute-start.23) | collective-permute-done | bytes 524320 | tf_op jit(solution)/shard_map/ppermute | solution.py:253
  102.3 2.8 %collective-permute-start.24 = (bf16[128,2048]{1,0:T(8,128)(2,1)S(1)}, bf16[128,2048]{1,0:T(8,128)(2,1)S(1)}, u32[]{:S(2)}, u32[]{:S(2)}) collective-permute-start(bf16[128,2048]{1,0:T(8,128)(2,1)S(1)} %add_convert_fusion.1), channel_id=1, source_target_pairs={{0,8},{1,9},{2,2},{3,3},{4,12},{5,13},{6,6},{7,7},{8,0},{9,1},{10,... | collective-permute-start | bytes 1572872 | tf_op jit(solution)/shard_map/ppermute | solution.py:253
  105.2 1.2 collective-permute-start.14
  106.5 20.2 %collective-permute-done.14 = bf16[64,2048]{1,0:T(8,128)(2,1)S(1)} collective-permute-done((bf16[64,2048]{1,0:T(8,128)(2,1)S(1)}, bf16[64,2048]{1,0:T(8,128)(2,1)S(1)}, u32[]{:S(2)}, u32[]{:S(2)}) %collective-permute-start.14) | collective-permute-done | bytes 262176 | tf_op jit(solution)/shard_map/ppermute | solution.py:253
  126.7 1.2 add_convert_fusion
  (46 shorter events, 1.7 us)
Async XLA Ops:
  0.9 12.0 %collective-permute-start = (bf16[3,2,2048]{2,1,0:T(2,128)(2,1)S(1)}, bf16[3,2,2048]{2,1,0:T(2,128)(2,1)S(1)}, u32[]{:S(2)}, u32[]{:S(2)}) collective-permute-start(bf16[3,2,2048]{2,1,0:T(2,128)(2,1)S(1)} %slice.79), channel_id=1, source_target_pairs={{0,4},{4,8},{8,12},{12,16},{16,20},{20,24},{24,28},{1,5},{5,9},{9,... | collective-permute-start | bytes 73736 | tf_op jit(solution)/shard_map/ppermute | solution.py:257
  5.8 1.4 %copy-start = (bf16[3,128,2048]{2,1,0:T(8,128)(2,1)S(1)}, bf16[3,128,2048]{2,1,0:T(8,128)(2,1)}, u32[]{:S(2)}) copy-start(bf16[3,128,2048]{2,1,0:T(8,128)(2,1)} %block_hbm.1) | copy-start | bytes 4718596
  7.2 0.9 copy-start.1
  8.1 0.8 copy-start.2
  8.9 0.8 copy-start.3
  9.8 0.8 copy-start.4
  13.1 4.3 %collective-permute-start.1 = (f32[8,2048]{1,0:T(8,128)S(1)}, f32[8,2048]{1,0:T(8,128)S(1)}, u32[]{:S(2)}, u32[]{:S(2)}) collective-permute-start(f32[8,2048]{1,0:T(8,128)S(1)} %add_add_fusion), channel_id=1, source_target_pairs={{0,4},{4,0},{8,12},{12,8},{16,20},{20,16},{24,28},{28,24},{1,5},{5... | collective-permute-start | bytes 196616 | tf_op jit(solution)/shard_map/ppermute | solution.py:267
  17.5 4.3 %collective-permute-start.2 = (f32[8,2048]{1,0:T(8,128)S(1)}, f32[8,2048]{1,0:T(8,128)S(1)}, u32[]{:S(2)}, u32[]{:S(2)}) collective-permute-start(f32[8,2048]{1,0:T(8,128)S(1)} %add_select_fusion.1), channel_id=1, source_target_pairs={{0,8},{4,12},{8,0},{12,4},{16,24},{20,28},{24,16},{28,20},{1,9},{5... | collective-permute-start | bytes 196616 | tf_op jit(solution)/shard_map/ppermute | solution.py:267
  21.9 5.2 %collective-permute-start.3 = (f32[8,2048]{1,0:T(8,128)S(1)}, f32[8,2048]{1,0:T(8,128)S(1)}, u32[]{:S(2)}, u32[]{:S(2)}) collective-permute-start(f32[8,2048]{1,0:T(8,128)S(1)} %get-tuple-element.27), channel_id=1, source_target_pairs={{0,16},{4,20},{8,24},{12,28},{16,0},{20,4},{24,8},{28,12},{1,17},{... | collective-permute-start | bytes 196616 | tf_op jit(solution)/shard_map/ppermute | solution.py:267
  29.5 5.0 %collective-permute-start.10 = (bf16[64,1024]{1,0:T(8,128)(2,1)S(1)}, bf16[64,1024]{1,0:T(8,128)(2,1)S(1)}, u32[]{:S(2)}, u32[]{:S(2)}) collective-permute-start(bf16[64,1024]{1,0:T(8,128)(2,1)S(1)} %get-tuple-element.24), channel_id=1, source_target_pairs={{0,2},{1,3},{2,0},{3,1},{4,6},{5,7},{6,4},{7,5},{8,10},{9,11},{10,... | collective-permute-start | bytes 393224 | tf_op jit(solution)/shard_map/ppermute | solution.py:253
  31.1 9.2 %collective-permute-start.6 = (bf16[64,1024]{1,0:T(8,128)(2,1)S(1)}, bf16[64,1024]{1,0:T(8,128)(2,1)S(1)}, u32[]{:S(2)}, u32[]{:S(2)}) collective-permute-start(bf16[64,1024]{1,0:T(8,128)(2,1)S(1)} %get-tuple-element.22), channel_id=1, source_target_pairs={{0,4},{1,14},{2,21},{3,31},{4,0},{5,10},{6,17},{7,27},{8,6},{9,12}... | collective-permute-start | bytes 393224 | tf_op jit(solution)/shard_map/ppermute | solution.py:253
  34.6 10.1 %collective-permute-start.11 = (bf16[64,1024]{1,0:T(8,128)(2,1)S(1)}, bf16[64,1024]{1,0:T(8,128)(2,1)S(1)}, u32[]{:S(2)}, u32[]{:S(2)}) collective-permute-start(bf16[64,1024]{1,0:T(8,128)(2,1)S(1)} %collective-permute-done.10), channel_id=1, source_target_pairs={{0,21},{1,31},{2,4},{3,14},{4,17},{5,27},{6,0},{7,10},{8,23},{9,29... | collective-permute-start | bytes 393224 | tf_op jit(solution)/shard_map/ppermute | solution.py:253
  40.3 4.9 %collective-permute-start.7 = (bf16[64,1024]{1,0:T(8,128)(2,1)S(1)}, bf16[64,1024]{1,0:T(8,128)(2,1)S(1)}, u32[]{:S(2)}, u32[]{:S(2)}) collective-permute-start(bf16[64,1024]{1,0:T(8,128)(2,1)S(1)} %collective-permute-done.6), channel_id=1, source_target_pairs={{0,1},{1,0},{2,3},{3,2},{4,5},{5,4},{6,7},{7,6},{8,9},{9,8},{10,11... | collective-permute-start | bytes 393224 | tf_op jit(solution)/shard_map/ppermute | solution.py:253
  40.3 19.1 %copy-start.5 = (bf16[1024,2048]{1,0:T(8,128)(2,1)S(1)}, bf16[1024,2048]{1,0:T(8,128)(2,1)}, u32[]{:S(2)}) copy-start(bf16[1024,2048]{1,0:T(8,128)(2,1)} %param.13) | copy-start | bytes 12582916
  42.7 9.8 %collective-permute-start.4 = (bf16[128,1024]{1,0:T(8,128)(2,1)S(1)}, bf16[128,1024]{1,0:T(8,128)(2,1)S(1)}, u32[]{:S(2)}, u32[]{:S(2)}) collective-permute-start(bf16[128,1024]{1,0:T(8,128)(2,1)S(1)} %gated_half.2), channel_id=1, source_target_pairs={{0,0},{1,10},{2,17},{3,27},{4,4},{5,14},{6,21},{7,31},{8,2},{9,8},... | collective-permute-start | bytes 786440 | tf_op jit(solution)/shard_map/ppermute | solution.py:253
  44.6 14.7 %collective-permute-start.12 = (bf16[64,1024]{1,0:T(8,128)(2,1)S(1)}, bf16[64,1024]{1,0:T(8,128)(2,1)S(1)}, u32[]{:S(2)}, u32[]{:S(2)}) collective-permute-start(bf16[64,1024]{1,0:T(8,128)(2,1)S(1)} %collective-permute-done.11), channel_id=1, source_target_pairs={{0,1},{1,0},{2,3},{3,2},{4,5},{5,4},{6,7},{7,6},{8,9},{9,8},{10,11... | collective-permute-start | bytes 393224 | tf_op jit(solution)/shard_map/ppermute | solution.py:253
  48.3 15.7 %collective-permute-start.8 = (bf16[64,2048]{1,0:T(8,128)(2,1)S(1)}, bf16[64,2048]{1,0:T(8,128)(2,1)S(1)}, u32[]{:S(2)}, u32[]{:S(2)}) collective-permute-start(bf16[64,2048]{1,0:T(8,128)(2,1)S(1)} %convolution_convert_fusion.4), channel_id=1, source_target_pairs={{0,4},{1,5},{2,6},{3,7},{4,0},{5,1},{6,2},{7,3},{8,12},{9,13},{10,... | collective-permute-start | bytes 786440 | tf_op jit(solution)/shard_map/ppermute | solution.py:253
  49.9 14.6 %collective-permute-start.17 = (bf16[128,1024]{1,0:T(8,128)(2,1)S(1)}, bf16[128,1024]{1,0:T(8,128)(2,1)S(1)}, u32[]{:S(2)}, u32[]{:S(2)}) collective-permute-start(bf16[128,1024]{1,0:T(8,128)(2,1)S(1)} %constant_dynamic-update-slice_fusion), channel_id=1, source_target_pairs={{0,2},{1,3},{2,0},{3,1},{4,6},{5,7},{6,4},{7,5},{8,10},{9,11},{10,... | collective-permute-start | bytes 786440 | tf_op jit(solution)/shard_map/ppermute | solution.py:253
  52.5 8.5 %collective-permute-start.5 = (bf16[128,1024]{1,0:T(8,128)(2,1)S(1)}, bf16[128,1024]{1,0:T(8,128)(2,1)S(1)}, u32[]{:S(2)}, u32[]{:S(2)}) collective-permute-start(bf16[128,1024]{1,0:T(8,128)(2,1)S(1)} %collective-permute-done.4), channel_id=1, source_target_pairs={{0,1},{1,0},{2,3},{3,2},{4,5},{5,4},{6,7},{7,6},{8,9},{9,8},{10,11... | collective-permute-start | bytes 786440 | tf_op jit(solution)/shard_map/ppermute | solution.py:253
  59.3 8.2 %collective-permute-start.15 = (bf16[128,1024]{1,0:T(8,128)(2,1)S(1)}, bf16[128,1024]{1,0:T(8,128)(2,1)S(1)}, u32[]{:S(2)}, u32[]{:S(2)}) collective-permute-start(bf16[128,1024]{1,0:T(8,128)(2,1)S(1)} %collective-permute-done.4), channel_id=1, source_target_pairs={{0,2},{1,3},{2,0},{3,1},{4,6},{5,7},{6,4},{7,5},{8,10},{9,11},{10,... | collective-permute-start | bytes 786440 | tf_op jit(solution)/shard_map/ppermute | solution.py:253
  60.2 44.9 %collective-permute-start.13 = (bf16[64,2048]{1,0:T(8,128)(2,1)S(1)}, bf16[64,2048]{1,0:T(8,128)(2,1)S(1)}, u32[]{:S(2)}, u32[]{:S(2)}) collective-permute-start(bf16[64,2048]{1,0:T(8,128)(2,1)S(1)} %convolution_convert_fusion.3), channel_id=1, source_target_pairs={{0,4},{1,5},{2,6},{3,7},{4,0},{5,1},{6,2},{7,3},{8,12},{9,13},{10,... | collective-permute-start | bytes 786440 | tf_op jit(solution)/shard_map/ppermute | solution.py:253
  61.1 19.6 %collective-permute-start.21 = (bf16[128,2048]{1,0:T(8,128)(2,1)S(1)}, bf16[128,2048]{1,0:T(8,128)(2,1)S(1)}, u32[]{:S(2)}, u32[]{:S(2)}) collective-permute-start(bf16[128,2048]{1,0:T(8,128)(2,1)S(1)} %convolution_convert_fusion.1), channel_id=1, source_target_pairs={{0,4},{1,5},{2,6},{3,7},{4,0},{5,1},{6,2},{7,3},{8,12},{9,13},{10,... | collective-permute-start | bytes 1572872 | tf_op jit(solution)/shard_map/ppermute | solution.py:253
  64.0 42.4 %collective-permute-start.9 = (bf16[64,2048]{1,0:T(8,128)(2,1)S(1)}, bf16[64,2048]{1,0:T(8,128)(2,1)S(1)}, u32[]{:S(2)}, u32[]{:S(2)}) collective-permute-start(bf16[64,2048]{1,0:T(8,128)(2,1)S(1)} %add_convert_fusion.5), channel_id=1, source_target_pairs={{0,16},{1,17},{2,26},{3,27},{4,20},{5,21},{6,30},{7,31},{8,24},{9,... | collective-permute-start | bytes 786440 | tf_op jit(solution)/shard_map/ppermute | solution.py:253
  64.5 3.1 %collective-permute-start.18 = (bf16[128,1024]{1,0:T(8,128)(2,1)S(1)}, bf16[128,1024]{1,0:T(8,128)(2,1)S(1)}, u32[]{:S(2)}, u32[]{:S(2)}) collective-permute-start(bf16[128,1024]{1,0:T(8,128)(2,1)S(1)} %collective-permute-done.17), channel_id=1, source_target_pairs={{0,1},{1,0},{2,3},{3,2},{4,5},{5,4},{6,7},{7,6},{8,9},{9,8},{10,11... | collective-permute-start | bytes 786440 | tf_op jit(solution)/shard_map/ppermute | solution.py:253
  67.6 1.5 %collective-permute-start.16 = (bf16[128,1024]{1,0:T(8,128)(2,1)S(1)}, bf16[128,1024]{1,0:T(8,128)(2,1)S(1)}, u32[]{:S(2)}, u32[]{:S(2)}) collective-permute-start(bf16[128,1024]{1,0:T(8,128)(2,1)S(1)} %collective-permute-done.15), channel_id=1, source_target_pairs={{0,1},{1,0},{2,3},{3,2},{4,5},{5,4},{6,7},{7,6},{8,9},{9,8},{10,11... | collective-permute-start | bytes 786440 | tf_op jit(solution)/shard_map/ppermute | solution.py:253
  68.3 23.6 %collective-permute-start.19 = (bf16[128,2048]{1,0:T(8,128)(2,1)S(1)}, bf16[128,2048]{1,0:T(8,128)(2,1)S(1)}, u32[]{:S(2)}, u32[]{:S(2)}) collective-permute-start(bf16[128,2048]{1,0:T(8,128)(2,1)S(1)} %convolution_convert_fusion.2), channel_id=1, source_target_pairs={{0,4},{1,5},{2,6},{3,7},{4,0},{5,1},{6,2},{7,3},{8,12},{9,13},{10,... | collective-permute-start | bytes 1572872 | tf_op jit(solution)/shard_map/ppermute | solution.py:253
  70.6 31.6 %collective-permute-start.23 = (bf16[128,2048]{1,0:T(8,128)(2,1)S(1)}, bf16[128,2048]{1,0:T(8,128)(2,1)S(1)}, u32[]{:S(2)}, u32[]{:S(2)}) collective-permute-start(bf16[128,2048]{1,0:T(8,128)(2,1)S(1)} %convolution_convert_fusion), channel_id=1, source_target_pairs={{0,4},{1,5},{2,6},{3,7},{4,0},{5,1},{6,2},{7,3},{8,12},{9,13},{10,... | collective-permute-start | bytes 1572872 | tf_op jit(solution)/shard_map/ppermute | solution.py:253
  72.7 54.0 %copy-start.6 = (bf16[128,2048]{1,0:T(8,128)(2,1)S(1)}, bf16[128,2048]{1,0:T(8,128)(2,1)}, u32[]{:S(2)}) copy-start(bf16[128,2048]{1,0:T(8,128)(2,1)} %param.7) | copy-start | bytes 1572868
  80.8 45.8 %collective-permute-start.22 = (bf16[128,2048]{1,0:T(8,128)(2,1)S(1)}, bf16[128,2048]{1,0:T(8,128)(2,1)S(1)}, u32[]{:S(2)}, u32[]{:S(2)}) collective-permute-start(bf16[128,2048]{1,0:T(8,128)(2,1)S(1)} %add_convert_fusion.2), channel_id=1, source_target_pairs={{0,0},{1,1},{2,10},{3,11},{4,4},{5,5},{6,14},{7,15},{8,8},{9,9},{1... | collective-permute-start | bytes 1572872 | tf_op jit(solution)/shard_map/ppermute | solution.py:253
  92.0 34.6 %collective-permute-start.20 = (bf16[128,2048]{1,0:T(8,128)(2,1)S(1)}, bf16[128,2048]{1,0:T(8,128)(2,1)S(1)}, u32[]{:S(2)}, u32[]{:S(2)}) collective-permute-start(bf16[128,2048]{1,0:T(8,128)(2,1)S(1)} %add_convert_fusion.3), channel_id=1, source_target_pairs={{0,24},{1,25},{2,18},{3,19},{4,28},{5,29},{6,22},{7,23},{8,16},{9,... | collective-permute-start | bytes 1572872 | tf_op jit(solution)/shard_map/ppermute | solution.py:253
  102.3 24.3 %collective-permute-start.24 = (bf16[128,2048]{1,0:T(8,128)(2,1)S(1)}, bf16[128,2048]{1,0:T(8,128)(2,1)S(1)}, u32[]{:S(2)}, u32[]{:S(2)}) collective-permute-start(bf16[128,2048]{1,0:T(8,128)(2,1)S(1)} %add_convert_fusion.1), channel_id=1, source_target_pairs={{0,8},{1,9},{2,2},{3,3},{4,12},{5,13},{6,6},{7,7},{8,0},{9,1},{10,... | collective-permute-start | bytes 1572872 | tf_op jit(solution)/shard_map/ppermute | solution.py:253
  105.2 21.4 %collective-permute-start.14 = (bf16[64,2048]{1,0:T(8,128)(2,1)S(1)}, bf16[64,2048]{1,0:T(8,128)(2,1)S(1)}, u32[]{:S(2)}, u32[]{:S(2)}) collective-permute-start(bf16[64,2048]{1,0:T(8,128)(2,1)S(1)} %add_convert_fusion.4), channel_id=1, source_target_pairs={{0,16},{1,17},{2,26},{3,27},{4,20},{5,21},{6,30},{7,31},{8,24},{9,... | collective-permute-start | bytes 786440 | tf_op jit(solution)/shard_map/ppermute | solution.py:253

commit v3 on v2

--- a/solution.py
+++ b/solution.py
@@ -64,22 +64,20 @@
 
 
 def states_kernel(
-    block_hbm, taps_hbm, decay_hbm, residues_hbm, carried_hbm,
-    end_ref, block_ref, taps_ref, decay_ref, residues_ref, carried_ref, kb, vb, sems,
+    block_hbm, taps_hbm, small_hbm, end_ref, block_ref, taps_ref, small_ref, kb, vb, sems
 ):
     tokens, count = block_ref.shape[1:]
-    poles = decay_ref.shape[0]
+    poles = end_ref.shape[0]
+    decay_ref = small_ref.at[0]
     steps = tokens // SUBLANES
-    parts = sems.shape[0] - 5
+    parts = sems.shape[0] - 3
     width = count // parts
     small = [
         pltpu.make_async_copy(source, target, sems.at[parts + i])
         for i, (source, target) in enumerate(
             [
                 (taps_hbm, taps_ref),
-                (decay_hbm, decay_ref),
-                (residues_hbm, residues_ref),
-                (carried_hbm, carried_ref),
+                (small_hbm, small_ref),
                 (block_hbm.at[:1], block_ref.at[:1]),
             ]
         )
@@ -125,12 +123,12 @@
 
 
 def gated_kernel(
-    j, lines, parts, place_ref, block_ref, halo_ref, taps_ref, decay_ref, residues_ref,
-    carried_ref, prefix_ref, last_ref, *refs,
+    j, lines, parts, place_ref, block_ref, halo_ref, taps_ref, small_ref, prefix_ref, last_ref, *refs
 ):
     *out_refs, qb, kb, vb, pb, ob = refs[len(refs) - parts - 5 :]
     tokens, share = block_ref.shape[1], out_refs[0].shape[1]
-    poles = decay_ref.shape[0]
+    poles = prefix_ref.shape[0]
+    decay_ref, residues_ref, carried_ref = (small_ref.at[i] for i in range(3))
     steps = tokens // SUBLANES
     first = lax.rem(place_ref[0] + j, lines) * share
     since_start = (place_ref[0] * tokens).astype(F32)
@@ -194,17 +192,17 @@
 
 
 def end_states(*arrays):
-    features, _, rates = arrays[:3]
+    features, _, small = arrays
     _, tokens, count = features.shape
-    poles = rates.shape[0]
+    poles = small.shape[1]
     return pl.pallas_call(
         states_kernel,
-        in_specs=[pl.BlockSpec(memory_space=pltpu.HBM)] * 5,
-        out_specs=[VMEM] * 6,
+        in_specs=[pl.BlockSpec(memory_space=pltpu.HBM)] * 3,
+        out_specs=[VMEM] * 4,
         out_shape=[jax.ShapeDtypeStruct((poles, count), F32)]
         + [jax.ShapeDtypeStruct(array.shape, array.dtype) for array in arrays],
         scratch_shapes=[pltpu.VMEM((TOGETHER, PAD + tokens, LANES), F32)] * 2
-        + [pltpu.SemaphoreType.DMA((math_gcd(count // LANES, 4) + 5,))],
+        + [pltpu.SemaphoreType.DMA((math_gcd(count // LANES, 4) + 3,))],
         compiler_params=ROOM,
         cost_estimate=pl.CostEstimate(
             flops=4 * poles * tokens * count, bytes_accessed=6 * tokens * count, transcendentals=0
@@ -252,14 +250,13 @@
     def moved(block, target):
         return lax.ppermute(block, both, [(number(*p), number(*target(*p))) for p in places])
 
-    rates, weights, carried = decay.T, residues.T, state_in.T
     reach = conv_taps.shape[1] - 1
     halo = lax.ppermute(
         features[:, tokens - reach :, :], "seq", [(s, s + 1) for s in range(seqs - 1)]
     )
-    ends, features, conv_taps, rates, weights, carried = end_states(
-        features, conv_taps, rates, weights, carried
-    )
+    small = jnp.stack([decay.T, residues.T, state_in.T])
+    ends, features, conv_taps, small = end_states(features, conv_taps, small)
+    rates = small[0]
     ends = ends + first_tokens(features[1:, :reach], halo[1:], conv_taps[1:], rates, tokens)
     prefix = jnp.zeros_like(ends)
     width = 1
@@ -280,8 +277,8 @@
     blocks = {}
     for j in order:
         results = gated_half(
-            j, lines, 2 if j else 1, place, share, (features, halo, conv_taps, rates, weights),
-            (carried, prefix, other), [],
+            j, lines, 2 if j else 1, place, share, (features, halo, conv_taps, small),
+            (prefix, other), [],
         )
         blocks[j] = [moved(results[0], lambda a, b, c: (c, (b + j) % lines, turned[a ^ c]))]
         if j:

time: 128 us -> 127 us (level)
  local copies, waits for them, and re-layouts: 5.83 us -> 3.32 us
    unnamed x15 -> x9, local copies, waits for them, and re-layouts: 4.83 us -> 2.32 us
where the time goes in v3:
time: 127 us; the launch traced here: 126 us
  waiting for transfers between devices  66.4 us (52%)
  starting transfers between devices  37.2 us (29%)
  matrix products  9.01 us (7%)
  Pallas kernels  7.08 us (6%)
  local copies, waits for them, and re-layouts  3.32 us (3%)
  other arithmetic  2.91 us (2%)
    ppermute x21, waiting for transfers between devices, moved(): lax.ppermute(block, both, [(number(*p), number(*target(*p))) for p in pla...  58.7 us
    ppermute x21, starting transfers between devices, moved(): lax.ppermute(block, both, [(number(*p), number(*target(*p))) for p in pla...  26.3 us
    dot_general x9, matrix products, product_of(): product = jnp.dot(block, weight, preferred_element_type=F32)  9.01 us
    ppermute x3, waiting for transfers between devices, shards(): other = lax.ppermute(ends, 'seq', [(s, s ^ width) for s in range(seqs)])  7.75 us
    ppermute x3, starting transfers between devices, shards(): other = lax.ppermute(ends, 'seq', [(s, s ^ width) for s in range(seqs)])  6.06 us
    ppermute x1, starting transfers between devices, shards(): lax.ppermute(features[:, tokens - reach:, :], 'seq', [(s, s + 1) for s in...  4.87 us
    pallas_call x2, Pallas kernels, gated_half(): pl.pallas_call(functools.partial(gated_kernel, j, lines, parts), in_specs...  4.8 us
  transfers between devices with their start and end apart: 25, of which 12 were waited for; matrix products, arithmetic and copies ran while one was open for 8% of the time, Pallas kernels for 4%

profile of v3, /device:TPU:0, one launch (start us, length us, event | category | flops | bytes accessed | tf_op | source)
XLA Modules:
  0.0 126.3 jit_solution(14890850593029056166)
XLA Ops:
  0.0 0.9 slice.82
  0.9 4.9 %collective-permute-start = (bf16[3,2,2048]{2,1,0:T(2,128)(2,1)S(1)}, bf16[3,2,2048]{2,1,0:T(2,128)(2,1)S(1)}, u32[]{:S(2)}, u32[]{:S(2)}) collective-permute-start(bf16[3,2,2048]{2,1,0:T(2,128)(2,1)S(1)} %slice.82), channel_id=1, source_target_pairs={{0,4},{4,8},{8,12},{12,16},{16,20},{20,24},{24,28},{1,5},{5,9},{9,... | collective-permute-start | bytes 73736 | tf_op jit(solution)/shard_map/ppermute | solution.py:254
  5.8 0.9 pad_maximum_fusion.small_hbm
  6.7 1.4 %copy-done = bf16[3,128,2048]{2,1,0:T(8,128)(2,1)S(1)} copy-done((bf16[3,128,2048]{2,1,0:T(8,128)(2,1)S(1)}, bf16[3,128,2048]{2,1,0:T(8,128)(2,1)}, u32[]{:S(2)}) %copy-start) | copy-done | bytes 1572888
  8.1 0.9 copy-done.1
  9.0 2.3 %end_states.1 = (f32[8,2048]{1,0:T(8,128)S(1)}, bf16[3,128,2048]{2,1,0:T(8,128)(2,1)S(1)}, f32[3,3,2048]{2,1,0:T(4,128)S(1)}, f32[3,8,2048]{2,1,0:T(8,128)S(1)}) custom-call(bf16[3,128,2048]{2,1,0:T(8,128)(2,1)S(1)} %copy-done, f32[3,3,2048]{2,1,0:T(4,128)S(1)} %copy-done.1, f32[3,8,2048]{2,1,0:T(8,128)S(1)} %pad_maximum_fusion.small_hbm), custom_call_target="tpu_custom_call" | custom-call | flops 8388608 | bytes 1572864 | tf_op jit(solution)/shard_map/end_states/pallas_call | solution.py:198
  11.5 1.6 %collective-permute-start.1 = (f32[8,2048]{1,0:T(8,128)S(1)}, f32[8,2048]{1,0:T(8,128)S(1)}, u32[]{:S(2)}, u32[]{:S(2)}) collective-permute-start(f32[8,2048]{1,0:T(8,128)S(1)} %fusion.29), channel_id=1, source_target_pairs={{0,4},{4,0},{8,12},{12,8},{16,20},{20,16},{24,28},{28,24},{1,5},{5... | collective-permute-start | bytes 196616 | tf_op jit(solution)/shard_map/ppermute | solution.py:264
  13.1 2.7 %collective-permute-done.1 = f32[8,2048]{1,0:T(8,128)S(1)} collective-permute-done((f32[8,2048]{1,0:T(8,128)S(1)}, f32[8,2048]{1,0:T(8,128)S(1)}, u32[]{:S(2)}, u32[]{:S(2)}) %collective-permute-start.1) | collective-permute-done | bytes 65568 | tf_op jit(solution)/shard_map/ppermute | solution.py:264
  15.9 1.6 %collective-permute-start.2 = (f32[8,2048]{1,0:T(8,128)S(1)}, f32[8,2048]{1,0:T(8,128)S(1)}, u32[]{:S(2)}, u32[]{:S(2)}) collective-permute-start(f32[8,2048]{1,0:T(8,128)S(1)} %fusion.31), channel_id=1, source_target_pairs={{0,8},{4,12},{8,0},{12,4},{16,24},{20,28},{24,16},{28,20},{1,9},{5... | collective-permute-start | bytes 196616 | tf_op jit(solution)/shard_map/ppermute | solution.py:264
  17.5 2.7 %collective-permute-done.2 = f32[8,2048]{1,0:T(8,128)S(1)} collective-permute-done((f32[8,2048]{1,0:T(8,128)S(1)}, f32[8,2048]{1,0:T(8,128)S(1)}, u32[]{:S(2)}, u32[]{:S(2)}) %collective-permute-start.2) | collective-permute-done | bytes 65568 | tf_op jit(solution)/shard_map/ppermute | solution.py:264
  20.3 2.8 %collective-permute-start.3 = (f32[8,2048]{1,0:T(8,128)S(1)}, f32[8,2048]{1,0:T(8,128)S(1)}, u32[]{:S(2)}, u32[]{:S(2)}) collective-permute-start(f32[8,2048]{1,0:T(8,128)S(1)} %get-tuple-element.23), channel_id=1, source_target_pairs={{0,16},{4,20},{8,24},{12,28},{16,0},{20,4},{24,8},{28,12},{1,17},{... | collective-permute-start | bytes 196616 | tf_op jit(solution)/shard_map/ppermute | solution.py:264
  23.1 2.4 %collective-permute-done.3.last_ref = f32[8,2048]{1,0:T(8,128)S(1)} collective-permute-done((f32[8,2048]{1,0:T(8,128)S(1)}, f32[8,2048]{1,0:T(8,128)S(1)}, u32[]{:S(2)}, u32[]{:S(2)}) %collective-permute-start.3) | collective-permute-done | bytes 65568 | tf_op jit(solution)/shard_map/ppermute | solution.py:264
  25.5 2.4 %gated_half.3 = (bf16[64,1024]{1,0:T(8,128)(2,1)S(1)}, bf16[64,1024]{1,0:T(8,128)(2,1)S(1)}) custom-call(s32[2]{0:T(128)S(1)} %pad_add_fusion.place_ref, bf16[3,128,2048]{2,1,0:T(8,128)(2,1)S(1)} %get-tuple-element.13.block_ref, bf16[3,2,2048]{2,1,0:T(2,128)(2,1)S(1)} %collective-permute-done.halo_ref, f32[3,3,2048]{2,1,0:T(4,128)S(1)} %get-tuple-element.14.taps_ref, ...), custom_call_target="tpu_custom_call" | custom-call | flops 8388608 | bytes 1048576 | tf_op jit(solution)/shard_map/gated_half/pallas_call | solution.py:217
  27.9 1.6 %collective-permute-start.10 = (bf16[64,1024]{1,0:T(8,128)(2,1)S(1)}, bf16[64,1024]{1,0:T(8,128)(2,1)S(1)}, u32[]{:S(2)}, u32[]{:S(2)}) collective-permute-start(bf16[64,1024]{1,0:T(8,128)(2,1)S(1)} %get-tuple-element.20), channel_id=1, source_target_pairs={{0,2},{1,3},{2,0},{3,1},{4,6},{5,7},{6,4},{7,5},{8,10},{9,11},{10,... | collective-permute-start | bytes 393224 | tf_op jit(solution)/shard_map/ppermute | solution.py:251
  29.5 1.5 %collective-permute-start.6 = (bf16[64,1024]{1,0:T(8,128)(2,1)S(1)}, bf16[64,1024]{1,0:T(8,128)(2,1)S(1)}, u32[]{:S(2)}, u32[]{:S(2)}) collective-permute-start(bf16[64,1024]{1,0:T(8,128)(2,1)S(1)} %get-tuple-element.18), channel_id=1, source_target_pairs={{0,4},{1,14},{2,21},{3,31},{4,0},{5,10},{6,17},{7,27},{8,6},{9,12}... | collective-permute-start | bytes 393224 | tf_op jit(solution)/shard_map/ppermute | solution.py:251
  31.0 1.9 %collective-permute-done.10 = bf16[64,1024]{1,0:T(8,128)(2,1)S(1)} collective-permute-done((bf16[64,1024]{1,0:T(8,128)(2,1)S(1)}, bf16[64,1024]{1,0:T(8,128)(2,1)S(1)}, u32[]{:S(2)}, u32[]{:S(2)}) %collective-permute-start.10) | collective-permute-done | bytes 131104 | tf_op jit(solution)/shard_map/ppermute | solution.py:251
  32.9 5.7 %collective-permute-done.6 = bf16[64,1024]{1,0:T(8,128)(2,1)S(1)} collective-permute-done((bf16[64,1024]{1,0:T(8,128)(2,1)S(1)}, bf16[64,1024]{1,0:T(8,128)(2,1)S(1)}, u32[]{:S(2)}, u32[]{:S(2)}) %collective-permute-start.6) | collective-permute-done | bytes 131104 | tf_op jit(solution)/shard_map/ppermute | solution.py:251
  38.7 2.4 %gated_half.2 = bf16[128,1024]{1,0:T(8,128)(2,1)S(1)} custom-call(s32[2]{0:T(128)S(1)} %pad_add_fusion.place_ref, bf16[3,128,2048]{2,1,0:T(8,128)(2,1)S(1)} %get-tuple-element.13.block_ref, bf16[3,2,2048]{2,1,0:T(2,128)(2,1)S(1)} %collective-permute-done.halo_ref, f32[3,3,2048]{2,1,0:T(4,128)S(1)} %get-tuple-element.14.taps_ref, ...), custom_call_target="tpu_custom_call" | custom-call | flops 8388608 | bytes 1048576 | tf_op jit(solution)/shard_map/gated_half/pallas_call | solution.py:217
  41.1 0.7 collective-permute-start.4
  41.8 1.2 collective-permute-done.11
  43.0 0.6 collective-permute-start.12
  43.6 3.0 %convolution_convert_fusion.4 = bf16[64,2048]{1,0:T(8,128)(2,1)S(1)} fusion(bf16[1024,2048]{1,0:T(8,128)(2,1)} %param.13, bf16[64,1024]{1,0:T(8,128)(2,1)S(1)} %collective-permute-done.6, bf16[64,1024]{1,0:T(8,128)(2,1)S(1)} %collective-permute-done.7, pred[]{:T(512)S(6)} %eq.8), kind=kOutput, calls=%fused_computation.4 | convolution fusion | flops 268632064 | bytes 4718593 | tf_op jit(solution)/shard_map/dot_general | solution.py:335
  46.7 1.6 %collective-permute-start.8 = (bf16[64,2048]{1,0:T(8,128)(2,1)S(1)}, bf16[64,2048]{1,0:T(8,128)(2,1)S(1)}, u32[]{:S(2)}, u32[]{:S(2)}) collective-permute-start(bf16[64,2048]{1,0:T(8,128)(2,1)S(1)} %convolution_convert_fusion.4), channel_id=1, source_target_pairs={{0,4},{1,5},{2,6},{3,7},{4,0},{5,1},{6,2},{7,3},{8,12},{9,13},{10,... | collective-permute-start | bytes 786440 | tf_op jit(solution)/shard_map/ppermute | solution.py:251
  48.3 2.6 %collective-permute-start.17 = (bf16[128,1024]{1,0:T(8,128)(2,1)S(1)}, bf16[128,1024]{1,0:T(8,128)(2,1)S(1)}, u32[]{:S(2)}, u32[]{:S(2)}) collective-permute-start(bf16[128,1024]{1,0:T(8,128)(2,1)S(1)} %constant_dynamic-update-slice_fusion), channel_id=1, source_target_pairs={{0,2},{1,3},{2,0},{3,1},{4,6},{5,7},{6,4},{7,5},{8,10},{9,11},{10,... | collective-permute-start | bytes 786440 | tf_op jit(solution)/shard_map/ppermute | solution.py:251
  50.9 6.8 %collective-permute-start.5 = (bf16[128,1024]{1,0:T(8,128)(2,1)S(1)}, bf16[128,1024]{1,0:T(8,128)(2,1)S(1)}, u32[]{:S(2)}, u32[]{:S(2)}) collective-permute-start(bf16[128,1024]{1,0:T(8,128)(2,1)S(1)} %collective-permute-done.4), channel_id=1, source_target_pairs={{0,1},{1,0},{2,3},{3,2},{4,5},{5,4},{6,7},{7,6},{8,9},{9,8},{10,11... | collective-permute-start | bytes 786440 | tf_op jit(solution)/shard_map/ppermute | solution.py:251
  57.7 0.9 convolution_convert_fusion.3
  58.7 0.7 convolution_convert_fusion.1
  59.5 2.1 %collective-permute-start.21 = (bf16[128,2048]{1,0:T(8,128)(2,1)S(1)}, bf16[128,2048]{1,0:T(8,128)(2,1)S(1)}, u32[]{:S(2)}, u32[]{:S(2)}) collective-permute-start(bf16[128,2048]{1,0:T(8,128)(2,1)S(1)} %convolution_convert_fusion.1), channel_id=1, source_target_pairs={{0,4},{1,5},{2,6},{3,7},{4,0},{5,1},{6,2},{7,3},{8,12},{9,13},{10,... | collective-permute-start | bytes 1572872 | tf_op jit(solution)/shard_map/ppermute | solution.py:251
  61.5 0.7 fusion.10
  62.4 0.5 collective-permute-start.9
  62.9 0.7 fusion.5
  63.6 2.3 %collective-permute-done.15 = bf16[128,1024]{1,0:T(8,128)(2,1)S(1)} collective-permute-done((bf16[128,1024]{1,0:T(8,128)(2,1)S(1)}, bf16[128,1024]{1,0:T(8,128)(2,1)S(1)}, u32[]{:S(2)}, u32[]{:S(2)}) %collective-permute-start.15) | collective-permute-done | bytes 262176 | tf_op jit(solution)/shard_map/ppermute | solution.py:251
  66.0 0.7 convolution_convert_fusion.2
  66.7 0.6 collective-permute-start.19
  67.2 0.2 collective-permute-done.16
  67.5 0.7 fusion.8
  68.2 0.7 convolution_convert_fusion
  69.0 1.4 %collective-permute-start.23 = (bf16[128,2048]{1,0:T(8,128)(2,1)S(1)}, bf16[128,2048]{1,0:T(8,128)(2,1)S(1)}, u32[]{:S(2)}, u32[]{:S(2)}) collective-permute-start(bf16[128,2048]{1,0:T(8,128)(2,1)S(1)} %convolution_convert_fusion), channel_id=1, source_target_pairs={{0,4},{1,5},{2,6},{3,7},{4,0},{5,1},{6,2},{7,3},{8,12},{9,13},{10,... | collective-permute-start | bytes 1572872 | tf_op jit(solution)/shard_map/ppermute | solution.py:251
  70.3 0.7 fusion.3
  71.1 8.0 %collective-permute-done.21 = bf16[128,2048]{1,0:T(8,128)(2,1)S(1)} collective-permute-done((bf16[128,2048]{1,0:T(8,128)(2,1)S(1)}, bf16[128,2048]{1,0:T(8,128)(2,1)S(1)}, u32[]{:S(2)}, u32[]{:S(2)}) %collective-permute-start.21) | collective-permute-done | bytes 524320 | tf_op jit(solution)/shard_map/ppermute | solution.py:251
  79.2 0.7 collective-permute-start.22
  79.9 10.4 %collective-permute-done.19 = bf16[128,2048]{1,0:T(8,128)(2,1)S(1)} collective-permute-done((bf16[128,2048]{1,0:T(8,128)(2,1)S(1)}, bf16[128,2048]{1,0:T(8,128)(2,1)S(1)}, u32[]{:S(2)}, u32[]{:S(2)}) %collective-permute-start.19) | collective-permute-done | bytes 524320 | tf_op jit(solution)/shard_map/ppermute | solution.py:251
  90.4 1.6 %collective-permute-start.20 = (bf16[128,2048]{1,0:T(8,128)(2,1)S(1)}, bf16[128,2048]{1,0:T(8,128)(2,1)S(1)}, u32[]{:S(2)}, u32[]{:S(2)}) collective-permute-start(bf16[128,2048]{1,0:T(8,128)(2,1)S(1)} %add_convert_fusion.3), channel_id=1, source_target_pairs={{0,24},{1,25},{2,18},{3,19},{4,28},{5,29},{6,22},{7,23},{8,16},{9,... | collective-permute-start | bytes 1572872 | tf_op jit(solution)/shard_map/ppermute | solution.py:251
  92.0 8.6 %collective-permute-done.23 = bf16[128,2048]{1,0:T(8,128)(2,1)S(1)} collective-permute-done((bf16[128,2048]{1,0:T(8,128)(2,1)S(1)}, bf16[128,2048]{1,0:T(8,128)(2,1)S(1)}, u32[]{:S(2)}, u32[]{:S(2)}) %collective-permute-start.23) | collective-permute-done | bytes 524320 | tf_op jit(solution)/shard_map/ppermute | solution.py:251
  100.7 2.8 %collective-permute-start.24 = (bf16[128,2048]{1,0:T(8,128)(2,1)S(1)}, bf16[128,2048]{1,0:T(8,128)(2,1)S(1)}, u32[]{:S(2)}, u32[]{:S(2)}) collective-permute-start(bf16[128,2048]{1,0:T(8,128)(2,1)S(1)} %add_convert_fusion.1), channel_id=1, source_target_pairs={{0,8},{1,9},{2,2},{3,3},{4,12},{5,13},{6,6},{7,7},{8,0},{9,1},{10,... | collective-permute-start | bytes 1572872 | tf_op jit(solution)/shard_map/ppermute | solution.py:251
  103.6 1.2 collective-permute-start.14
  104.8 20.2 %collective-permute-done.14 = bf16[64,2048]{1,0:T(8,128)(2,1)S(1)} collective-permute-done((bf16[64,2048]{1,0:T(8,128)(2,1)S(1)}, bf16[64,2048]{1,0:T(8,128)(2,1)S(1)}, u32[]{:S(2)}, u32[]{:S(2)}) %collective-permute-start.14) | collective-permute-done | bytes 262176 | tf_op jit(solution)/shard_map/ppermute | solution.py:251
  125.1 1.2 add_convert_fusion
  (41 shorter events, 1.0 us)
Async XLA Ops:
  0.9 10.4 %collective-permute-start = (bf16[3,2,2048]{2,1,0:T(2,128)(2,1)S(1)}, bf16[3,2,2048]{2,1,0:T(2,128)(2,1)S(1)}, u32[]{:S(2)}, u32[]{:S(2)}) collective-permute-start(bf16[3,2,2048]{2,1,0:T(2,128)(2,1)S(1)} %slice.82), channel_id=1, source_target_pairs={{0,4},{4,8},{8,12},{12,16},{16,20},{20,24},{24,28},{1,5},{5,9},{9,... | collective-permute-start | bytes 73736 | tf_op jit(solution)/shard_map/ppermute | solution.py:254
  6.7 1.4 %copy-start = (bf16[3,128,2048]{2,1,0:T(8,128)(2,1)S(1)}, bf16[3,128,2048]{2,1,0:T(8,128)(2,1)}, u32[]{:S(2)}) copy-start(bf16[3,128,2048]{2,1,0:T(8,128)(2,1)} %block_hbm.1) | copy-start | bytes 4718596
  8.1 0.9 copy-start.1
  11.5 4.3 %collective-permute-start.1 = (f32[8,2048]{1,0:T(8,128)S(1)}, f32[8,2048]{1,0:T(8,128)S(1)}, u32[]{:S(2)}, u32[]{:S(2)}) collective-permute-start(f32[8,2048]{1,0:T(8,128)S(1)} %fusion.29), channel_id=1, source_target_pairs={{0,4},{4,0},{8,12},{12,8},{16,20},{20,16},{24,28},{28,24},{1,5},{5... | collective-permute-start | bytes 196616 | tf_op jit(solution)/shard_map/ppermute | solution.py:264
  15.9 4.3 %collective-permute-start.2 = (f32[8,2048]{1,0:T(8,128)S(1)}, f32[8,2048]{1,0:T(8,128)S(1)}, u32[]{:S(2)}, u32[]{:S(2)}) collective-permute-start(f32[8,2048]{1,0:T(8,128)S(1)} %fusion.31), channel_id=1, source_target_pairs={{0,8},{4,12},{8,0},{12,4},{16,24},{20,28},{24,16},{28,20},{1,9},{5... | collective-permute-start | bytes 196616 | tf_op jit(solution)/shard_map/ppermute | solution.py:264
  20.3 5.2 %collective-permute-start.3 = (f32[8,2048]{1,0:T(8,128)S(1)}, f32[8,2048]{1,0:T(8,128)S(1)}, u32[]{:S(2)}, u32[]{:S(2)}) collective-permute-start(f32[8,2048]{1,0:T(8,128)S(1)} %get-tuple-element.23), channel_id=1, source_target_pairs={{0,16},{4,20},{8,24},{12,28},{16,0},{20,4},{24,8},{28,12},{1,17},{... | collective-permute-start | bytes 196616 | tf_op jit(solution)/shard_map/ppermute | solution.py:264
  27.9 5.0 %collective-permute-start.10 = (bf16[64,1024]{1,0:T(8,128)(2,1)S(1)}, bf16[64,1024]{1,0:T(8,128)(2,1)S(1)}, u32[]{:S(2)}, u32[]{:S(2)}) collective-permute-start(bf16[64,1024]{1,0:T(8,128)(2,1)S(1)} %get-tuple-element.20), channel_id=1, source_target_pairs={{0,2},{1,3},{2,0},{3,1},{4,6},{5,7},{6,4},{7,5},{8,10},{9,11},{10,... | collective-permute-start | bytes 393224 | tf_op jit(solution)/shard_map/ppermute | solution.py:251
  29.5 9.2 %collective-permute-start.6 = (bf16[64,1024]{1,0:T(8,128)(2,1)S(1)}, bf16[64,1024]{1,0:T(8,128)(2,1)S(1)}, u32[]{:S(2)}, u32[]{:S(2)}) collective-permute-start(bf16[64,1024]{1,0:T(8,128)(2,1)S(1)} %get-tuple-element.18), channel_id=1, source_target_pairs={{0,4},{1,14},{2,21},{3,31},{4,0},{5,10},{6,17},{7,27},{8,6},{9,12}... | collective-permute-start | bytes 393224 | tf_op jit(solution)/shard_map/ppermute | solution.py:251
  32.9 10.1 %collective-permute-start.11 = (bf16[64,1024]{1,0:T(8,128)(2,1)S(1)}, bf16[64,1024]{1,0:T(8,128)(2,1)S(1)}, u32[]{:S(2)}, u32[]{:S(2)}) collective-permute-start(bf16[64,1024]{1,0:T(8,128)(2,1)S(1)} %collective-permute-done.10), channel_id=1, source_target_pairs={{0,21},{1,31},{2,4},{3,14},{4,17},{5,27},{6,0},{7,10},{8,23},{9,29... | collective-permute-start | bytes 393224 | tf_op jit(solution)/shard_map/ppermute | solution.py:251
  38.7 4.9 %collective-permute-start.7 = (bf16[64,1024]{1,0:T(8,128)(2,1)S(1)}, bf16[64,1024]{1,0:T(8,128)(2,1)S(1)}, u32[]{:S(2)}, u32[]{:S(2)}) collective-permute-start(bf16[64,1024]{1,0:T(8,128)(2,1)S(1)} %collective-permute-done.6), channel_id=1, source_target_pairs={{0,1},{1,0},{2,3},{3,2},{4,5},{5,4},{6,7},{7,6},{8,9},{9,8},{10,11... | collective-permute-start | bytes 393224 | tf_op jit(solution)/shard_map/ppermute | solution.py:251
  38.7 19.1 %copy-start.2 = (bf16[1024,2048]{1,0:T(8,128)(2,1)S(1)}, bf16[1024,2048]{1,0:T(8,128)(2,1)}, u32[]{:S(2)}) copy-start(bf16[1024,2048]{1,0:T(8,128)(2,1)} %param.13) | copy-start | bytes 12582916
  41.1 9.8 %collective-permute-start.4 = (bf16[128,1024]{1,0:T(8,128)(2,1)S(1)}, bf16[128,1024]{1,0:T(8,128)(2,1)S(1)}, u32[]{:S(2)}, u32[]{:S(2)}) collective-permute-start(bf16[128,1024]{1,0:T(8,128)(2,1)S(1)} %gated_half.2), channel_id=1, source_target_pairs={{0,0},{1,10},{2,17},{3,27},{4,4},{5,14},{6,21},{7,31},{8,2},{9,8},... | collective-permute-start | bytes 786440 | tf_op jit(solution)/shard_map/ppermute | solution.py:251
  43.0 14.7 %collective-permute-start.12 = (bf16[64,1024]{1,0:T(8,128)(2,1)S(1)}, bf16[64,1024]{1,0:T(8,128)(2,1)S(1)}, u32[]{:S(2)}, u32[]{:S(2)}) collective-permute-start(bf16[64,1024]{1,0:T(8,128)(2,1)S(1)} %collective-permute-done.11), channel_id=1, source_target_pairs={{0,1},{1,0},{2,3},{3,2},{4,5},{5,4},{6,7},{7,6},{8,9},{9,8},{10,11... | collective-permute-start | bytes 393224 | tf_op jit(solution)/shard_map/ppermute | solution.py:251
  46.7 15.7 %collective-permute-start.8 = (bf16[64,2048]{1,0:T(8,128)(2,1)S(1)}, bf16[64,2048]{1,0:T(8,128)(2,1)S(1)}, u32[]{:S(2)}, u32[]{:S(2)}) collective-permute-start(bf16[64,2048]{1,0:T(8,128)(2,1)S(1)} %convolution_convert_fusion.4), channel_id=1, source_target_pairs={{0,4},{1,5},{2,6},{3,7},{4,0},{5,1},{6,2},{7,3},{8,12},{9,13},{10,... | collective-permute-start | bytes 786440 | tf_op jit(solution)/shard_map/ppermute | solution.py:251
  48.3 14.6 %collective-permute-start.17 = (bf16[128,1024]{1,0:T(8,128)(2,1)S(1)}, bf16[128,1024]{1,0:T(8,128)(2,1)S(1)}, u32[]{:S(2)}, u32[]{:S(2)}) collective-permute-start(bf16[128,1024]{1,0:T(8,128)(2,1)S(1)} %constant_dynamic-update-slice_fusion), channel_id=1, source_target_pairs={{0,2},{1,3},{2,0},{3,1},{4,6},{5,7},{6,4},{7,5},{8,10},{9,11},{10,... | collective-permute-start | bytes 786440 | tf_op jit(solution)/shard_map/ppermute | solution.py:251
  50.9 8.5 %collective-permute-start.5 = (bf16[128,1024]{1,0:T(8,128)(2,1)S(1)}, bf16[128,1024]{1,0:T(8,128)(2,1)S(1)}, u32[]{:S(2)}, u32[]{:S(2)}) collective-permute-start(bf16[128,1024]{1,0:T(8,128)(2,1)S(1)} %collective-permute-done.4), channel_id=1, source_target_pairs={{0,1},{1,0},{2,3},{3,2},{4,5},{5,4},{6,7},{7,6},{8,9},{9,8},{10,11... | collective-permute-start | bytes 786440 | tf_op jit(solution)/shard_map/ppermute | solution.py:251
  57.7 8.2 %collective-permute-start.15 = (bf16[128,1024]{1,0:T(8,128)(2,1)S(1)}, bf16[128,1024]{1,0:T(8,128)(2,1)S(1)}, u32[]{:S(2)}, u32[]{:S(2)}) collective-permute-start(bf16[128,1024]{1,0:T(8,128)(2,1)S(1)} %collective-permute-done.4), channel_id=1, source_target_pairs={{0,2},{1,3},{2,0},{3,1},{4,6},{5,7},{6,4},{7,5},{8,10},{9,11},{10,... | collective-permute-start | bytes 786440 | tf_op jit(solution)/shard_map/ppermute | solution.py:251
  58.6 44.9 %collective-permute-start.13 = (bf16[64,2048]{1,0:T(8,128)(2,1)S(1)}, bf16[64,2048]{1,0:T(8,128)(2,1)S(1)}, u32[]{:S(2)}, u32[]{:S(2)}) collective-permute-start(bf16[64,2048]{1,0:T(8,128)(2,1)S(1)} %convolution_convert_fusion.3), channel_id=1, source_target_pairs={{0,4},{1,5},{2,6},{3,7},{4,0},{5,1},{6,2},{7,3},{8,12},{9,13},{10,... | collective-permute-start | bytes 786440 | tf_op jit(solution)/shard_map/ppermute | solution.py:251
  59.5 19.6 %collective-permute-start.21 = (bf16[128,2048]{1,0:T(8,128)(2,1)S(1)}, bf16[128,2048]{1,0:T(8,128)(2,1)S(1)}, u32[]{:S(2)}, u32[]{:S(2)}) collective-permute-start(bf16[128,2048]{1,0:T(8,128)(2,1)S(1)} %convolution_convert_fusion.1), channel_id=1, source_target_pairs={{0,4},{1,5},{2,6},{3,7},{4,0},{5,1},{6,2},{7,3},{8,12},{9,13},{10,... | collective-permute-start | bytes 1572872 | tf_op jit(solution)/shard_map/ppermute | solution.py:251
  62.4 42.4 %collective-permute-start.9 = (bf16[64,2048]{1,0:T(8,128)(2,1)S(1)}, bf16[64,2048]{1,0:T(8,128)(2,1)S(1)}, u32[]{:S(2)}, u32[]{:S(2)}) collective-permute-start(bf16[64,2048]{1,0:T(8,128)(2,1)S(1)} %add_convert_fusion.5), channel_id=1, source_target_pairs={{0,16},{1,17},{2,26},{3,27},{4,20},{5,21},{6,30},{7,31},{8,24},{9,... | collective-permute-start | bytes 786440 | tf_op jit(solution)/shard_map/ppermute | solution.py:251
  62.9 3.1 %collective-permute-start.18 = (bf16[128,1024]{1,0:T(8,128)(2,1)S(1)}, bf16[128,1024]{1,0:T(8,128)(2,1)S(1)}, u32[]{:S(2)}, u32[]{:S(2)}) collective-permute-start(bf16[128,1024]{1,0:T(8,128)(2,1)S(1)} %collective-permute-done.17), channel_id=1, source_target_pairs={{0,1},{1,0},{2,3},{3,2},{4,5},{5,4},{6,7},{7,6},{8,9},{9,8},{10,11... | collective-permute-start | bytes 786440 | tf_op jit(solution)/shard_map/ppermute | solution.py:251
  66.0 1.5 %collective-permute-start.16 = (bf16[128,1024]{1,0:T(8,128)(2,1)S(1)}, bf16[128,1024]{1,0:T(8,128)(2,1)S(1)}, u32[]{:S(2)}, u32[]{:S(2)}) collective-permute-start(bf16[128,1024]{1,0:T(8,128)(2,1)S(1)} %collective-permute-done.15), channel_id=1, source_target_pairs={{0,1},{1,0},{2,3},{3,2},{4,5},{5,4},{6,7},{7,6},{8,9},{9,8},{10,11... | collective-permute-start | bytes 786440 | tf_op jit(solution)/shard_map/ppermute | solution.py:251
  66.7 23.6 %collective-permute-start.19 = (bf16[128,2048]{1,0:T(8,128)(2,1)S(1)}, bf16[128,2048]{1,0:T(8,128)(2,1)S(1)}, u32[]{:S(2)}, u32[]{:S(2)}) collective-permute-start(bf16[128,2048]{1,0:T(8,128)(2,1)S(1)} %convolution_convert_fusion.2), channel_id=1, source_target_pairs={{0,4},{1,5},{2,6},{3,7},{4,0},{5,1},{6,2},{7,3},{8,12},{9,13},{10,... | collective-permute-start | bytes 1572872 | tf_op jit(solution)/shard_map/ppermute | solution.py:251
  69.0 31.6 %collective-permute-start.23 = (bf16[128,2048]{1,0:T(8,128)(2,1)S(1)}, bf16[128,2048]{1,0:T(8,128)(2,1)S(1)}, u32[]{:S(2)}, u32[]{:S(2)}) collective-permute-start(bf16[128,2048]{1,0:T(8,128)(2,1)S(1)} %convolution_convert_fusion), channel_id=1, source_target_pairs={{0,4},{1,5},{2,6},{3,7},{4,0},{5,1},{6,2},{7,3},{8,12},{9,13},{10,... | collective-permute-start | bytes 1572872 | tf_op jit(solution)/shard_map/ppermute | solution.py:251
  71.1 54.0 %copy-start.3 = (bf16[128,2048]{1,0:T(8,128)(2,1)S(1)}, bf16[128,2048]{1,0:T(8,128)(2,1)}, u32[]{:S(2)}) copy-start(bf16[128,2048]{1,0:T(8,128)(2,1)} %param.7) | copy-start | bytes 1572868
  79.2 45.8 %collective-permute-start.22 = (bf16[128,2048]{1,0:T(8,128)(2,1)S(1)}, bf16[128,2048]{1,0:T(8,128)(2,1)S(1)}, u32[]{:S(2)}, u32[]{:S(2)}) collective-permute-start(bf16[128,2048]{1,0:T(8,128)(2,1)S(1)} %add_convert_fusion.2), channel_id=1, source_target_pairs={{0,0},{1,1},{2,10},{3,11},{4,4},{5,5},{6,14},{7,15},{8,8},{9,9},{1... | collective-permute-start | bytes 1572872 | tf_op jit(solution)/shard_map/ppermute | solution.py:251
  90.4 34.6 %collective-permute-start.20 = (bf16[128,2048]{1,0:T(8,128)(2,1)S(1)}, bf16[128,2048]{1,0:T(8,128)(2,1)S(1)}, u32[]{:S(2)}, u32[]{:S(2)}) collective-permute-start(bf16[128,2048]{1,0:T(8,128)(2,1)S(1)} %add_convert_fusion.3), channel_id=1, source_target_pairs={{0,24},{1,25},{2,18},{3,19},{4,28},{5,29},{6,22},{7,23},{8,16},{9,... | collective-permute-start | bytes 1572872 | tf_op jit(solution)/shard_map/ppermute | solution.py:251
  100.7 24.3 %collective-permute-start.24 = (bf16[128,2048]{1,0:T(8,128)(2,1)S(1)}, bf16[128,2048]{1,0:T(8,128)(2,1)S(1)}, u32[]{:S(2)}, u32[]{:S(2)}) collective-permute-start(bf16[128,2048]{1,0:T(8,128)(2,1)S(1)} %add_convert_fusion.1), channel_id=1, source_target_pairs={{0,8},{1,9},{2,2},{3,3},{4,12},{5,13},{6,6},{7,7},{8,0},{9,1},{10,... | collective-permute-start | bytes 1572872 | tf_op jit(solution)/shard_map/ppermute | solution.py:251
  103.6 21.4 %collective-permute-start.14 = (bf16[64,2048]{1,0:T(8,128)(2,1)S(1)}, bf16[64,2048]{1,0:T(8,128)(2,1)S(1)}, u32[]{:S(2)}, u32[]{:S(2)}) collective-permute-start(bf16[64,2048]{1,0:T(8,128)(2,1)S(1)} %add_convert_fusion.4), channel_id=1, source_target_pairs={{0,16},{1,17},{2,26},{3,27},{4,20},{5,21},{6,30},{7,31},{8,24},{9,... | collective-permute-start | bytes 786440 | tf_op jit(solution)/shard_map/ppermute | solution.py:251

commit v4 on v3

--- a/solution.py
+++ b/solution.py
@@ -313,20 +313,25 @@
     total = stream_in.astype(F32)
     for group in range(2):
         for slot in range(top):
-            cut = group == 0 and slot == 0
+            cut = group == 1 or slot == 0
             own = [pieces[0, group, slot, 0]]
             if cut:
                 own = lax.optimization_barrier((own[0][:half], own[0][half:]))
             came = []
             for p, mixed in enumerate(own):
                 for j in range(1, lines):
-                    part = moved(pieces[j, group, slot, p], lambda a, b, c: (a, (b - j) % lines, c))
+                    if group:
+                        part = pieces[j, group, slot, 0][p * half : (p + 1) * half]
+                    else:
+                        part = pieces[j, group, slot, p]
+                    part = moved(part, lambda a, b, c: (a, (b - j) % lines, c))
                     mixed = mixed + part.astype(F32)
+                    mixed = mixed.astype(BF16) if j == lines - 1 else mixed
 
                 def target(a, b, c):
                     return a ^ turned[c] ^ (slot + top * (c % 2 == group)), b, c
 
-                came.append(moved(mixed.astype(BF16), target))
+                came.append(moved(mixed, target))
             total = total + (jnp.concatenate(came, axis=0) if cut else came[0]).astype(F32)
     return total.astype(BF16)
 

time: 127 us -> 130 us (1.024)
  starting transfers between devices: 37.2 us -> 45.4 us
  waiting for transfers between devices: 66.4 us -> 59.9 us
    ppermute x21 -> x25, starting transfers between devices: 26.3 us -> 34.4 us  [moved(): lax.ppermute(block, both, [(number(*p), number(*target(*p))) for p in pla...]
    ppermute x21 -> x25, waiting for transfers between devices: 58.7 us -> 52.1 us  [moved(): lax.ppermute(block, both, [(number(*p), number(*target(*p))) for p in pla...]
  transfers between devices with their start and end apart: 25 -> 29, of which waited for: 12 -> 13; matrix products, arithmetic and copies ran while one was open for 8% -> 8% of each run, Pallas kernels for 4% -> 4%
where the time goes in v4:
time: 130 us; the launch traced here: 128 us
  waiting for transfers between devices  59.9 us (46%)
  starting transfers between devices  45.4 us (35%)
  matrix products  8.96 us (7%)
  Pallas kernels  7.04 us (5%)
  local copies, waits for them, and re-layouts  3.6 us (3%)
  other arithmetic  2.89 us (2%)
    ppermute x25, waiting for transfers between devices, moved(): lax.ppermute(block, both, [(number(*p), number(*target(*p))) for p in pla...  52.1 us
    ppermute x25, starting transfers between devices, moved(): lax.ppermute(block, both, [(number(*p), number(*target(*p))) for p in pla...  34.4 us
    dot_general x9, matrix products, product_of(): product = jnp.dot(block, weight, preferred_element_type=F32)  8.96 us
    ppermute x3, waiting for transfers between devices, shards(): other = lax.ppermute(ends, 'seq', [(s, s ^ width) for s in range(seqs)])  7.75 us
    ppermute x3, starting transfers between devices, shards(): other = lax.ppermute(ends, 'seq', [(s, s ^ width) for s in range(seqs)])  6.06 us
    ppermute x1, starting transfers between devices, shards(): lax.ppermute(features[:, tokens - reach:, :], 'seq', [(s, s + 1) for s in...  4.87 us
    pallas_call x2, Pallas kernels, gated_half(): pl.pallas_call(functools.partial(gated_kernel, j, lines, parts), in_specs...  4.8 us
  transfers between devices with their start and end apart: 29, of which 13 were waited for; matrix products, arithmetic and copies ran while one was open for 8% of the time, Pallas kernels for 4%

profile of v4, /device:TPU:0, one launch (start us, length us, event | category | flops | bytes accessed | tf_op | source)
XLA Modules:
  0.0 128.1 jit_solution(2001686602734538215)
XLA Ops:
  0.0 0.9 slice.106
  0.9 4.9 %collective-permute-start = (bf16[3,2,2048]{2,1,0:T(2,128)(2,1)S(1)}, bf16[3,2,2048]{2,1,0:T(2,128)(2,1)S(1)}, u32[]{:S(2)}, u32[]{:S(2)}) collective-permute-start(bf16[3,2,2048]{2,1,0:T(2,128)(2,1)S(1)} %slice.106), channel_id=1, source_target_pairs={{0,4},{4,8},{8,12},{12,16},{16,20},{20,24},{24,28},{1,5},{5,9},{9,... | collective-permute-start | bytes 73736 | tf_op jit(solution)/shard_map/ppermute | solution.py:254
  5.8 0.9 pad_maximum_fusion.small_hbm
  6.7 1.4 %copy-done = bf16[3,128,2048]{2,1,0:T(8,128)(2,1)S(1)} copy-done((bf16[3,128,2048]{2,1,0:T(8,128)(2,1)S(1)}, bf16[3,128,2048]{2,1,0:T(8,128)(2,1)}, u32[]{:S(2)}) %copy-start) | copy-done | bytes 1572888
  8.1 0.9 copy-done.1
  9.0 2.2 %end_states.1 = (f32[8,2048]{1,0:T(8,128)S(1)}, bf16[3,128,2048]{2,1,0:T(8,128)(2,1)S(1)}, f32[3,3,2048]{2,1,0:T(4,128)S(1)}, f32[3,8,2048]{2,1,0:T(8,128)S(1)}) custom-call(bf16[3,128,2048]{2,1,0:T(8,128)(2,1)S(1)} %copy-done, f32[3,3,2048]{2,1,0:T(4,128)S(1)} %copy-done.1, f32[3,8,2048]{2,1,0:T(8,128)S(1)} %pad_maximum_fusion.small_hbm), custom_call_target="tpu_custom_call" | custom-call | flops 8388608 | bytes 1572864 | tf_op jit(solution)/shard_map/end_states/pallas_call | solution.py:198
  11.5 1.6 %collective-permute-start.1 = (f32[8,2048]{1,0:T(8,128)S(1)}, f32[8,2048]{1,0:T(8,128)S(1)}, u32[]{:S(2)}, u32[]{:S(2)}) collective-permute-start(f32[8,2048]{1,0:T(8,128)S(1)} %fusion.29), channel_id=1, source_target_pairs={{0,4},{4,0},{8,12},{12,8},{16,20},{20,16},{24,28},{28,24},{1,5},{5... | collective-permute-start | bytes 196616 | tf_op jit(solution)/shard_map/ppermute | solution.py:264
  13.1 2.7 %collective-permute-done.1 = f32[8,2048]{1,0:T(8,128)S(1)} collective-permute-done((f32[8,2048]{1,0:T(8,128)S(1)}, f32[8,2048]{1,0:T(8,128)S(1)}, u32[]{:S(2)}, u32[]{:S(2)}) %collective-permute-start.1) | collective-permute-done | bytes 65568 | tf_op jit(solution)/shard_map/ppermute | solution.py:264
  15.9 1.6 %collective-permute-start.2 = (f32[8,2048]{1,0:T(8,128)S(1)}, f32[8,2048]{1,0:T(8,128)S(1)}, u32[]{:S(2)}, u32[]{:S(2)}) collective-permute-start(f32[8,2048]{1,0:T(8,128)S(1)} %fusion.31), channel_id=1, source_target_pairs={{0,8},{4,12},{8,0},{12,4},{16,24},{20,28},{24,16},{28,20},{1,9},{5... | collective-permute-start | bytes 196616 | tf_op jit(solution)/shard_map/ppermute | solution.py:264
  17.5 2.7 %collective-permute-done.2 = f32[8,2048]{1,0:T(8,128)S(1)} collective-permute-done((f32[8,2048]{1,0:T(8,128)S(1)}, f32[8,2048]{1,0:T(8,128)S(1)}, u32[]{:S(2)}, u32[]{:S(2)}) %collective-permute-start.2) | collective-permute-done | bytes 65568 | tf_op jit(solution)/shard_map/ppermute | solution.py:264
  20.2 2.8 %collective-permute-start.3 = (f32[8,2048]{1,0:T(8,128)S(1)}, f32[8,2048]{1,0:T(8,128)S(1)}, u32[]{:S(2)}, u32[]{:S(2)}) collective-permute-start(f32[8,2048]{1,0:T(8,128)S(1)} %get-tuple-element.39), channel_id=1, source_target_pairs={{0,16},{4,20},{8,24},{12,28},{16,0},{20,4},{24,8},{28,12},{1,17},{... | collective-permute-start | bytes 196616 | tf_op jit(solution)/shard_map/ppermute | solution.py:264
  23.1 2.4 %collective-permute-done.3.last_ref = f32[8,2048]{1,0:T(8,128)S(1)} collective-permute-done((f32[8,2048]{1,0:T(8,128)S(1)}, f32[8,2048]{1,0:T(8,128)S(1)}, u32[]{:S(2)}, u32[]{:S(2)}) %collective-permute-start.3) | collective-permute-done | bytes 65568 | tf_op jit(solution)/shard_map/ppermute | solution.py:264
  25.5 2.4 %gated_half.3 = (bf16[64,1024]{1,0:T(8,128)(2,1)S(1)}, bf16[64,1024]{1,0:T(8,128)(2,1)S(1)}) custom-call(s32[2]{0:T(128)S(1)} %pad_add_fusion.place_ref, bf16[3,128,2048]{2,1,0:T(8,128)(2,1)S(1)} %get-tuple-element.17.block_ref, bf16[3,2,2048]{2,1,0:T(2,128)(2,1)S(1)} %collective-permute-done.halo_ref, f32[3,3,2048]{2,1,0:T(4,128)S(1)} %get-tuple-element.18.taps_ref, ...), custom_call_target="tpu_custom_call" | custom-call | flops 8388608 | bytes 1048576 | tf_op jit(solution)/shard_map/gated_half/pallas_call | solution.py:217
  27.9 1.6 %collective-permute-start.10 = (bf16[64,1024]{1,0:T(8,128)(2,1)S(1)}, bf16[64,1024]{1,0:T(8,128)(2,1)S(1)}, u32[]{:S(2)}, u32[]{:S(2)}) collective-permute-start(bf16[64,1024]{1,0:T(8,128)(2,1)S(1)} %get-tuple-element.24), channel_id=1, source_target_pairs={{0,2},{1,3},{2,0},{3,1},{4,6},{5,7},{6,4},{7,5},{8,10},{9,11},{10,... | collective-permute-start | bytes 393224 | tf_op jit(solution)/shard_map/ppermute | solution.py:251
  29.5 1.6 %collective-permute-start.6 = (bf16[64,1024]{1,0:T(8,128)(2,1)S(1)}, bf16[64,1024]{1,0:T(8,128)(2,1)S(1)}, u32[]{:S(2)}, u32[]{:S(2)}) collective-permute-start(bf16[64,1024]{1,0:T(8,128)(2,1)S(1)} %get-tuple-element.22), channel_id=1, source_target_pairs={{0,4},{1,14},{2,21},{3,31},{4,0},{5,10},{6,17},{7,27},{8,6},{9,12}... | collective-permute-start | bytes 393224 | tf_op jit(solution)/shard_map/ppermute | solution.py:251
  31.0 1.9 %collective-permute-done.10 = bf16[64,1024]{1,0:T(8,128)(2,1)S(1)} collective-permute-done((bf16[64,1024]{1,0:T(8,128)(2,1)S(1)}, bf16[64,1024]{1,0:T(8,128)(2,1)S(1)}, u32[]{:S(2)}, u32[]{:S(2)}) %collective-permute-start.10) | collective-permute-done | bytes 131104 | tf_op jit(solution)/shard_map/ppermute | solution.py:251
  32.9 2.4 %gated_half.2 = bf16[128,1024]{1,0:T(8,128)(2,1)S(1)} custom-call(s32[2]{0:T(128)S(1)} %pad_add_fusion.place_ref, bf16[3,128,2048]{2,1,0:T(8,128)(2,1)S(1)} %get-tuple-element.17.block_ref, bf16[3,2,2048]{2,1,0:T(2,128)(2,1)S(1)} %collective-permute-done.halo_ref, f32[3,3,2048]{2,1,0:T(4,128)S(1)} %get-tuple-element.18.taps_ref, ...), custom_call_target="tpu_custom_call" | custom-call | flops 8388608 | bytes 1048576 | tf_op jit(solution)/shard_map/gated_half/pallas_call | solution.py:217
  36.0 2.6 %collective-permute-done.6 = bf16[64,1024]{1,0:T(8,128)(2,1)S(1)} collective-permute-done((bf16[64,1024]{1,0:T(8,128)(2,1)S(1)}, bf16[64,1024]{1,0:T(8,128)(2,1)S(1)}, u32[]{:S(2)}, u32[]{:S(2)}) %collective-permute-start.6) | collective-permute-done | bytes 131104 | tf_op jit(solution)/shard_map/ppermute | solution.py:251
  38.6 2.7 %collective-permute-start.7 = (bf16[64,1024]{1,0:T(8,128)(2,1)S(1)}, bf16[64,1024]{1,0:T(8,128)(2,1)S(1)}, u32[]{:S(2)}, u32[]{:S(2)}) collective-permute-start(bf16[64,1024]{1,0:T(8,128)(2,1)S(1)} %collective-permute-done.6), channel_id=1, source_target_pairs={{0,1},{1,0},{2,3},{3,2},{4,5},{5,4},{6,7},{7,6},{8,9},{9,8},{10,11... | collective-permute-start | bytes 393224 | tf_op jit(solution)/shard_map/ppermute | solution.py:251
  41.4 1.6 %collective-permute-done.11 = bf16[64,1024]{1,0:T(8,128)(2,1)S(1)} collective-permute-done((bf16[64,1024]{1,0:T(8,128)(2,1)S(1)}, bf16[64,1024]{1,0:T(8,128)(2,1)S(1)}, u32[]{:S(2)}, u32[]{:S(2)}) %collective-permute-start.11) | collective-permute-done | bytes 131104 | tf_op jit(solution)/shard_map/ppermute | solution.py:251
  43.4 3.0 %convolution_convert_fusion.4 = bf16[64,2048]{1,0:T(8,128)(2,1)S(1)} fusion(bf16[1024,2048]{1,0:T(8,128)(2,1)} %param.13, bf16[64,1024]{1,0:T(8,128)(2,1)S(1)} %collective-permute-done.6, bf16[64,1024]{1,0:T(8,128)(2,1)S(1)} %collective-permute-done.7, pred[]{:T(512)S(6)} %eq.8), kind=kOutput, calls=%fused_computation.4 | convolution fusion | flops 268632064 | bytes 4718593 | tf_op jit(solution)/shard_map/dot_general | solution.py:340
  46.4 2.8 %collective-permute-start.8 = (bf16[64,2048]{1,0:T(8,128)(2,1)S(1)}, bf16[64,2048]{1,0:T(8,128)(2,1)S(1)}, u32[]{:S(2)}, u32[]{:S(2)}) collective-permute-start(bf16[64,2048]{1,0:T(8,128)(2,1)S(1)} %convolution_convert_fusion.4), channel_id=1, source_target_pairs={{0,4},{1,5},{2,6},{3,7},{4,0},{5,1},{6,2},{7,3},{8,12},{9,13},{10,... | collective-permute-start | bytes 786440 | tf_op jit(solution)/shard_map/ppermute | solution.py:251
  49.2 1.9 %collective-permute-start.15 = (bf16[128,1024]{1,0:T(8,128)(2,1)S(1)}, bf16[128,1024]{1,0:T(8,128)(2,1)S(1)}, u32[]{:S(2)}, u32[]{:S(2)}) collective-permute-start(bf16[128,1024]{1,0:T(8,128)(2,1)S(1)} %collective-permute-done.4), channel_id=1, source_target_pairs={{0,2},{1,3},{2,0},{3,1},{4,6},{5,7},{6,4},{7,5},{8,10},{9,11},{10,... | collective-permute-start | bytes 786440 | tf_op jit(solution)/shard_map/ppermute | solution.py:251
  51.2 2.2 %collective-permute-start.5 = (bf16[128,1024]{1,0:T(8,128)(2,1)S(1)}, bf16[128,1024]{1,0:T(8,128)(2,1)S(1)}, u32[]{:S(2)}, u32[]{:S(2)}) collective-permute-start(bf16[128,1024]{1,0:T(8,128)(2,1)S(1)} %collective-permute-done.4), channel_id=1, source_target_pairs={{0,1},{1,0},{2,3},{3,2},{4,5},{5,4},{6,7},{7,6},{8,9},{9,8},{10,11... | collective-permute-start | bytes 786440 | tf_op jit(solution)/shard_map/ppermute | solution.py:251
  53.3 0.8 convolution_convert_fusion.3
  54.2 2.3 %collective-permute-start.13 = (bf16[64,2048]{1,0:T(8,128)(2,1)S(1)}, bf16[64,2048]{1,0:T(8,128)(2,1)S(1)}, u32[]{:S(2)}, u32[]{:S(2)}) collective-permute-start(bf16[64,2048]{1,0:T(8,128)(2,1)S(1)} %convolution_convert_fusion.3), channel_id=1, source_target_pairs={{0,4},{1,5},{2,6},{3,7},{4,0},{5,1},{6,2},{7,3},{8,12},{9,13},{10,... | collective-permute-start | bytes 786440 | tf_op jit(solution)/shard_map/ppermute | solution.py:251
  56.5 0.7 convolution_convert_fusion.1
  57.3 0.7 fusion.10
  58.2 0.7 fusion.5
  59.0 2.1 %collective-permute-start.21 = (bf16[64,2048]{1,0:T(8,128)(2,1)S(1)}, bf16[64,2048]{1,0:T(8,128)(2,1)S(1)}, u32[]{:S(2)}, u32[]{:S(2)}) collective-permute-start(bf16[64,2048]{1,0:T(8,128)(2,1)S(1)} %get-tuple-element.37), channel_id=1, source_target_pairs={{0,4},{1,5},{2,6},{3,7},{4,0},{5,1},{6,2},{7,3},{8,12},{9,13},{10,... | collective-permute-start | bytes 786440 | tf_op jit(solution)/shard_map/ppermute | solution.py:251
  61.1 1.7 %collective-permute-start.9 = (bf16[64,2048]{1,0:T(8,128)(2,1)S(1)}, bf16[64,2048]{1,0:T(8,128)(2,1)S(1)}, u32[]{:S(2)}, u32[]{:S(2)}) collective-permute-start(bf16[64,2048]{1,0:T(8,128)(2,1)S(1)} %add_convert_fusion.7), channel_id=1, source_target_pairs={{0,16},{1,17},{2,26},{3,27},{4,20},{5,21},{6,30},{7,31},{8,24},{9,... | collective-permute-start | bytes 786440 | tf_op jit(solution)/shard_map/ppermute | solution.py:251
  62.9 0.8 collective-permute-done.13
  63.7 5.6 %collective-permute-done.23 = bf16[64,2048]{1,0:T(8,128)(2,1)S(1)} collective-permute-done((bf16[64,2048]{1,0:T(8,128)(2,1)S(1)}, bf16[64,2048]{1,0:T(8,128)(2,1)S(1)}, u32[]{:S(2)}, u32[]{:S(2)}) %collective-permute-start.23) | collective-permute-done | bytes 262176 | tf_op jit(solution)/shard_map/ppermute | solution.py:251
  69.2 1.7 %collective-permute-start.14 = (bf16[64,2048]{1,0:T(8,128)(2,1)S(1)}, bf16[64,2048]{1,0:T(8,128)(2,1)S(1)}, u32[]{:S(2)}, u32[]{:S(2)}) collective-permute-start(bf16[64,2048]{1,0:T(8,128)(2,1)S(1)} %add_convert_fusion.6), channel_id=1, source_target_pairs={{0,16},{1,17},{2,26},{3,27},{4,20},{5,21},{6,30},{7,31},{8,24},{9,... | collective-permute-start | bytes 786440 | tf_op jit(solution)/shard_map/ppermute | solution.py:251
  71.0 3.2 %collective-permute-done.21 = bf16[64,2048]{1,0:T(8,128)(2,1)S(1)} collective-permute-done((bf16[64,2048]{1,0:T(8,128)(2,1)S(1)}, bf16[64,2048]{1,0:T(8,128)(2,1)S(1)}, u32[]{:S(2)}, u32[]{:S(2)}) %collective-permute-start.21) | collective-permute-done | bytes 262176 | tf_op jit(solution)/shard_map/ppermute | solution.py:251
  74.9 0.7 convolution_convert_fusion.2
  75.7 1.8 %collective-permute-start.19 = (bf16[128,2048]{1,0:T(8,128)(2,1)S(1)}, bf16[128,2048]{1,0:T(8,128)(2,1)S(1)}, u32[]{:S(2)}, u32[]{:S(2)}) collective-permute-start(bf16[128,2048]{1,0:T(8,128)(2,1)S(1)} %convolution_convert_fusion.2), channel_id=1, source_target_pairs={{0,4},{1,5},{2,6},{3,7},{4,0},{5,1},{6,2},{7,3},{8,12},{9,13},{10,... | collective-permute-start | bytes 1572872 | tf_op jit(solution)/shard_map/ppermute | solution.py:251
  78.3 0.7 convolution_convert_fusion
  79.4 0.7 fusion.8
  80.2 14.4 %collective-permute-done.27 = bf16[64,2048]{1,0:T(8,128)(2,1)S(1)} collective-permute-done((bf16[64,2048]{1,0:T(8,128)(2,1)S(1)}, bf16[64,2048]{1,0:T(8,128)(2,1)S(1)}, u32[]{:S(2)}, u32[]{:S(2)}) %collective-permute-start.27) | collective-permute-done | bytes 262176 | tf_op jit(solution)/shard_map/ppermute | solution.py:251
  95.4 1.5 %collective-permute-start.25 = (bf16[64,2048]{1,0:T(8,128)(2,1)S(1)}, bf16[64,2048]{1,0:T(8,128)(2,1)S(1)}, u32[]{:S(2)}, u32[]{:S(2)}) collective-permute-start(bf16[64,2048]{1,0:T(8,128)(2,1)S(1)} %get-tuple-element.35), channel_id=1, source_target_pairs={{0,4},{1,5},{2,6},{3,7},{4,0},{5,1},{6,2},{7,3},{8,12},{9,13},{10,... | collective-permute-start | bytes 786440 | tf_op jit(solution)/shard_map/ppermute | solution.py:251
  97.0 5.2 %collective-permute-done.25 = bf16[64,2048]{1,0:T(8,128)(2,1)S(1)} collective-permute-done((bf16[64,2048]{1,0:T(8,128)(2,1)S(1)}, bf16[64,2048]{1,0:T(8,128)(2,1)S(1)}, u32[]{:S(2)}, u32[]{:S(2)}) %collective-permute-start.25) | collective-permute-done | bytes 262176 | tf_op jit(solution)/shard_map/ppermute | solution.py:251
  102.2 1.9 %collective-permute-start.20 = (bf16[128,2048]{1,0:T(8,128)(2,1)S(1)}, bf16[128,2048]{1,0:T(8,128)(2,1)S(1)}, u32[]{:S(2)}, u32[]{:S(2)}) collective-permute-start(bf16[128,2048]{1,0:T(8,128)(2,1)S(1)} %add_convert_fusion.1), channel_id=1, source_target_pairs={{0,24},{1,25},{2,18},{3,19},{4,28},{5,29},{6,22},{7,23},{8,16},{9,... | collective-permute-start | bytes 1572872 | tf_op jit(solution)/shard_map/ppermute | solution.py:251
  104.2 1.9 %collective-permute-start.28 = (bf16[64,2048]{1,0:T(8,128)(2,1)S(1)}, bf16[64,2048]{1,0:T(8,128)(2,1)S(1)}, u32[]{:S(2)}, u32[]{:S(2)}) collective-permute-start(bf16[64,2048]{1,0:T(8,128)(2,1)S(1)} %add_convert_fusion.2), channel_id=1, source_target_pairs={{0,8},{1,9},{2,2},{3,3},{4,12},{5,13},{6,6},{7,7},{8,0},{9,1},{10,... | collective-permute-start | bytes 786440 | tf_op jit(solution)/shard_map/ppermute | solution.py:251
  106.1 3.9 %collective-permute-start.26 = (bf16[64,2048]{1,0:T(8,128)(2,1)S(1)}, bf16[64,2048]{1,0:T(8,128)(2,1)S(1)}, u32[]{:S(2)}, u32[]{:S(2)}) collective-permute-start(bf16[64,2048]{1,0:T(8,128)(2,1)S(1)} %add_convert_fusion.3), channel_id=1, source_target_pairs={{0,8},{1,9},{2,2},{3,3},{4,12},{5,13},{6,6},{7,7},{8,0},{9,1},{10,... | collective-permute-start | bytes 786440 | tf_op jit(solution)/shard_map/ppermute | solution.py:251
  110.1 11.4 %collective-permute-done.28 = bf16[64,2048]{1,0:T(8,128)(2,1)S(1)} collective-permute-done((bf16[64,2048]{1,0:T(8,128)(2,1)S(1)}, bf16[64,2048]{1,0:T(8,128)(2,1)S(1)}, u32[]{:S(2)}, u32[]{:S(2)}) %collective-permute-start.28) | collective-permute-done | bytes 262176 | tf_op jit(solution)/shard_map/ppermute | solution.py:251
  121.4 5.5 %collective-permute-done.26 = bf16[64,2048]{1,0:T(8,128)(2,1)S(1)} collective-permute-done((bf16[64,2048]{1,0:T(8,128)(2,1)S(1)}, bf16[64,2048]{1,0:T(8,128)(2,1)S(1)}, u32[]{:S(2)}, u32[]{:S(2)}) %collective-permute-start.26) | collective-permute-done | bytes 262176 | tf_op jit(solution)/shard_map/ppermute | solution.py:251
  126.9 1.2 add_convert_fusion
  (55 shorter events, 4.7 us)
Async XLA Ops:
  0.9 10.4 %collective-permute-start = (bf16[3,2,2048]{2,1,0:T(2,128)(2,1)S(1)}, bf16[3,2,2048]{2,1,0:T(2,128)(2,1)S(1)}, u32[]{:S(2)}, u32[]{:S(2)}) collective-permute-start(bf16[3,2,2048]{2,1,0:T(2,128)(2,1)S(1)} %slice.106), channel_id=1, source_target_pairs={{0,4},{4,8},{8,12},{12,16},{16,20},{20,24},{24,28},{1,5},{5,9},{9,... | collective-permute-start | bytes 73736 | tf_op jit(solution)/shard_map/ppermute | solution.py:254
  6.7 1.4 %copy-start = (bf16[3,128,2048]{2,1,0:T(8,128)(2,1)S(1)}, bf16[3,128,2048]{2,1,0:T(8,128)(2,1)}, u32[]{:S(2)}) copy-start(bf16[3,128,2048]{2,1,0:T(8,128)(2,1)} %block_hbm.1) | copy-start | bytes 4718596
  8.1 0.9 copy-start.1
  11.5 4.3 %collective-permute-start.1 = (f32[8,2048]{1,0:T(8,128)S(1)}, f32[8,2048]{1,0:T(8,128)S(1)}, u32[]{:S(2)}, u32[]{:S(2)}) collective-permute-start(f32[8,2048]{1,0:T(8,128)S(1)} %fusion.29), channel_id=1, source_target_pairs={{0,4},{4,0},{8,12},{12,8},{16,20},{20,16},{24,28},{28,24},{1,5},{5... | collective-permute-start | bytes 196616 | tf_op jit(solution)/shard_map/ppermute | solution.py:264
  15.9 4.3 %collective-permute-start.2 = (f32[8,2048]{1,0:T(8,128)S(1)}, f32[8,2048]{1,0:T(8,128)S(1)}, u32[]{:S(2)}, u32[]{:S(2)}) collective-permute-start(f32[8,2048]{1,0:T(8,128)S(1)} %fusion.31), channel_id=1, source_target_pairs={{0,8},{4,12},{8,0},{12,4},{16,24},{20,28},{24,16},{28,20},{1,9},{5... | collective-permute-start | bytes 196616 | tf_op jit(solution)/shard_map/ppermute | solution.py:264
  20.2 5.2 %collective-permute-start.3 = (f32[8,2048]{1,0:T(8,128)S(1)}, f32[8,2048]{1,0:T(8,128)S(1)}, u32[]{:S(2)}, u32[]{:S(2)}) collective-permute-start(f32[8,2048]{1,0:T(8,128)S(1)} %get-tuple-element.39), channel_id=1, source_target_pairs={{0,16},{4,20},{8,24},{12,28},{16,0},{20,4},{24,8},{28,12},{1,17},{... | collective-permute-start | bytes 196616 | tf_op jit(solution)/shard_map/ppermute | solution.py:264
  27.9 5.0 %collective-permute-start.10 = (bf16[64,1024]{1,0:T(8,128)(2,1)S(1)}, bf16[64,1024]{1,0:T(8,128)(2,1)S(1)}, u32[]{:S(2)}, u32[]{:S(2)}) collective-permute-start(bf16[64,1024]{1,0:T(8,128)(2,1)S(1)} %get-tuple-element.24), channel_id=1, source_target_pairs={{0,2},{1,3},{2,0},{3,1},{4,6},{5,7},{6,4},{7,5},{8,10},{9,11},{10,... | collective-permute-start | bytes 393224 | tf_op jit(solution)/shard_map/ppermute | solution.py:251
  29.5 9.2 %collective-permute-start.6 = (bf16[64,1024]{1,0:T(8,128)(2,1)S(1)}, bf16[64,1024]{1,0:T(8,128)(2,1)S(1)}, u32[]{:S(2)}, u32[]{:S(2)}) collective-permute-start(bf16[64,1024]{1,0:T(8,128)(2,1)S(1)} %get-tuple-element.22), channel_id=1, source_target_pairs={{0,4},{1,14},{2,21},{3,31},{4,0},{5,10},{6,17},{7,27},{8,6},{9,12}... | collective-permute-start | bytes 393224 | tf_op jit(solution)/shard_map/ppermute | solution.py:251
  32.9 10.1 %collective-permute-start.11 = (bf16[64,1024]{1,0:T(8,128)(2,1)S(1)}, bf16[64,1024]{1,0:T(8,128)(2,1)S(1)}, u32[]{:S(2)}, u32[]{:S(2)}) collective-permute-start(bf16[64,1024]{1,0:T(8,128)(2,1)S(1)} %collective-permute-done.10), channel_id=1, source_target_pairs={{0,21},{1,31},{2,4},{3,14},{4,17},{5,27},{6,0},{7,10},{8,23},{9,29... | collective-permute-start | bytes 393224 | tf_op jit(solution)/shard_map/ppermute | solution.py:251
  32.9 20.4 %copy-start.2 = (bf16[1024,2048]{1,0:T(8,128)(2,1)S(1)}, bf16[1024,2048]{1,0:T(8,128)(2,1)}, u32[]{:S(2)}) copy-start(bf16[1024,2048]{1,0:T(8,128)(2,1)} %param.13) | copy-start | bytes 12582916
  35.3 13.9 %collective-permute-start.4 = (bf16[128,1024]{1,0:T(8,128)(2,1)S(1)}, bf16[128,1024]{1,0:T(8,128)(2,1)S(1)}, u32[]{:S(2)}, u32[]{:S(2)}) collective-permute-start(bf16[128,1024]{1,0:T(8,128)(2,1)S(1)} %gated_half.2), channel_id=1, source_target_pairs={{0,0},{1,10},{2,17},{3,27},{4,4},{5,14},{6,21},{7,31},{8,2},{9,8},... | collective-permute-start | bytes 786440 | tf_op jit(solution)/shard_map/ppermute | solution.py:251
  38.6 4.8 %collective-permute-start.7 = (bf16[64,1024]{1,0:T(8,128)(2,1)S(1)}, bf16[64,1024]{1,0:T(8,128)(2,1)S(1)}, u32[]{:S(2)}, u32[]{:S(2)}) collective-permute-start(bf16[64,1024]{1,0:T(8,128)(2,1)S(1)} %collective-permute-done.6), channel_id=1, source_target_pairs={{0,1},{1,0},{2,3},{3,2},{4,5},{5,4},{6,7},{7,6},{8,9},{9,8},{10,11... | collective-permute-start | bytes 393224 | tf_op jit(solution)/shard_map/ppermute | solution.py:251
  43.0 19.9 %collective-permute-start.17 = (bf16[128,1024]{1,0:T(8,128)(2,1)S(1)}, bf16[128,1024]{1,0:T(8,128)(2,1)S(1)}, u32[]{:S(2)}, u32[]{:S(2)}) collective-permute-start(bf16[128,1024]{1,0:T(8,128)(2,1)S(1)} %constant_dynamic-update-slice_fusion), channel_id=1, source_target_pairs={{0,2},{1,3},{2,0},{3,1},{4,6},{5,7},{6,4},{7,5},{8,10},{9,11},{10,... | collective-permute-start | bytes 786440 | tf_op jit(solution)/shard_map/ppermute | solution.py:251
  43.3 10.0 %collective-permute-start.12 = (bf16[64,1024]{1,0:T(8,128)(2,1)S(1)}, bf16[64,1024]{1,0:T(8,128)(2,1)S(1)}, u32[]{:S(2)}, u32[]{:S(2)}) collective-permute-start(bf16[64,1024]{1,0:T(8,128)(2,1)S(1)} %collective-permute-done.11), channel_id=1, source_target_pairs={{0,1},{1,0},{2,3},{3,2},{4,5},{5,4},{6,7},{7,6},{8,9},{9,8},{10,11... | collective-permute-start | bytes 393224 | tf_op jit(solution)/shard_map/ppermute | solution.py:251
  46.4 12.6 %collective-permute-start.8 = (bf16[64,2048]{1,0:T(8,128)(2,1)S(1)}, bf16[64,2048]{1,0:T(8,128)(2,1)S(1)}, u32[]{:S(2)}, u32[]{:S(2)}) collective-permute-start(bf16[64,2048]{1,0:T(8,128)(2,1)S(1)} %convolution_convert_fusion.4), channel_id=1, source_target_pairs={{0,4},{1,5},{2,6},{3,7},{4,0},{5,1},{6,2},{7,3},{8,12},{9,13},{10,... | collective-permute-start | bytes 786440 | tf_op jit(solution)/shard_map/ppermute | solution.py:251
  49.2 11.9 %collective-permute-start.15 = (bf16[128,1024]{1,0:T(8,128)(2,1)S(1)}, bf16[128,1024]{1,0:T(8,128)(2,1)S(1)}, u32[]{:S(2)}, u32[]{:S(2)}) collective-permute-start(bf16[128,1024]{1,0:T(8,128)(2,1)S(1)} %collective-permute-done.4), channel_id=1, source_target_pairs={{0,2},{1,3},{2,0},{3,1},{4,6},{5,7},{6,4},{7,5},{8,10},{9,11},{10,... | collective-permute-start | bytes 786440 | tf_op jit(solution)/shard_map/ppermute | solution.py:251
  51.2 6.1 %collective-permute-start.5 = (bf16[128,1024]{1,0:T(8,128)(2,1)S(1)}, bf16[128,1024]{1,0:T(8,128)(2,1)S(1)}, u32[]{:S(2)}, u32[]{:S(2)}) collective-permute-start(bf16[128,1024]{1,0:T(8,128)(2,1)S(1)} %collective-permute-done.4), channel_id=1, source_target_pairs={{0,1},{1,0},{2,3},{3,2},{4,5},{5,4},{6,7},{7,6},{8,9},{9,8},{10,11... | collective-permute-start | bytes 786440 | tf_op jit(solution)/shard_map/ppermute | solution.py:251
  54.2 9.4 %collective-permute-start.13 = (bf16[64,2048]{1,0:T(8,128)(2,1)S(1)}, bf16[64,2048]{1,0:T(8,128)(2,1)S(1)}, u32[]{:S(2)}, u32[]{:S(2)}) collective-permute-start(bf16[64,2048]{1,0:T(8,128)(2,1)S(1)} %convolution_convert_fusion.3), channel_id=1, source_target_pairs={{0,4},{1,5},{2,6},{3,7},{4,0},{5,1},{6,2},{7,3},{8,12},{9,13},{10,... | collective-permute-start | bytes 786440 | tf_op jit(solution)/shard_map/ppermute | solution.py:251
  57.3 12.0 %collective-permute-start.23 = (bf16[64,2048]{1,0:T(8,128)(2,1)S(1)}, bf16[64,2048]{1,0:T(8,128)(2,1)S(1)}, u32[]{:S(2)}, u32[]{:S(2)}) collective-permute-start(bf16[64,2048]{1,0:T(8,128)(2,1)S(1)} %get-tuple-element.38), channel_id=1, source_target_pairs={{0,4},{1,5},{2,6},{3,7},{4,0},{5,1},{6,2},{7,3},{8,12},{9,13},{10,... | collective-permute-start | bytes 786440 | tf_op jit(solution)/shard_map/ppermute | solution.py:251
  59.0 15.2 %collective-permute-start.21 = (bf16[64,2048]{1,0:T(8,128)(2,1)S(1)}, bf16[64,2048]{1,0:T(8,128)(2,1)S(1)}, u32[]{:S(2)}, u32[]{:S(2)}) collective-permute-start(bf16[64,2048]{1,0:T(8,128)(2,1)S(1)} %get-tuple-element.37), channel_id=1, source_target_pairs={{0,4},{1,5},{2,6},{3,7},{4,0},{5,1},{6,2},{7,3},{8,12},{9,13},{10,... | collective-permute-start | bytes 786440 | tf_op jit(solution)/shard_map/ppermute | solution.py:251
  61.1 43.0 %collective-permute-start.9 = (bf16[64,2048]{1,0:T(8,128)(2,1)S(1)}, bf16[64,2048]{1,0:T(8,128)(2,1)S(1)}, u32[]{:S(2)}, u32[]{:S(2)}) collective-permute-start(bf16[64,2048]{1,0:T(8,128)(2,1)S(1)} %add_convert_fusion.7), channel_id=1, source_target_pairs={{0,16},{1,17},{2,26},{3,27},{4,20},{5,21},{6,30},{7,31},{8,24},{9,... | collective-permute-start | bytes 786440 | tf_op jit(solution)/shard_map/ppermute | solution.py:251
  62.9 14.6 %collective-permute-start.16 = (bf16[128,1024]{1,0:T(8,128)(2,1)S(1)}, bf16[128,1024]{1,0:T(8,128)(2,1)S(1)}, u32[]{:S(2)}, u32[]{:S(2)}) collective-permute-start(bf16[128,1024]{1,0:T(8,128)(2,1)S(1)} %collective-permute-done.15), channel_id=1, source_target_pairs={{0,1},{1,0},{2,3},{3,2},{4,5},{5,4},{6,7},{7,6},{8,9},{9,8},{10,11... | collective-permute-start | bytes 786440 | tf_op jit(solution)/shard_map/ppermute | solution.py:251
  63.6 11.3 %collective-permute-start.18 = (bf16[128,1024]{1,0:T(8,128)(2,1)S(1)}, bf16[128,1024]{1,0:T(8,128)(2,1)S(1)}, u32[]{:S(2)}, u32[]{:S(2)}) collective-permute-start(bf16[128,1024]{1,0:T(8,128)(2,1)S(1)} %collective-permute-done.17), channel_id=1, source_target_pairs={{0,1},{1,0},{2,3},{3,2},{4,5},{5,4},{6,7},{7,6},{8,9},{9,8},{10,11... | collective-permute-start | bytes 786440 | tf_op jit(solution)/shard_map/ppermute | solution.py:251
  69.2 36.9 %collective-permute-start.14 = (bf16[64,2048]{1,0:T(8,128)(2,1)S(1)}, bf16[64,2048]{1,0:T(8,128)(2,1)S(1)}, u32[]{:S(2)}, u32[]{:S(2)}) collective-permute-start(bf16[64,2048]{1,0:T(8,128)(2,1)S(1)} %add_convert_fusion.6), channel_id=1, source_target_pairs={{0,16},{1,17},{2,26},{3,27},{4,20},{5,21},{6,30},{7,31},{8,24},{9,... | collective-permute-start | bytes 786440 | tf_op jit(solution)/shard_map/ppermute | solution.py:251
  74.2 35.9 %collective-permute-start.24 = (bf16[64,2048]{1,0:T(8,128)(2,1)S(1)}, bf16[64,2048]{1,0:T(8,128)(2,1)S(1)}, u32[]{:S(2)}, u32[]{:S(2)}) collective-permute-start(bf16[64,2048]{1,0:T(8,128)(2,1)S(1)} %add_convert_fusion.4), channel_id=1, source_target_pairs={{0,0},{1,1},{2,10},{3,11},{4,4},{5,5},{6,14},{7,15},{8,8},{9,9},{1... | collective-permute-start | bytes 786440 | tf_op jit(solution)/shard_map/ppermute | solution.py:251
  75.7 19.7 %collective-permute-start.19 = (bf16[128,2048]{1,0:T(8,128)(2,1)S(1)}, bf16[128,2048]{1,0:T(8,128)(2,1)S(1)}, u32[]{:S(2)}, u32[]{:S(2)}) collective-permute-start(bf16[128,2048]{1,0:T(8,128)(2,1)S(1)} %convolution_convert_fusion.2), channel_id=1, source_target_pairs={{0,4},{1,5},{2,6},{3,7},{4,0},{5,1},{6,2},{7,3},{8,12},{9,13},{10,... | collective-permute-start | bytes 1572872 | tf_op jit(solution)/shard_map/ppermute | solution.py:251
  79.1 47.8 %copy-start.3 = (bf16[128,2048]{1,0:T(8,128)(2,1)S(1)}, bf16[128,2048]{1,0:T(8,128)(2,1)}, u32[]{:S(2)}) copy-start(bf16[128,2048]{1,0:T(8,128)(2,1)} %param.7) | copy-start | bytes 1572868
  79.1 15.5 %collective-permute-start.27 = (bf16[64,2048]{1,0:T(8,128)(2,1)S(1)}, bf16[64,2048]{1,0:T(8,128)(2,1)S(1)}, u32[]{:S(2)}, u32[]{:S(2)}) collective-permute-start(bf16[64,2048]{1,0:T(8,128)(2,1)S(1)} %get-tuple-element.36), channel_id=1, source_target_pairs={{0,4},{1,5},{2,6},{3,7},{4,0},{5,1},{6,2},{7,3},{8,12},{9,13},{10,... | collective-permute-start | bytes 786440 | tf_op jit(solution)/shard_map/ppermute | solution.py:251
  94.6 15.4 %collective-permute-start.22 = (bf16[64,2048]{1,0:T(8,128)(2,1)S(1)}, bf16[64,2048]{1,0:T(8,128)(2,1)S(1)}, u32[]{:S(2)}, u32[]{:S(2)}) collective-permute-start(bf16[64,2048]{1,0:T(8,128)(2,1)S(1)} %add_convert_fusion.5), channel_id=1, source_target_pairs={{0,0},{1,1},{2,10},{3,11},{4,4},{5,5},{6,14},{7,15},{8,8},{9,9},{1... | collective-permute-start | bytes 786440 | tf_op jit(solution)/shard_map/ppermute | solution.py:251
  95.4 6.9 %collective-permute-start.25 = (bf16[64,2048]{1,0:T(8,128)(2,1)S(1)}, bf16[64,2048]{1,0:T(8,128)(2,1)S(1)}, u32[]{:S(2)}, u32[]{:S(2)}) collective-permute-start(bf16[64,2048]{1,0:T(8,128)(2,1)S(1)} %get-tuple-element.35), channel_id=1, source_target_pairs={{0,4},{1,5},{2,6},{3,7},{4,0},{5,1},{6,2},{7,3},{8,12},{9,13},{10,... | collective-permute-start | bytes 786440 | tf_op jit(solution)/shard_map/ppermute | solution.py:251
  102.2 24.7 %collective-permute-start.20 = (bf16[128,2048]{1,0:T(8,128)(2,1)S(1)}, bf16[128,2048]{1,0:T(8,128)(2,1)S(1)}, u32[]{:S(2)}, u32[]{:S(2)}) collective-permute-start(bf16[128,2048]{1,0:T(8,128)(2,1)S(1)} %add_convert_fusion.1), channel_id=1, source_target_pairs={{0,24},{1,25},{2,18},{3,19},{4,28},{5,29},{6,22},{7,23},{8,16},{9,... | collective-permute-start | bytes 1572872 | tf_op jit(solution)/shard_map/ppermute | solution.py:251
  104.2 17.2 %collective-permute-start.28 = (bf16[64,2048]{1,0:T(8,128)(2,1)S(1)}, bf16[64,2048]{1,0:T(8,128)(2,1)S(1)}, u32[]{:S(2)}, u32[]{:S(2)}) collective-permute-start(bf16[64,2048]{1,0:T(8,128)(2,1)S(1)} %add_convert_fusion.2), channel_id=1, source_target_pairs={{0,8},{1,9},{2,2},{3,3},{4,12},{5,13},{6,6},{7,7},{8,0},{9,1},{10,... | collective-permute-start | bytes 786440 | tf_op jit(solution)/shard_map/ppermute | solution.py:251
  106.1 20.8 %collective-permute-start.26 = (bf16[64,2048]{1,0:T(8,128)(2,1)S(1)}, bf16[64,2048]{1,0:T(8,128)(2,1)S(1)}, u32[]{:S(2)}, u32[]{:S(2)}) collective-permute-start(bf16[64,2048]{1,0:T(8,128)(2,1)S(1)} %add_convert_fusion.3), channel_id=1, source_target_pairs={{0,8},{1,9},{2,2},{3,3},{4,12},{5,13},{6,6},{7,7},{8,0},{9,1},{10,... | collective-permute-start | bytes 786440 | tf_op jit(solution)/shard_map/ppermute | solution.py:251

commit v5 on v4

--- a/solution.py
+++ b/solution.py
@@ -122,35 +122,26 @@
         copy.wait()
 
 
-def gated_kernel(
-    j, lines, parts, place_ref, block_ref, halo_ref, taps_ref, small_ref, prefix_ref, last_ref, *refs
+def local_kernel(
+    block_ref, halo_ref, taps_ref, small_ref, product_ref, query_ref, scan_ref, qb, kb, vb
 ):
-    *out_refs, qb, kb, vb, pb, ob = refs[len(refs) - parts - 5 :]
-    tokens, share = block_ref.shape[1], out_refs[0].shape[1]
-    poles = prefix_ref.shape[0]
-    decay_ref, residues_ref, carried_ref = (small_ref.at[i] for i in range(3))
-    steps = tokens // SUBLANES
-    first = lax.rem(place_ref[0] + j, lines) * share
-    since_start = (place_ref[0] * tokens).astype(F32)
-    since_last = (place_ref[1] * tokens).astype(F32)
-    upper = place_ref[1] != place_ref[0]
+    steps = product_ref.shape[1]
+    poles = scan_ref.shape[1]
     place = lax.broadcasted_iota(jnp.int32, (SUBLANES, LANES), 0)
-    before = (place * steps).astype(F32)
 
     def body(which, plane):
-        lanes = lanes_at(plane, first)
+        lanes = lanes_at(plane)
         key = Convolved(block_ref, halo_ref, taps_ref, 1, lanes, kb.at[which])
         value = Convolved(block_ref, halo_ref, taps_ref, 2, lanes, vb.at[which])
-        rates = decay_ref[:, lanes]
+        query = Convolved(block_ref, halo_ref, taps_ref, 0, lanes, qb.at[which])
+        rates = small_ref[0, :, lanes]
         every = jnp.exp(-rates)
-        state = jnp.exp(-rates * since_start) * carried_ref[:, lanes] + prefix_ref[:, lanes]
-        last = jnp.exp(-rates * since_last) * last_ref[:, lanes]
-        state = state + jnp.where(upper, last, 0.0)
         fades = [spread(every[r : r + 1]) for r in range(poles)]
         sums = None
         for j in range(steps):
             product = key(j) * value(j)
-            pb[which, j] = product
+            product_ref[plane, j] = product
+            query_ref[plane, j] = query(j)
             if sums is None:
                 sums = [product] * poles
             else:
@@ -163,12 +154,43 @@
                 moved = jnp.where(place >= reach, pltpu.roll(scan, reach, 0), 0.0)
                 scan = scan + jnp.exp(-rate * float(reach * steps)) * moved
                 reach *= 2
-            earlier = jnp.where(place >= 1, pltpu.roll(scan, 1, 0), 0.0)
-            sums[r] = earlier + jnp.exp(-rate * before) * spread(state[r : r + 1])
-        query = Convolved(block_ref, halo_ref, taps_ref, 0, lanes, qb.at[which])
+            scan_ref[plane, r] = jnp.where(place >= 1, pltpu.roll(scan, 1, 0), 0.0)
+
+    over_planes(block_ref.shape[2], kb.shape[0], body)
+
+
+def gated_kernel(
+    j, lines, place_ref, product_ref, query_ref, scan_ref, small_ref, prefix_ref, last_ref,
+    *refs,
+):
+    *out_refs, ob = refs
+    steps = product_ref.shape[1]
+    tokens, share = steps * SUBLANES, out_refs[0].shape[1]
+    poles = prefix_ref.shape[0]
+    decay_ref, residues_ref, carried_ref = (small_ref.at[i] for i in range(3))
+    half = lax.rem(place_ref[0] + j, lines)
+    since_start = (place_ref[0] * tokens).astype(F32)
+    since_last = (place_ref[1] * tokens).astype(F32)
+    upper = place_ref[1] != place_ref[0]
+    place = lax.broadcasted_iota(jnp.int32, (SUBLANES, LANES), 0)
+    before = (place * steps).astype(F32)
+
+    def body(which, plane):
+        lanes = lanes_at(plane, half * share)
+        held = half * (share // LANES) + plane
+        rates = decay_ref[:, lanes]
+        every = jnp.exp(-rates)
+        state = jnp.exp(-rates * since_start) * carried_ref[:, lanes] + prefix_ref[:, lanes]
+        last = jnp.exp(-rates * since_last) * last_ref[:, lanes]
+        state = state + jnp.where(upper, last, 0.0)
+        fades = [spread(every[r : r + 1]) for r in range(poles)]
+        sums = []
+        for r in range(poles):
+            within = jnp.exp(-spread(rates[r : r + 1]) * before)
+            sums.append(scan_ref[held, r] + within * spread(state[r : r + 1]))
         weights = [spread(residues_ref[r : r + 1, lanes]) for r in range(poles)]
         for j in range(steps):
-            product = pb[which, j]
+            product = product_ref[held, j]
             if j:
                 sums = [fades[r] * sums[r] + product for r in range(poles)]
             else:
@@ -176,13 +198,13 @@
             terms = [weights[r] * sums[r] for r in range(poles)]
             while len(terms) > 1:
                 terms = [a + b for a, b in zip(terms[::2], terms[1::2])] + terms[len(terms) & ~1 :]
-            ob[which, pl.ds(j, SUBLANES, stride=steps), :] = query(j) * terms[0]
+            ob[which, pl.ds(j, SUBLANES, stride=steps), :] = query_ref[held, j] * terms[0]
         for i, out_ref in enumerate(out_refs):
             rows = out_ref.shape[0]
             part = ob[which, i * rows : (i + 1) * rows]
             out_ref[:, lanes_at(plane)] = part.astype(out_ref.dtype)
 
-    over_planes(share, kb.shape[0], body)
+    over_planes(share, ob.shape[0], body)
 
 
 VMEM = pl.BlockSpec(memory_space=pltpu.VMEM)
@@ -211,26 +233,40 @@
     )(*arrays)
 
 
-def gated_half(j, lines, parts, place, share, arrays, states, brought=()):
-    tokens, poles = arrays[0].shape[1], states[0].shape[0]
-    shapes = [jax.ShapeDtypeStruct((tokens // parts, share), BF16)] * parts
+def local_parts(features, halo, taps, small):
+    _, tokens, count = features.shape
+    poles = small.shape[1]
+    rows = (count // LANES, tokens // SUBLANES, SUBLANES, LANES)
+    scans = (count // LANES, poles, SUBLANES, LANES)
     return pl.pallas_call(
-        functools.partial(gated_kernel, j, lines, parts),
-        in_specs=[SMEM]
-        + [VMEM] * (len(arrays) + len(states) + len(brought)),
-        out_specs=[VMEM] * len(shapes),
-        out_shape=shapes,
-        scratch_shapes=[pltpu.VMEM((TOGETHER, PAD + tokens, LANES), F32)] * 3
-        + [
-            pltpu.VMEM((TOGETHER, tokens // SUBLANES, SUBLANES, LANES), F32),
-            pltpu.VMEM((TOGETHER, tokens, LANES), F32),
-        ],
+        local_kernel,
+        in_specs=[VMEM] * 4,
+        out_specs=[VMEM] * 3,
+        out_shape=[jax.ShapeDtypeStruct(shape, F32) for shape in (rows, rows, scans)],
+        scratch_shapes=[pltpu.VMEM((TOGETHER, PAD + tokens, LANES), F32)] * 3,
         compiler_params=ROOM,
         cost_estimate=pl.CostEstimate(
-            flops=8 * poles * tokens * share, bytes_accessed=8 * tokens * share, transcendentals=0
+            flops=4 * poles * tokens * count, bytes_accessed=8 * tokens * count, transcendentals=0
+        ),
+        name="local_parts",
+    )(features, halo, taps, small)
+
+
+def gated_half(j, lines, parts, place, share, arrays, states):
+    tokens = arrays[0].shape[1] * SUBLANES
+    poles = states[0].shape[0]
+    return pl.pallas_call(
+        functools.partial(gated_kernel, j, lines),
+        in_specs=[SMEM] + [VMEM] * (len(arrays) + len(states)),
+        out_specs=[VMEM] * parts,
+        out_shape=[jax.ShapeDtypeStruct((tokens // parts, share), BF16)] * parts,
+        scratch_shapes=[pltpu.VMEM((TOGETHER, tokens, LANES), F32)],
+        compiler_params=ROOM,
+        cost_estimate=pl.CostEstimate(
+            flops=4 * poles * tokens * share, bytes_accessed=8 * tokens * share, transcendentals=0
         ),
         name="gated_half",
-    )(place, *arrays, *states, *brought)
+    )(place, *arrays, *states)
 
 
 def shards(stream_in, features, conv_taps, decay, residues, state_in, out_weight):
@@ -257,6 +293,7 @@
     small = jnp.stack([decay.T, residues.T, state_in.T])
     ends, features, conv_taps, small = end_states(features, conv_taps, small)
     rates = small[0]
+    parts = local_parts(features, halo, conv_taps, small)
     ends = ends + first_tokens(features[1:, :reach], halo[1:], conv_taps[1:], rates, tokens)
     prefix = jnp.zeros_like(ends)
     width = 1
@@ -277,8 +314,7 @@
     blocks = {}
     for j in order:
         results = gated_half(
-            j, lines, 2 if j else 1, place, share, (features, halo, conv_taps, small),
-            (prefix, other), [],
+            j, lines, 2 if j else 1, place, share, (*parts, small), (prefix, other),
         )
         blocks[j] = [moved(results[0], lambda a, b, c: (c, (b + j) % lines, turned[a ^ c]))]
         if j:

time: 130 us -> 130 us (level)
  local copies, waits for them, and re-layouts: 3.6 us -> 6.17 us
  starting transfers between devices: 45.4 us -> 42.9 us
    unnamed x9 -> x13, local copies, waits for them, and re-layouts: 2.31 us -> 4.88 us
    ppermute x25, starting transfers between devices: 34.4 us -> 32 us  [moved(): lax.ppermute(block, both, [(number(*p), number(*target(*p))) for p in pla...]
    ppermute x3, waiting for transfers between devices: 7.75 us -> 5.4 us  [shards(): other = lax.ppermute(ends, 'seq', [(s, s ^ width) for s in range(seqs)])]
    ppermute x25, waiting for transfers between devices: 52.1 us -> 54 us  [moved(): lax.ppermute(block, both, [(number(*p), number(*target(*p))) for p in pla...]
    pallas_call x2 -> x3, Pallas kernels: 4.8 us -> 5.01 us  [the longest x2 2.61 us: gated_half(): pl.pallas_call(functools.partial(gated_kernel, j, lines), in_specs=[SMEM]...]
  transfers between devices with their start and end apart: 29 -> 29, of which waited for: 13 -> 13; matrix products, arithmetic and copies ran while one was open for 8% -> 8% of each run, Pallas kernels for 4% -> 5%
where the time goes in v5:
time: 130 us; the launch traced here: 128 us
  waiting for transfers between devices  59.4 us (46%)
  starting transfers between devices  42.9 us (33%)
  matrix products  8.96 us (7%)
  Pallas kernels  7.28 us (6%)
  local copies, waits for them, and re-layouts  6.17 us (5%)
  other arithmetic  2.89 us (2%)
    ppermute x25, waiting for transfers between devices, moved(): lax.ppermute(block, both, [(number(*p), number(*target(*p))) for p in pla...  54 us
    ppermute x25, starting transfers between devices, moved(): lax.ppermute(block, both, [(number(*p), number(*target(*p))) for p in pla...  32 us
    dot_general x9, matrix products, product_of(): product = jnp.dot(block, weight, preferred_element_type=F32)  8.96 us
    ppermute x3, starting transfers between devices, shards(): other = lax.ppermute(ends, 'seq', [(s, s ^ width) for s in range(seqs)])  6.06 us
    ppermute x3, waiting for transfers between devices, shards(): other = lax.ppermute(ends, 'seq', [(s, s ^ width) for s in range(seqs)])  5.4 us
    unnamed x13, local copies, waits for them, and re-layouts  4.88 us
    ppermute x1, starting transfers between devices, shards(): lax.ppermute(features[:, tokens - reach:, :], 'seq', [(s, s + 1) for s in...  4.87 us
    pallas_call x2, Pallas kernels, gated_half(): pl.pallas_call(functools.partial(gated_kernel, j, lines), in_specs=[SMEM]...  2.61 us
  transfers between devices with their start and end apart: 29, of which 13 were waited for; matrix products, arithmetic and copies ran while one was open for 8% of the time, Pallas kernels for 5%

profile of v5, /device:TPU:0, one launch (start us, length us, event | category | flops | bytes accessed | tf_op | source)
XLA Modules:
  0.0 128.0 jit_solution(1737170675573859422)
XLA Ops:
  0.0 0.9 slice.106
  0.9 4.9 %collective-permute-start = (bf16[3,2,2048]{2,1,0:T(2,128)(2,1)S(1)}, bf16[3,2,2048]{2,1,0:T(2,128)(2,1)S(1)}, u32[]{:S(2)}, u32[]{:S(2)}) collective-permute-start(bf16[3,2,2048]{2,1,0:T(2,128)(2,1)S(1)} %slice.106), channel_id=1, source_target_pairs={{0,4},{4,8},{8,12},{12,16},{16,20},{20,24},{24,28},{1,5},{5,9},{9,... | collective-permute-start | bytes 73736 | tf_op jit(solution)/shard_map/ppermute | solution.py:290
  5.8 0.9 pad_maximum_fusion.small_hbm
  6.7 1.4 %copy-done = bf16[3,128,2048]{2,1,0:T(8,128)(2,1)S(1)} copy-done((bf16[3,128,2048]{2,1,0:T(8,128)(2,1)S(1)}, bf16[3,128,2048]{2,1,0:T(8,128)(2,1)}, u32[]{:S(2)}) %copy-start) | copy-done | bytes 1572888
  8.1 0.9 copy-done.3
  9.0 2.3 %end_states.1 = (f32[8,2048]{1,0:T(8,128)S(1)}, bf16[3,128,2048]{2,1,0:T(8,128)(2,1)S(1)}, f32[3,3,2048]{2,1,0:T(4,128)S(1)}, f32[3,8,2048]{2,1,0:T(8,128)S(1)}) custom-call(bf16[3,128,2048]{2,1,0:T(8,128)(2,1)S(1)} %copy-done, f32[3,3,2048]{2,1,0:T(4,128)S(1)} %copy-done.3, f32[3,8,2048]{2,1,0:T(8,128)S(1)} %pad_maximum_fusion.small_hbm), custom_call_target="tpu_custom_call" | custom-call | flops 8388608 | bytes 1572864 | tf_op jit(solution)/shard_map/end_states/pallas_call | solution.py:220
  11.3 1.2 copy-done.1
  12.7 1.6 %collective-permute-start.1 = (f32[8,2048]{1,0:T(8,128)S(1)}, f32[8,2048]{1,0:T(8,128)S(1)}, u32[]{:S(2)}, u32[]{:S(2)}) collective-permute-start(f32[8,2048]{1,0:T(8,128)S(1)} %fusion.29), channel_id=1, source_target_pairs={{0,4},{4,0},{8,12},{12,8},{16,20},{20,16},{24,28},{28,24},{1,5},{5... | collective-permute-start | bytes 196616 | tf_op jit(solution)/shard_map/ppermute | solution.py:301
  14.3 2.7 %collective-permute-done.1 = f32[8,2048]{1,0:T(8,128)S(1)} collective-permute-done((f32[8,2048]{1,0:T(8,128)S(1)}, f32[8,2048]{1,0:T(8,128)S(1)}, u32[]{:S(2)}, u32[]{:S(2)}) %collective-permute-start.1) | collective-permute-done | bytes 65568 | tf_op jit(solution)/shard_map/ppermute | solution.py:301
  17.0 1.6 %collective-permute-start.2 = (f32[8,2048]{1,0:T(8,128)S(1)}, f32[8,2048]{1,0:T(8,128)S(1)}, u32[]{:S(2)}, u32[]{:S(2)}) collective-permute-start(f32[8,2048]{1,0:T(8,128)S(1)} %fusion.31), channel_id=1, source_target_pairs={{0,8},{4,12},{8,0},{12,4},{16,24},{20,28},{24,16},{28,20},{1,9},{5... | collective-permute-start | bytes 196616 | tf_op jit(solution)/shard_map/ppermute | solution.py:301
  18.7 2.7 %collective-permute-done.2 = f32[8,2048]{1,0:T(8,128)S(1)} collective-permute-done((f32[8,2048]{1,0:T(8,128)S(1)}, f32[8,2048]{1,0:T(8,128)S(1)}, u32[]{:S(2)}, u32[]{:S(2)}) %collective-permute-start.2) | collective-permute-done | bytes 65568 | tf_op jit(solution)/shard_map/ppermute | solution.py:301
  21.4 2.8 %collective-permute-start.3 = (f32[8,2048]{1,0:T(8,128)S(1)}, f32[8,2048]{1,0:T(8,128)S(1)}, u32[]{:S(2)}, u32[]{:S(2)}) collective-permute-start(f32[8,2048]{1,0:T(8,128)S(1)} %get-tuple-element.45), channel_id=1, source_target_pairs={{0,16},{4,20},{8,24},{12,28},{16,0},{20,4},{24,8},{28,12},{1,17},{... | collective-permute-start | bytes 196616 | tf_op jit(solution)/shard_map/ppermute | solution.py:301
  24.3 1.4 %copy-done.2 = bf16[3,128,2048]{2,1,0:T(8,128)(2,1)S(1)} copy-done((bf16[3,128,2048]{2,1,0:T(8,128)(2,1)S(1)}, bf16[3,128,2048]{2,1,0:T(8,128)(2,1)}, u32[]{:S(2)}) %copy-start.2) | copy-done | bytes 1572888
  25.7 2.4 %local_parts.1 = (f32[16,16,8,128]{3,2,1,0:T(8,128)S(1)}, f32[16,16,8,128]{3,2,1,0:T(8,128)S(1)}, f32[16,8,8,128]{3,2,1,0:T(8,128)S(1)}) custom-call(bf16[3,128,2048]{2,1,0:T(8,128)(2,1)S(1)} %copy-done.2, bf16[3,2,2048]{2,1,0:T(2,128)(2,1)S(1)} %collective-permute-done.halo_ref, f32[3,3,2048]{2,1,0:T(4,128)S(1)} %get-tuple-element.21.taps_ref, ...), custom_call_target="tpu_custom_call" | custom-call | flops 8388608 | bytes 2097152 | tf_op jit(solution)/shard_map/local_parts/pallas_call | solution.py:241
  28.1 1.3 %gated_half.3 = (bf16[64,1024]{1,0:T(8,128)(2,1)S(1)}, bf16[64,1024]{1,0:T(8,128)(2,1)S(1)}) custom-call(s32[2]{0:T(128)S(1)} %pad_add_fusion.place_ref, f32[16,16,8,128]{3,2,1,0:T(8,128)S(1)} %get-tuple-element.23.product_ref, f32[16,16,8,128]{3,2,1,0:T(8,128)S(1)} %get-tuple-element.24.query_ref, f32[16,8,8,128]{3,2,1,0:T(8,128)S(1)} %get-tuple-element.25.scan_ref, ...), custom_call_target="tpu_custom_call" | custom-call | flops 4194304 | bytes 1048576 | tf_op jit(solution)/shard_map/gated_half/pallas_call | solution.py:258
  29.4 1.6 %collective-permute-start.10 = (bf16[64,1024]{1,0:T(8,128)(2,1)S(1)}, bf16[64,1024]{1,0:T(8,128)(2,1)}, u32[]{:S(2)}, u32[]{:S(2)}) collective-permute-start(bf16[64,1024]{1,0:T(8,128)(2,1)S(1)} %get-tuple-element.30), channel_id=1, source_target_pairs={{0,2},{1,3},{2,0},{3,1},{4,6},{5,7},{6,4},{7,5},{8,10},{9,11},{10,... | collective-permute-start | bytes 393224 | tf_op jit(solution)/shard_map/ppermute | solution.py:287
  31.0 1.5 %collective-permute-start.6 = (bf16[64,1024]{1,0:T(8,128)(2,1)S(1)}, bf16[64,1024]{1,0:T(8,128)(2,1)S(1)}, u32[]{:S(2)}, u32[]{:S(2)}) collective-permute-start(bf16[64,1024]{1,0:T(8,128)(2,1)S(1)} %get-tuple-element.28), channel_id=1, source_target_pairs={{0,4},{1,14},{2,21},{3,31},{4,0},{5,10},{6,17},{7,27},{8,6},{9,12}... | collective-permute-start | bytes 393224 | tf_op jit(solution)/shard_map/ppermute | solution.py:287
  32.6 2.0 %collective-permute-done.10 = bf16[64,1024]{1,0:T(8,128)(2,1)} collective-permute-done((bf16[64,1024]{1,0:T(8,128)(2,1)S(1)}, bf16[64,1024]{1,0:T(8,128)(2,1)}, u32[]{:S(2)}, u32[]{:S(2)}) %collective-permute-start.10) | collective-permute-done | bytes 131104 | tf_op jit(solution)/shard_map/ppermute | solution.py:287
  34.6 1.3 %gated_half.2 = bf16[128,1024]{1,0:T(8,128)(2,1)S(1)} custom-call(s32[2]{0:T(128)S(1)} %pad_add_fusion.place_ref, f32[16,16,8,128]{3,2,1,0:T(8,128)S(1)} %get-tuple-element.23.product_ref, f32[16,16,8,128]{3,2,1,0:T(8,128)S(1)} %get-tuple-element.24.query_ref, f32[16,8,8,128]{3,2,1,0:T(8,128)S(1)} %get-tuple-element.25.scan_ref, ...), custom_call_target="tpu_custom_call" | custom-call | flops 4194304 | bytes 1048576 | tf_op jit(solution)/shard_map/gated_half/pallas_call | solution.py:258
  36.6 3.6 %collective-permute-done.6 = bf16[64,1024]{1,0:T(8,128)(2,1)S(1)} collective-permute-done((bf16[64,1024]{1,0:T(8,128)(2,1)S(1)}, bf16[64,1024]{1,0:T(8,128)(2,1)S(1)}, u32[]{:S(2)}, u32[]{:S(2)}) %collective-permute-start.6) | collective-permute-done | bytes 131104 | tf_op jit(solution)/shard_map/ppermute | solution.py:287
  40.2 1.8 %collective-permute-start.7 = (bf16[64,1024]{1,0:T(8,128)(2,1)S(1)}, bf16[64,1024]{1,0:T(8,128)(2,1)S(1)}, u32[]{:S(2)}, u32[]{:S(2)}) collective-permute-start(bf16[64,1024]{1,0:T(8,128)(2,1)S(1)} %collective-permute-done.6), channel_id=1, source_target_pairs={{0,1},{1,0},{2,3},{3,2},{4,5},{5,4},{6,7},{7,6},{8,9},{9,8},{10,11... | collective-permute-start | bytes 393224 | tf_op jit(solution)/shard_map/ppermute | solution.py:287
  42.0 2.9 %collective-permute-done.11 = bf16[64,1024]{1,0:T(8,128)(2,1)S(1)} collective-permute-done((bf16[64,1024]{1,0:T(8,128)(2,1)}, bf16[64,1024]{1,0:T(8,128)(2,1)S(1)}, u32[]{:S(2)}, u32[]{:S(2)}) %collective-permute-start.11) | collective-permute-done | bytes 131104 | tf_op jit(solution)/shard_map/ppermute | solution.py:287
  45.0 3.0 %convolution_convert_fusion.4 = bf16[64,2048]{1,0:T(8,128)(2,1)S(1)} fusion(bf16[1024,2048]{1,0:T(8,128)(2,1)} %param.13, bf16[64,1024]{1,0:T(8,128)(2,1)S(1)} %collective-permute-done.6, bf16[64,1024]{1,0:T(8,128)(2,1)S(1)} %collective-permute-done.7, pred[]{:T(512)S(6)} %eq.8), kind=kOutput, calls=%fused_computation.4 | convolution fusion | flops 268632064 | bytes 4718593 | tf_op jit(solution)/shard_map/dot_general | solution.py:376
  48.1 1.5 %collective-permute-start.8 = (bf16[64,2048]{1,0:T(8,128)(2,1)S(1)}, bf16[64,2048]{1,0:T(8,128)(2,1)S(1)}, u32[]{:S(2)}, u32[]{:S(2)}) collective-permute-start(bf16[64,2048]{1,0:T(8,128)(2,1)S(1)} %convolution_convert_fusion.4), channel_id=1, source_target_pairs={{0,4},{1,5},{2,6},{3,7},{4,0},{5,1},{6,2},{7,3},{8,12},{9,13},{10,... | collective-permute-start | bytes 786440 | tf_op jit(solution)/shard_map/ppermute | solution.py:287
  49.7 2.5 %collective-permute-start.15 = (bf16[128,1024]{1,0:T(8,128)(2,1)S(1)}, bf16[128,1024]{1,0:T(8,128)(2,1)S(1)}, u32[]{:S(2)}, u32[]{:S(2)}) collective-permute-start(bf16[128,1024]{1,0:T(8,128)(2,1)S(1)} %collective-permute-done.4), channel_id=1, source_target_pairs={{0,2},{1,3},{2,0},{3,1},{4,6},{5,7},{6,4},{7,5},{8,10},{9,11},{10,... | collective-permute-start | bytes 786440 | tf_op jit(solution)/shard_map/ppermute | solution.py:287
  52.1 1.4 %collective-permute-start.5 = (bf16[128,1024]{1,0:T(8,128)(2,1)S(1)}, bf16[128,1024]{1,0:T(8,128)(2,1)S(1)}, u32[]{:S(2)}, u32[]{:S(2)}) collective-permute-start(bf16[128,1024]{1,0:T(8,128)(2,1)S(1)} %collective-permute-done.4), channel_id=1, source_target_pairs={{0,1},{1,0},{2,3},{3,2},{4,5},{5,4},{6,7},{7,6},{8,9},{9,8},{10,11... | collective-permute-start | bytes 786440 | tf_op jit(solution)/shard_map/ppermute | solution.py:287
  53.5 0.8 convolution_convert_fusion.3
  54.9 0.7 convolution_convert_fusion.1
  55.7 1.7 %collective-permute-start.23 = (bf16[64,2048]{1,0:T(8,128)(2,1)S(1)}, bf16[64,2048]{1,0:T(8,128)(2,1)S(1)}, u32[]{:S(2)}, u32[]{:S(2)}) collective-permute-start(bf16[64,2048]{1,0:T(8,128)(2,1)S(1)} %get-tuple-element.44), channel_id=1, source_target_pairs={{0,4},{1,5},{2,6},{3,7},{4,0},{5,1},{6,2},{7,3},{8,12},{9,13},{10,... | collective-permute-start | bytes 786440 | tf_op jit(solution)/shard_map/ppermute | solution.py:287
  58.2 0.7 fusion.5
  59.6 2.8 %collective-permute-start.9 = (bf16[64,2048]{1,0:T(8,128)(2,1)S(1)}, bf16[64,2048]{1,0:T(8,128)(2,1)S(1)}, u32[]{:S(2)}, u32[]{:S(2)}) collective-permute-start(bf16[64,2048]{1,0:T(8,128)(2,1)S(1)} %add_convert_fusion.7), channel_id=1, source_target_pairs={{0,16},{1,17},{2,26},{3,27},{4,20},{5,21},{6,30},{7,31},{8,24},{9,... | collective-permute-start | bytes 786440 | tf_op jit(solution)/shard_map/ppermute | solution.py:287
  62.4 1.2 collective-permute-done.13
  63.7 5.6 %collective-permute-done.23 = bf16[64,2048]{1,0:T(8,128)(2,1)S(1)} collective-permute-done((bf16[64,2048]{1,0:T(8,128)(2,1)S(1)}, bf16[64,2048]{1,0:T(8,128)(2,1)S(1)}, u32[]{:S(2)}, u32[]{:S(2)}) %collective-permute-start.23) | collective-permute-done | bytes 262176 | tf_op jit(solution)/shard_map/ppermute | solution.py:287
  69.2 2.2 %collective-permute-start.14 = (bf16[64,2048]{1,0:T(8,128)(2,1)S(1)}, bf16[64,2048]{1,0:T(8,128)(2,1)S(1)}, u32[]{:S(2)}, u32[]{:S(2)}) collective-permute-start(bf16[64,2048]{1,0:T(8,128)(2,1)S(1)} %add_convert_fusion.6), channel_id=1, source_target_pairs={{0,16},{1,17},{2,26},{3,27},{4,20},{5,21},{6,30},{7,31},{8,24},{9,... | collective-permute-start | bytes 786440 | tf_op jit(solution)/shard_map/ppermute | solution.py:287
  71.5 2.4 %collective-permute-done.21 = bf16[64,2048]{1,0:T(8,128)(2,1)S(1)} collective-permute-done((bf16[64,2048]{1,0:T(8,128)(2,1)S(1)}, bf16[64,2048]{1,0:T(8,128)(2,1)S(1)}, u32[]{:S(2)}, u32[]{:S(2)}) %collective-permute-start.21) | collective-permute-done | bytes 262176 | tf_op jit(solution)/shard_map/ppermute | solution.py:287
  74.6 0.7 convolution_convert_fusion.2
  75.4 1.4 %collective-permute-start.19 = (bf16[128,2048]{1,0:T(8,128)(2,1)S(1)}, bf16[128,2048]{1,0:T(8,128)(2,1)S(1)}, u32[]{:S(2)}, u32[]{:S(2)}) collective-permute-start(bf16[128,2048]{1,0:T(8,128)(2,1)S(1)} %convolution_convert_fusion.2), channel_id=1, source_target_pairs={{0,4},{1,5},{2,6},{3,7},{4,0},{5,1},{6,2},{7,3},{8,12},{9,13},{10,... | collective-permute-start | bytes 1572872 | tf_op jit(solution)/shard_map/ppermute | solution.py:287
  77.6 0.7 convolution_convert_fusion
  78.4 0.8 collective-permute-start.27
  79.9 14.2 %collective-permute-done.27 = bf16[64,2048]{1,0:T(8,128)(2,1)S(1)} collective-permute-done((bf16[64,2048]{1,0:T(8,128)(2,1)S(1)}, bf16[64,2048]{1,0:T(8,128)(2,1)S(1)}, u32[]{:S(2)}, u32[]{:S(2)}) %collective-permute-start.27) | collective-permute-done | bytes 262176 | tf_op jit(solution)/shard_map/ppermute | solution.py:287
  94.8 1.8 %collective-permute-start.25 = (bf16[64,2048]{1,0:T(8,128)(2,1)S(1)}, bf16[64,2048]{1,0:T(8,128)(2,1)S(1)}, u32[]{:S(2)}, u32[]{:S(2)}) collective-permute-start(bf16[64,2048]{1,0:T(8,128)(2,1)S(1)} %get-tuple-element.41), channel_id=1, source_target_pairs={{0,4},{1,5},{2,6},{3,7},{4,0},{5,1},{6,2},{7,3},{8,12},{9,13},{10,... | collective-permute-start | bytes 786440 | tf_op jit(solution)/shard_map/ppermute | solution.py:287
  96.8 5.1 %collective-permute-done.25 = bf16[64,2048]{1,0:T(8,128)(2,1)S(1)} collective-permute-done((bf16[64,2048]{1,0:T(8,128)(2,1)S(1)}, bf16[64,2048]{1,0:T(8,128)(2,1)S(1)}, u32[]{:S(2)}, u32[]{:S(2)}) %collective-permute-start.25) | collective-permute-done | bytes 262176 | tf_op jit(solution)/shard_map/ppermute | solution.py:287
  101.9 2.0 %collective-permute-start.20 = (bf16[128,2048]{1,0:T(8,128)(2,1)S(1)}, bf16[128,2048]{1,0:T(8,128)(2,1)S(1)}, u32[]{:S(2)}, u32[]{:S(2)}) collective-permute-start(bf16[128,2048]{1,0:T(8,128)(2,1)S(1)} %add_convert_fusion.1), channel_id=1, source_target_pairs={{0,24},{1,25},{2,18},{3,19},{4,28},{5,29},{6,22},{7,23},{8,16},{9,... | collective-permute-start | bytes 1572872 | tf_op jit(solution)/shard_map/ppermute | solution.py:287
  104.0 2.1 %collective-permute-start.28 = (bf16[64,2048]{1,0:T(8,128)(2,1)S(1)}, bf16[64,2048]{1,0:T(8,128)(2,1)S(1)}, u32[]{:S(2)}, u32[]{:S(2)}) collective-permute-start(bf16[64,2048]{1,0:T(8,128)(2,1)S(1)} %add_convert_fusion.2), channel_id=1, source_target_pairs={{0,8},{1,9},{2,2},{3,3},{4,12},{5,13},{6,6},{7,7},{8,0},{9,1},{10,... | collective-permute-start | bytes 786440 | tf_op jit(solution)/shard_map/ppermute | solution.py:287
  106.1 3.7 %collective-permute-start.26 = (bf16[64,2048]{1,0:T(8,128)(2,1)S(1)}, bf16[64,2048]{1,0:T(8,128)(2,1)S(1)}, u32[]{:S(2)}, u32[]{:S(2)}) collective-permute-start(bf16[64,2048]{1,0:T(8,128)(2,1)S(1)} %add_convert_fusion.3), channel_id=1, source_target_pairs={{0,8},{1,9},{2,2},{3,3},{4,12},{5,13},{6,6},{7,7},{8,0},{9,1},{10,... | collective-permute-start | bytes 786440 | tf_op jit(solution)/shard_map/ppermute | solution.py:287
  109.9 11.4 %collective-permute-done.28 = bf16[64,2048]{1,0:T(8,128)(2,1)S(1)} collective-permute-done((bf16[64,2048]{1,0:T(8,128)(2,1)S(1)}, bf16[64,2048]{1,0:T(8,128)(2,1)S(1)}, u32[]{:S(2)}, u32[]{:S(2)}) %collective-permute-start.28) | collective-permute-done | bytes 262176 | tf_op jit(solution)/shard_map/ppermute | solution.py:287
  121.3 5.5 %collective-permute-done.26 = bf16[64,2048]{1,0:T(8,128)(2,1)S(1)} collective-permute-done((bf16[64,2048]{1,0:T(8,128)(2,1)S(1)}, bf16[64,2048]{1,0:T(8,128)(2,1)S(1)}, u32[]{:S(2)}, u32[]{:S(2)}) %collective-permute-start.26) | collective-permute-done | bytes 262176 | tf_op jit(solution)/shard_map/ppermute | solution.py:287
  126.8 1.2 add_convert_fusion
  (60 shorter events, 6.6 us)
Async XLA Ops:
  0.9 11.6 %collective-permute-start = (bf16[3,2,2048]{2,1,0:T(2,128)(2,1)S(1)}, bf16[3,2,2048]{2,1,0:T(2,128)(2,1)S(1)}, u32[]{:S(2)}, u32[]{:S(2)}) collective-permute-start(bf16[3,2,2048]{2,1,0:T(2,128)(2,1)S(1)} %slice.106), channel_id=1, source_target_pairs={{0,4},{4,8},{8,12},{12,16},{16,20},{20,24},{24,28},{1,5},{5,9},{9,... | collective-permute-start | bytes 73736 | tf_op jit(solution)/shard_map/ppermute | solution.py:290
  6.7 1.4 %copy-start = (bf16[3,128,2048]{2,1,0:T(8,128)(2,1)S(1)}, bf16[3,128,2048]{2,1,0:T(8,128)(2,1)}, u32[]{:S(2)}) copy-start(bf16[3,128,2048]{2,1,0:T(8,128)(2,1)} %block_hbm.1) | copy-start | bytes 4718596
  8.1 0.9 copy-start.3
  11.3 1.2 copy-start.1
  12.7 4.3 %collective-permute-start.1 = (f32[8,2048]{1,0:T(8,128)S(1)}, f32[8,2048]{1,0:T(8,128)S(1)}, u32[]{:S(2)}, u32[]{:S(2)}) collective-permute-start(f32[8,2048]{1,0:T(8,128)S(1)} %fusion.29), channel_id=1, source_target_pairs={{0,4},{4,0},{8,12},{12,8},{16,20},{20,16},{24,28},{28,24},{1,5},{5... | collective-permute-start | bytes 196616 | tf_op jit(solution)/shard_map/ppermute | solution.py:301
  17.0 4.3 %collective-permute-start.2 = (f32[8,2048]{1,0:T(8,128)S(1)}, f32[8,2048]{1,0:T(8,128)S(1)}, u32[]{:S(2)}, u32[]{:S(2)}) collective-permute-start(f32[8,2048]{1,0:T(8,128)S(1)} %fusion.31), channel_id=1, source_target_pairs={{0,8},{4,12},{8,0},{12,4},{16,24},{20,28},{24,16},{28,20},{1,9},{5... | collective-permute-start | bytes 196616 | tf_op jit(solution)/shard_map/ppermute | solution.py:301
  21.4 6.7 %collective-permute-start.3 = (f32[8,2048]{1,0:T(8,128)S(1)}, f32[8,2048]{1,0:T(8,128)S(1)}, u32[]{:S(2)}, u32[]{:S(2)}) collective-permute-start(f32[8,2048]{1,0:T(8,128)S(1)} %get-tuple-element.45), channel_id=1, source_target_pairs={{0,16},{4,20},{8,24},{12,28},{16,0},{20,4},{24,8},{28,12},{1,17},{... | collective-permute-start | bytes 196616 | tf_op jit(solution)/shard_map/ppermute | solution.py:301
  24.3 1.4 %copy-start.2 = (bf16[3,128,2048]{2,1,0:T(8,128)(2,1)S(1)}, bf16[3,128,2048]{2,1,0:T(8,128)(2,1)}, u32[]{:S(2)}) copy-start(bf16[3,128,2048]{2,1,0:T(8,128)(2,1)} %copy-done.1) | copy-start | bytes 4718596
  29.4 5.1 %collective-permute-start.10 = (bf16[64,1024]{1,0:T(8,128)(2,1)S(1)}, bf16[64,1024]{1,0:T(8,128)(2,1)}, u32[]{:S(2)}, u32[]{:S(2)}) collective-permute-start(bf16[64,1024]{1,0:T(8,128)(2,1)S(1)} %get-tuple-element.30), channel_id=1, source_target_pairs={{0,2},{1,3},{2,0},{3,1},{4,6},{5,7},{6,4},{7,5},{8,10},{9,11},{10,... | collective-permute-start | bytes 393224 | tf_op jit(solution)/shard_map/ppermute | solution.py:287
  31.0 9.2 %collective-permute-start.6 = (bf16[64,1024]{1,0:T(8,128)(2,1)S(1)}, bf16[64,1024]{1,0:T(8,128)(2,1)S(1)}, u32[]{:S(2)}, u32[]{:S(2)}) collective-permute-start(bf16[64,1024]{1,0:T(8,128)(2,1)S(1)} %get-tuple-element.28), channel_id=1, source_target_pairs={{0,4},{1,14},{2,21},{3,31},{4,0},{5,10},{6,17},{7,27},{8,6},{9,12}... | collective-permute-start | bytes 393224 | tf_op jit(solution)/shard_map/ppermute | solution.py:287
  34.6 10.3 %collective-permute-start.11 = (bf16[64,1024]{1,0:T(8,128)(2,1)}, bf16[64,1024]{1,0:T(8,128)(2,1)S(1)}, u32[]{:S(2)}, u32[]{:S(2)}) collective-permute-start(bf16[64,1024]{1,0:T(8,128)(2,1)} %collective-permute-done.10), channel_id=1, source_target_pairs={{0,21},{1,31},{2,4},{3,14},{4,17},{5,27},{6,0},{7,10},{8,23},{9,29... | collective-permute-start | bytes 393224 | tf_op jit(solution)/shard_map/ppermute | solution.py:287
  34.6 18.9 %copy-start.4 = (bf16[1024,2048]{1,0:T(8,128)(2,1)S(1)}, bf16[1024,2048]{1,0:T(8,128)(2,1)}, u32[]{:S(2)}) copy-start(bf16[1024,2048]{1,0:T(8,128)(2,1)} %param.13) | copy-start | bytes 12582916
  35.9 13.8 %collective-permute-start.4 = (bf16[128,1024]{1,0:T(8,128)(2,1)S(1)}, bf16[128,1024]{1,0:T(8,128)(2,1)S(1)}, u32[]{:S(2)}, u32[]{:S(2)}) collective-permute-start(bf16[128,1024]{1,0:T(8,128)(2,1)S(1)} %gated_half.2), channel_id=1, source_target_pairs={{0,0},{1,10},{2,17},{3,27},{4,4},{5,14},{6,21},{7,31},{8,2},{9,8},... | collective-permute-start | bytes 786440 | tf_op jit(solution)/shard_map/ppermute | solution.py:287
  40.2 4.8 %collective-permute-start.7 = (bf16[64,1024]{1,0:T(8,128)(2,1)S(1)}, bf16[64,1024]{1,0:T(8,128)(2,1)S(1)}, u32[]{:S(2)}, u32[]{:S(2)}) collective-permute-start(bf16[64,1024]{1,0:T(8,128)(2,1)S(1)} %collective-permute-done.6), channel_id=1, source_target_pairs={{0,1},{1,0},{2,3},{3,2},{4,5},{5,4},{6,7},{7,6},{8,9},{9,8},{10,11... | collective-permute-start | bytes 393224 | tf_op jit(solution)/shard_map/ppermute | solution.py:287
  44.9 17.5 %collective-permute-start.17 = (bf16[128,1024]{1,0:T(8,128)(2,1)S(1)}, bf16[128,1024]{1,0:T(8,128)(2,1)S(1)}, u32[]{:S(2)}, u32[]{:S(2)}) collective-permute-start(bf16[128,1024]{1,0:T(8,128)(2,1)S(1)} %constant_dynamic-update-slice_fusion), channel_id=1, source_target_pairs={{0,2},{1,3},{2,0},{3,1},{4,6},{5,7},{6,4},{7,5},{8,10},{9,11},{10,... | collective-permute-start | bytes 786440 | tf_op jit(solution)/shard_map/ppermute | solution.py:287
  45.0 8.6 %collective-permute-start.12 = (bf16[64,1024]{1,0:T(8,128)(2,1)S(1)}, bf16[64,1024]{1,0:T(8,128)(2,1)S(1)}, u32[]{:S(2)}, u32[]{:S(2)}) collective-permute-start(bf16[64,1024]{1,0:T(8,128)(2,1)S(1)} %collective-permute-done.11), channel_id=1, source_target_pairs={{0,1},{1,0},{2,3},{3,2},{4,5},{5,4},{6,7},{7,6},{8,9},{9,8},{10,11... | collective-permute-start | bytes 393224 | tf_op jit(solution)/shard_map/ppermute | solution.py:287
  48.1 10.9 %collective-permute-start.8 = (bf16[64,2048]{1,0:T(8,128)(2,1)S(1)}, bf16[64,2048]{1,0:T(8,128)(2,1)S(1)}, u32[]{:S(2)}, u32[]{:S(2)}) collective-permute-start(bf16[64,2048]{1,0:T(8,128)(2,1)S(1)} %convolution_convert_fusion.4), channel_id=1, source_target_pairs={{0,4},{1,5},{2,6},{3,7},{4,0},{5,1},{6,2},{7,3},{8,12},{9,13},{10,... | collective-permute-start | bytes 786440 | tf_op jit(solution)/shard_map/ppermute | solution.py:287
  49.7 10.0 %collective-permute-start.15 = (bf16[128,1024]{1,0:T(8,128)(2,1)S(1)}, bf16[128,1024]{1,0:T(8,128)(2,1)S(1)}, u32[]{:S(2)}, u32[]{:S(2)}) collective-permute-start(bf16[128,1024]{1,0:T(8,128)(2,1)S(1)} %collective-permute-done.4), channel_id=1, source_target_pairs={{0,2},{1,3},{2,0},{3,1},{4,6},{5,7},{6,4},{7,5},{8,10},{9,11},{10,... | collective-permute-start | bytes 786440 | tf_op jit(solution)/shard_map/ppermute | solution.py:287
  52.1 3.6 %collective-permute-start.5 = (bf16[128,1024]{1,0:T(8,128)(2,1)S(1)}, bf16[128,1024]{1,0:T(8,128)(2,1)S(1)}, u32[]{:S(2)}, u32[]{:S(2)}) collective-permute-start(bf16[128,1024]{1,0:T(8,128)(2,1)S(1)} %collective-permute-done.4), channel_id=1, source_target_pairs={{0,1},{1,0},{2,3},{3,2},{4,5},{5,4},{6,7},{7,6},{8,9},{9,8},{10,11... | collective-permute-start | bytes 786440 | tf_op jit(solution)/shard_map/ppermute | solution.py:287
  54.4 9.2 %collective-permute-start.13 = (bf16[64,2048]{1,0:T(8,128)(2,1)S(1)}, bf16[64,2048]{1,0:T(8,128)(2,1)S(1)}, u32[]{:S(2)}, u32[]{:S(2)}) collective-permute-start(bf16[64,2048]{1,0:T(8,128)(2,1)S(1)} %convolution_convert_fusion.3), channel_id=1, source_target_pairs={{0,4},{1,5},{2,6},{3,7},{4,0},{5,1},{6,2},{7,3},{8,12},{9,13},{10,... | collective-permute-start | bytes 786440 | tf_op jit(solution)/shard_map/ppermute | solution.py:287
  55.7 13.6 %collective-permute-start.23 = (bf16[64,2048]{1,0:T(8,128)(2,1)S(1)}, bf16[64,2048]{1,0:T(8,128)(2,1)S(1)}, u32[]{:S(2)}, u32[]{:S(2)}) collective-permute-start(bf16[64,2048]{1,0:T(8,128)(2,1)S(1)} %get-tuple-element.44), channel_id=1, source_target_pairs={{0,4},{1,5},{2,6},{3,7},{4,0},{5,1},{6,2},{7,3},{8,12},{9,13},{10,... | collective-permute-start | bytes 786440 | tf_op jit(solution)/shard_map/ppermute | solution.py:287
  59.0 14.9 %collective-permute-start.21 = (bf16[64,2048]{1,0:T(8,128)(2,1)S(1)}, bf16[64,2048]{1,0:T(8,128)(2,1)S(1)}, u32[]{:S(2)}, u32[]{:S(2)}) collective-permute-start(bf16[64,2048]{1,0:T(8,128)(2,1)S(1)} %get-tuple-element.43), channel_id=1, source_target_pairs={{0,4},{1,5},{2,6},{3,7},{4,0},{5,1},{6,2},{7,3},{8,12},{9,13},{10,... | collective-permute-start | bytes 786440 | tf_op jit(solution)/shard_map/ppermute | solution.py:287
  59.6 44.4 %collective-permute-start.9 = (bf16[64,2048]{1,0:T(8,128)(2,1)S(1)}, bf16[64,2048]{1,0:T(8,128)(2,1)S(1)}, u32[]{:S(2)}, u32[]{:S(2)}) collective-permute-start(bf16[64,2048]{1,0:T(8,128)(2,1)S(1)} %add_convert_fusion.7), channel_id=1, source_target_pairs={{0,16},{1,17},{2,26},{3,27},{4,20},{5,21},{6,30},{7,31},{8,24},{9,... | collective-permute-start | bytes 786440 | tf_op jit(solution)/shard_map/ppermute | solution.py:287
  62.4 14.3 %collective-permute-start.16 = (bf16[128,1024]{1,0:T(8,128)(2,1)S(1)}, bf16[128,1024]{1,0:T(8,128)(2,1)S(1)}, u32[]{:S(2)}, u32[]{:S(2)}) collective-permute-start(bf16[128,1024]{1,0:T(8,128)(2,1)S(1)} %collective-permute-done.15), channel_id=1, source_target_pairs={{0,1},{1,0},{2,3},{3,2},{4,5},{5,4},{6,7},{7,6},{8,9},{9,8},{10,11... | collective-permute-start | bytes 786440 | tf_op jit(solution)/shard_map/ppermute | solution.py:287
  63.6 11.0 %collective-permute-start.18 = (bf16[128,1024]{1,0:T(8,128)(2,1)S(1)}, bf16[128,1024]{1,0:T(8,128)(2,1)S(1)}, u32[]{:S(2)}, u32[]{:S(2)}) collective-permute-start(bf16[128,1024]{1,0:T(8,128)(2,1)S(1)} %collective-permute-done.17), channel_id=1, source_target_pairs={{0,1},{1,0},{2,3},{3,2},{4,5},{5,4},{6,7},{7,6},{8,9},{9,8},{10,11... | collective-permute-start | bytes 786440 | tf_op jit(solution)/shard_map/ppermute | solution.py:287
  69.2 36.9 %collective-permute-start.14 = (bf16[64,2048]{1,0:T(8,128)(2,1)S(1)}, bf16[64,2048]{1,0:T(8,128)(2,1)S(1)}, u32[]{:S(2)}, u32[]{:S(2)}) collective-permute-start(bf16[64,2048]{1,0:T(8,128)(2,1)S(1)} %add_convert_fusion.6), channel_id=1, source_target_pairs={{0,16},{1,17},{2,26},{3,27},{4,20},{5,21},{6,30},{7,31},{8,24},{9,... | collective-permute-start | bytes 786440 | tf_op jit(solution)/shard_map/ppermute | solution.py:287
  73.9 36.0 %collective-permute-start.24 = (bf16[64,2048]{1,0:T(8,128)(2,1)S(1)}, bf16[64,2048]{1,0:T(8,128)(2,1)S(1)}, u32[]{:S(2)}, u32[]{:S(2)}) collective-permute-start(bf16[64,2048]{1,0:T(8,128)(2,1)S(1)} %add_convert_fusion.4), channel_id=1, source_target_pairs={{0,0},{1,1},{2,10},{3,11},{4,4},{5,5},{6,14},{7,15},{8,8},{9,9},{1... | collective-permute-start | bytes 786440 | tf_op jit(solution)/shard_map/ppermute | solution.py:287
  75.4 19.5 %collective-permute-start.19 = (bf16[128,2048]{1,0:T(8,128)(2,1)S(1)}, bf16[128,2048]{1,0:T(8,128)(2,1)S(1)}, u32[]{:S(2)}, u32[]{:S(2)}) collective-permute-start(bf16[128,2048]{1,0:T(8,128)(2,1)S(1)} %convolution_convert_fusion.2), channel_id=1, source_target_pairs={{0,4},{1,5},{2,6},{3,7},{4,0},{5,1},{6,2},{7,3},{8,12},{9,13},{10,... | collective-permute-start | bytes 1572872 | tf_op jit(solution)/shard_map/ppermute | solution.py:287
  78.4 48.4 %copy-start.5 = (bf16[128,2048]{1,0:T(8,128)(2,1)S(1)}, bf16[128,2048]{1,0:T(8,128)(2,1)}, u32[]{:S(2)}) copy-start(bf16[128,2048]{1,0:T(8,128)(2,1)} %param.7) | copy-start | bytes 1572868
  78.4 15.7 %collective-permute-start.27 = (bf16[64,2048]{1,0:T(8,128)(2,1)S(1)}, bf16[64,2048]{1,0:T(8,128)(2,1)S(1)}, u32[]{:S(2)}, u32[]{:S(2)}) collective-permute-start(bf16[64,2048]{1,0:T(8,128)(2,1)S(1)} %get-tuple-element.42), channel_id=1, source_target_pairs={{0,4},{1,5},{2,6},{3,7},{4,0},{5,1},{6,2},{7,3},{8,12},{9,13},{10,... | collective-permute-start | bytes 786440 | tf_op jit(solution)/shard_map/ppermute | solution.py:287
  94.1 15.8 %collective-permute-start.22 = (bf16[64,2048]{1,0:T(8,128)(2,1)S(1)}, bf16[64,2048]{1,0:T(8,128)(2,1)S(1)}, u32[]{:S(2)}, u32[]{:S(2)}) collective-permute-start(bf16[64,2048]{1,0:T(8,128)(2,1)S(1)} %add_convert_fusion.5), channel_id=1, source_target_pairs={{0,0},{1,1},{2,10},{3,11},{4,4},{5,5},{6,14},{7,15},{8,8},{9,9},{1... | collective-permute-start | bytes 786440 | tf_op jit(solution)/shard_map/ppermute | solution.py:287
  94.8 7.1 %collective-permute-start.25 = (bf16[64,2048]{1,0:T(8,128)(2,1)S(1)}, bf16[64,2048]{1,0:T(8,128)(2,1)S(1)}, u32[]{:S(2)}, u32[]{:S(2)}) collective-permute-start(bf16[64,2048]{1,0:T(8,128)(2,1)S(1)} %get-tuple-element.41), channel_id=1, source_target_pairs={{0,4},{1,5},{2,6},{3,7},{4,0},{5,1},{6,2},{7,3},{8,12},{9,13},{10,... | collective-permute-start | bytes 786440 | tf_op jit(solution)/shard_map/ppermute | solution.py:287
  101.9 24.9 %collective-permute-start.20 = (bf16[128,2048]{1,0:T(8,128)(2,1)S(1)}, bf16[128,2048]{1,0:T(8,128)(2,1)S(1)}, u32[]{:S(2)}, u32[]{:S(2)}) collective-permute-start(bf16[128,2048]{1,0:T(8,128)(2,1)S(1)} %add_convert_fusion.1), channel_id=1, source_target_pairs={{0,24},{1,25},{2,18},{3,19},{4,28},{5,29},{6,22},{7,23},{8,16},{9,... | collective-permute-start | bytes 1572872 | tf_op jit(solution)/shard_map/ppermute | solution.py:287
  104.0 17.3 %collective-permute-start.28 = (bf16[64,2048]{1,0:T(8,128)(2,1)S(1)}, bf16[64,2048]{1,0:T(8,128)(2,1)S(1)}, u32[]{:S(2)}, u32[]{:S(2)}) collective-permute-start(bf16[64,2048]{1,0:T(8,128)(2,1)S(1)} %add_convert_fusion.2), channel_id=1, source_target_pairs={{0,8},{1,9},{2,2},{3,3},{4,12},{5,13},{6,6},{7,7},{8,0},{9,1},{10,... | collective-permute-start | bytes 786440 | tf_op jit(solution)/shard_map/ppermute | solution.py:287
  106.1 20.7 %collective-permute-start.26 = (bf16[64,2048]{1,0:T(8,128)(2,1)S(1)}, bf16[64,2048]{1,0:T(8,128)(2,1)S(1)}, u32[]{:S(2)}, u32[]{:S(2)}) collective-permute-start(bf16[64,2048]{1,0:T(8,128)(2,1)S(1)} %add_convert_fusion.3), channel_id=1, source_target_pairs={{0,8},{1,9},{2,2},{3,3},{4,12},{5,13},{6,6},{7,7},{8,0},{9,1},{10,... | collective-permute-start | bytes 786440 | tf_op jit(solution)/shard_map/ppermute | solution.py:287
